TPU v7x, 32 devices: a whole 2x2x4 slice. The times are simulated.
32 devices in a mesh: ctx: 16 (over z, x, core), vocab: 2 (over y).
Axes of the slice: x: 2, y: 2, z: 4, core: 2. Of those that a mesh axis runs over, the one named last changes fastest.
Arguments:
- hidden: bfloat16 [4096, 8192], P('ctx', 'vocab'), may hold values from -540 to 540
- norm_gain: float32 [8192], P('vocab'), may hold values from 0.5 to 1.5
- head: bfloat16 [15808, 8192], P('ctx', 'vocab'), may hold values from -0.53033009 to 0.53033009
- masked_pos: int32 [2, 16], replicated, may hold values from 0 to 2047, as said below
- masked_targets: int32 [2, 16], replicated, may hold values from 0 to 15807
- t_num: int32 [2], replicated, may hold values from 1 to 3, as said below
- t_den: int32 [2], replicated, may hold values from 192 to 319
Outputs:
- loss_value: float32 [], replicated
- grad_hidden: bfloat16 [4096, 8192], P('ctx', 'vocab')
- grad_head: bfloat16 [15808, 8192], P('ctx', 'vocab')
- grad_gain: float32 [8192], P('vocab')
Inputs may be any that keep to these rules, and one draw needn't show every extreme that they name: `masked_pos`: each row lists 16 distinct positions of one sequence in increasing order; at most 8 of them fall in one aligned block of 256 positions, and exactly 8 in some blocks of every sequence. `t_num`: the two numerators differ.
All inputs are finite; a program needn't handle non-finite values.
Results may differ from a plain program's by a relative error of at most 0.0081.
Values may be sent and summed in bfloat16 or wider, within the bound.
No kernel may reach another device: no remote copies, remote signals or barrier semaphores. Data moves between devices by JAX's collectives and lax.ppermute only.
A program may use at most 64 MiB of HBM per device.

v0:
```python
import jax
import jax.numpy as jnp
from jax import lax
from jax.sharding import PartitionSpec as P

CAP = 8


EPSILON = 1e-05
LOSS_SCALE = 1024.0


def joined(part, axis, combine):
    gathered = jax.tree.map(lambda a: lax.all_gather(a, axis), part)

    def take(source):
        return jax.tree.map(lambda a: lax.dynamic_index_in_dim(a, source, 0, False), gathered)

    return lax.fori_loop(
        1, lax.axis_size(axis), lambda source, state: combine(state, take(source)), take(0)
    )


def contract_last(left, right):
    return lax.dot_general(
        left, right, (((1,), (1,)), ((), ())), preferred_element_type=jnp.float32
    )


def combine_stats(first, second):
    row_top = jnp.maximum(first[0], second[0])
    exp_total = first[1] * jnp.exp(first[0] - row_top) + second[1] * jnp.exp(second[0] - row_top)
    return (row_top, exp_total, first[2] + second[2])


def on_device(hidden, norm_gain, head, masked_pos, masked_targets, t_num, t_den):
    tok_here, width_here = hidden.shape
    voc_here = head.shape[0]
    ctx_count = lax.axis_size("ctx")
    vocab_count = lax.axis_size("vocab")
    ctx_index = lax.axis_index("ctx")
    vocab_index = lax.axis_index("vocab")
    blocks = ctx_count // 2
    slot_count = masked_pos.shape[1]
    model_width = width_here * vocab_count
    seq_here = ctx_index // blocks
    block_here = ctx_index % blocks
    block_of = masked_pos // tok_here
    block_ids = jnp.arange(blocks, dtype=jnp.int32)
    counts = jnp.sum((block_of[:, :, None] == block_ids[None, None, :]).astype(jnp.int32), axis=1)
    offsets = jnp.cumsum(counts, axis=1) - counts
    weight = t_den.astype(jnp.float32) / (t_num.astype(jnp.float32) * (2.0 * tok_here * blocks))
    lane_ids = jnp.arange(CAP, dtype=jnp.int32)
    own_count = counts[seq_here, block_here]
    own_start = offsets[seq_here, block_here]
    own_valid = lane_ids < own_count
    seq_list = jnp.concatenate([masked_pos[seq_here], jnp.zeros((CAP,), jnp.int32)])
    own_pos = lax.dynamic_slice_in_dim(seq_list, own_start, CAP) - block_here * tok_here
    own_pos = jnp.where(own_valid, own_pos, 0)
    own_rows = jnp.where(own_valid[:, None], hidden[own_pos].astype(jnp.float32), 0.0)
    squares = lax.psum(jnp.sum(own_rows * own_rows, axis=1), "vocab")
    inverse = lax.rsqrt(squares / model_width + EPSILON)
    normed_own = (own_rows * inverse[:, None] * norm_gain[None, :]).astype(jnp.bfloat16)
    normed_all = lax.all_gather(normed_own, "ctx", axis=0, tiled=True)
    row_ids = jnp.arange(ctx_count * CAP, dtype=jnp.int32)
    owner_ctx = row_ids // CAP
    lane_of = row_ids % CAP
    owner_seq = owner_ctx // blocks
    owner_block = owner_ctx % blocks
    row_valid = lane_of < counts[owner_seq, owner_block]
    list_slot = jnp.minimum(offsets[owner_seq, owner_block] + lane_of, slot_count - 1)
    row_targets = masked_targets[owner_seq, list_slot]
    row_factor = jnp.where(row_valid, weight[owner_seq], 0.0)
    row_total = normed_all.shape[0]
    rows_block = row_total // vocab_count
    logits = lax.psum_scatter(
        contract_last(normed_all, head), "vocab", scatter_dimension=0, tiled=True
    )
    block_start = vocab_index * rows_block
    target_cols = (
        lax.dynamic_slice_in_dim(row_targets, block_start, rows_block) - ctx_index * voc_here
    )
    factor = lax.dynamic_slice_in_dim(row_factor, block_start, rows_block)
    columns = jnp.arange(voc_here, dtype=jnp.int32)
    is_target = columns[None, :] == target_cols[:, None]
    picked = jnp.sum(jnp.where(is_target, logits, 0.0), axis=1)
    local_top = jnp.max(logits, axis=1)
    local_total = jnp.sum(jnp.exp(logits - local_top[:, None]), axis=1)
    row_top, exp_total, picked = joined((local_top, local_total, picked), "ctx", combine_stats)
    log_total = row_top + jnp.log(exp_total)
    loss_value = lax.psum(jnp.sum(factor * (log_total - picked)), "vocab")
    softmax_out = jnp.exp(logits - log_total[:, None])
    dlogits = (
        (LOSS_SCALE * factor)[:, None] * (softmax_out - is_target.astype(jnp.float32))
    ).astype(jnp.bfloat16)
    all_grads = lax.all_gather(dlogits, "vocab", axis=0, tiled=True)
    grad_head = lax.dot_general(
        all_grads, normed_all, (((0,), (0,)), ((), ())), preferred_element_type=jnp.float32
    ).astype(jnp.bfloat16)
    own_grad = lax.psum_scatter(
        jnp.dot(all_grads, head, preferred_element_type=jnp.float32),
        "ctx",
        scatter_dimension=0,
        tiled=True,
    )
    own_grad = jnp.where(own_valid[:, None], own_grad, 0.0)
    grad_gain = lax.psum(jnp.sum(own_grad * own_rows * inverse[:, None], axis=0), "ctx")
    inner_mean = (
        lax.psum(jnp.sum(norm_gain[None, :] * own_grad * own_rows, axis=1), "vocab") / model_width
    )
    row_grads = (
        inverse[:, None] * norm_gain[None, :] * own_grad
        - own_rows * (inverse * inverse * inverse * inner_mean)[:, None]
    )
    write_rows = jnp.where(own_valid, own_pos, tok_here)
    grad_hidden = (
        jnp.zeros((tok_here, width_here), jnp.bfloat16)
        .at[write_rows]
        .set(row_grads.astype(jnp.bfloat16), mode="drop")
    )
    return (loss_value, grad_hidden, grad_head, grad_gain)


def solution(mesh):
    placed = (P("ctx", "vocab"), P("vocab"), P("ctx", "vocab"), P(), P(), P(), P())
    return jax.shard_map(
        on_device,
        mesh=mesh,
        in_specs=placed,
        out_specs=(P(), P("ctx", "vocab"), P("ctx", "vocab"), P("vocab")),
        check_vma=False,
    )
```

profile of v0, /device:TPU:0, one launch (start us, length us, event | category | flops | bytes accessed | tf_op | source)
XLA Modules:
  0.0 292.8 jit_solution(3344552635716309176)
XLA Ops:
  7.2 0.0 copy-start
  7.2 0.0 copy-start.6
  7.2 0.0 copy-start.1
  7.2 0.0 copy-start.4
  7.2 0.0 copy-start.5
  7.2 0.0 all-gather.5.cloned.1.call-start
  7.3 0.8 and_select_fusion.4
  8.1 0.1 convert_reduce_fusion
  8.3 0.2 reduce_window_sum.11
  8.4 0.7 dynamic-slice_bitcast_fusion
  9.1 0.6 dynamic_slice.59
  9.7 0.6 dynamic_slice.61
  11.6 0.7 iota_compare_fusion.2
  12.9 0.7 compare_select_fusion
  13.7 0.0 copy-done
  13.7 0.6 gather_fusion.1
  14.3 0.2 multiply_reduce_fusion.2
  14.5 5.9 %psum.28 = f32[8]{0:T(128)S(1)} all-reduce(f32[8]{0:T(128)S(1)} %multiply_reduce_fusion.2), channel_id=1, replica_groups=mesh['ctx'=16,'vocab'=2] {'vocab'}, use_global_device_ids=true, to_apply=%region_3.4 | all-reduce | flops 8 | bytes 64 | tf_op jit(solution)/shard_map/psum | solution.py:61
  20.4 1.4 multiply_convert_fusion.1
  21.8 0.0 all-gather.5.cloned.1.call-update
  21.8 0.0 reduce-scatter.3.cloned.1.call-start
  21.9 39.7 %all-gather.5.cloned.1.call-done = bf16[128,4096]{1,0:T(8,128)(2,1)} async-done(((bf16[8,4096]{1,0:T(8,128)(2,1)}), bf16[128,4096]{1,0:T(8,128)(2,1)}) %all-gather.5.cloned.1.call-update) | async-done | bytes 1048592 | tf_op jit(solution)/shard_map/all_gather | solution.py:64
  61.6 7.1 %fusion.28 = f32[128,988]{1,0:T(8,128)} fusion(bf16[128,4096]{1,0:T(8,128)(2,1)} %all-gather.5.cloned.1.call-done, bf16[988,4096]{1,0:T(8,128)(2,1)} %param.11), kind=kOutput, calls=%fused_computation.82 | convolution fusion | flops 1035993088 | bytes 9648128 | tf_op jit(solution)/shard_map/dot_general | solution.py:25
  68.7 0.0 reduce-scatter.3.cloned.1.call-update
  68.7 0.0 reduce-scatter.5.cloned.1.call-start
  68.8 1.5 gather_fusion.2
  70.3 1.5 gather_fusion
  71.9 0.0 copy-done.1
  71.9 1.5 gather_fusion.3
  73.4 0.0 copy-done.6
  73.4 0.6 dynamic-slice
  74.6 0.1 dynamic-slice_subtract_fusion
  74.7 0.0 copy-done.4
  74.7 0.0 copy-done.5
  74.7 0.6 fusion.27
  75.3 1.3 compare_select_fusion.6
  76.6 5.8 %reduce-scatter.3.cloned.1.call-done = f32[64,988]{1,0:T(8,128)} async-done(((f32[128,988]{1,0:T(8,128)}), f32[64,988]{1,0:T(8,128)}) %reduce-scatter.3.cloned.1.call-update) | async-done | bytes 252944 | tf_op jit(solution)/shard_map/reduce_scatter | solution.py:76
  82.4 1.1 reduce_max.9
  83.5 0.2 dynamic-update-slice
  83.8 1.2 select_reduce_fusion
  85.0 0.2 dynamic-update-slice.2
  85.2 0.2 dynamic-update-slice.1
  85.4 61.0 %all-reduce.4 = (f32[1024]{0:T(1024)S(1)}, f32[1024]{0:T(1024)S(1)}, f32[1024]{0:T(1024)S(1)}) all-reduce(f32[1024]{0:T(1024)S(1)} %dynamic-update-slice, f32[1024]{0:T(1024)S(1)} %dynamic-update-slice.1, f32[1024]{0:T(1024)S(1)} %dynamic-update-slice.2), channel_id=2, replica_groups=mesh['ctx'=16,'vocab'=2] {'ctx'}, use_global_device_ids=true, to_apply=%add.1 | all-reduce | flops 3072 | bytes 24576
  146.4 0.1 reshape.215
  146.5 0.1 reshape.216
  146.6 0.1 reshape.217
  146.6 0.7 while.19
  147.3 0.7 multiply_reduce_fusion.3
  148.0 1.1 multiply_convert_fusion
  149.1 5.6 %all_gather.31 = bf16[128,988]{1,0:T(8,128)(2,1)S(1)} all-gather(bf16[64,988]{1,0:T(8,128)(2,1)S(1)} %multiply_convert_fusion), channel_id=1, replica_groups=mesh['ctx'=16,'vocab'=2] {'vocab'}, dimensions={0}, use_global_device_ids=true | all-gather | bytes 379392 | tf_op jit(solution)/shard_map/all_gather | solution.py:96
  154.8 0.0 copy-start.2
  154.8 6.0 %fusion.29 = f32[128,4096]{1,0:T(8,128)} fusion(bf16[128,988]{1,0:T(8,128)(2,1)S(1)} %all_gather.31, bf16[988,4096]{1,0:T(8,128)(2,1)} %param.11), kind=kOutput, calls=%fused_computation.83 | convolution fusion | flops 1035993088 | bytes 10443776 | tf_op jit(solution)/shard_map/dot_general | solution.py:101
  160.8 0.0 copy-start.3
  160.8 0.0 reduce-scatter.5.cloned.1.call-update
  160.8 0.0 copy-done.2
  160.8 5.6 %convolution_convert_fusion = bf16[988,4096]{1,0:T(8,128)(2,1)} fusion(bf16[128,988]{1,0:T(8,128)(2,1)S(1)} %all_gather.31, bf16[128,4096]{1,0:T(8,128)(2,1)S(1)} %copy-done.2), kind=kOutput, calls=%fused_computation.15 | convolution fusion | flops 1040039936 | bytes 9395200 | tf_op jit(solution)/shard_map/dot_general | solution.py:97
  166.4 52.7 %reduce-scatter.5.cloned.1.call-done = f32[8,4096]{1,0:T(8,128)} async-done(((f32[128,4096]{1,0:T(8,128)}), f32[8,4096]{1,0:T(8,128)}) %reduce-scatter.5.cloned.1.call-update) | async-done | bytes 131088 | tf_op jit(solution)/shard_map/reduce_scatter | solution.py:100
  219.1 0.0 copy-done.3
  219.1 1.2 multiply_reduce_fusion
  220.2 5.6 %all-reduce.5 = (f32[]{:T(128)}, f32[8]{0:T(128)S(1)}) all-reduce(f32[]{:T(128)} %get-tuple-element.212, f32[8]{0:T(128)S(1)} %get-tuple-element.188), channel_id=1, replica_groups=mesh['ctx'=16,'vocab'=2] {'vocab'}, use_global_device_ids=true, to_apply=%region_11.12 | all-reduce | flops 9 | bytes 72 | tf_op jit(solution)/shard_map/psum | solution.py:91
  225.8 57.6 %psum.31 = f32[4096]{0:T(1024)} all-reduce(f32[4096]{0:T(1024)S(1)} %get-tuple-element.187), channel_id=1, replica_groups=mesh['ctx'=16,'vocab'=2] {'ctx'}, use_global_device_ids=true, to_apply=%region_17.18 | all-reduce | flops 4096 | bytes 32768 | tf_op jit(solution)/shard_map/psum | solution.py:107
  283.4 2.9 scatter_custom_fusion
  (29 shorter events, 0.5 us)
Async XLA Ops:
  7.2 6.5 %copy-start = (bf16[256,4096]{1,0:T(8,128)(2,1)S(1)}, bf16[256,4096]{1,0:T(8,128)(2,1)}, u32[]{:S(2)}) copy-start(bf16[256,4096]{1,0:T(8,128)(2,1)} %param.9) | copy-start | bytes 6291460
  7.2 66.2 %copy-start.6 = (u32[32]{0:T(128)S(1)}, u32[32]{0:T(128)}, u32[]{:S(2)}) copy-start(u32[32]{0:T(128)} %constant.218) | copy-start | bytes 388
  7.2 64.7 %copy-start.1 = (s32[2,16]{1,0:T(2,128)S(1)}, s32[2,16]{1,0:T(2,128)}, u32[]{:S(2)}) copy-start(s32[2,16]{1,0:T(2,128)} %param.13) | copy-start | bytes 388
  7.2 67.5 %copy-start.4 = (s32[2]{0:T(128)S(1)}, s32[2]{0:T(128)}, u32[]{:S(2)}) copy-start(s32[2]{0:T(128)} %param.14) | copy-start | bytes 28
  7.2 67.5 %copy-start.5 = (s32[2]{0:T(128)S(1)}, s32[2]{0:T(128)}, u32[]{:S(2)}) copy-start(s32[2]{0:T(128)} %param.15) | copy-start | bytes 28
  7.2 54.4 %all-gather.5.cloned.1.call-start = ((), (), s32[]{:S(2)}) async-start(), calls=%async_computation.2 | async-start | bytes 1114112 | tf_op jit(solution)/shard_map/all_gather | solution.py:64
  21.8 60.6 %reduce-scatter.3.cloned.1.call-start = ((), (), s32[]{:S(2)}) async-start(), calls=%async_computation.3 | async-start | bytes 786432 | tf_op jit(solution)/shard_map/reduce_scatter | solution.py:76
  68.7 150.4 %reduce-scatter.5.cloned.1.call-start = ((), (), s32[]{:S(2)}) async-start(), calls=%async_computation.4 | async-start | bytes 2228224 | tf_op jit(solution)/shard_map/reduce_scatter | solution.py:100
  154.8 6.0 %copy-start.2 = (bf16[128,4096]{1,0:T(8,128)(2,1)S(1)}, bf16[128,4096]{1,0:T(8,128)(2,1)}, u32[]{:S(2)}) copy-start(bf16[128,4096]{1,0:T(8,128)(2,1)} %all-gather.5.cloned.1.call-done) | copy-start | bytes 3145732
  160.8 58.3 %copy-start.3 = (f32[4096]{0:T(1024)S(1)}, f32[4096]{0:T(1024)}, u32[]{:S(2)}) copy-start(f32[4096]{0:T(1024)} %param.10) | copy-start | bytes 49156
Sparse Core Ops, SparseCore 0:
  22.0 39.5 all-gather.4
  68.8 13.5 reduce-scatter.2
  160.9 58.1 reduce-scatter.4
where the time goes:
time: 293 us
  blocking collectives  136 us (46%)
  waiting for transfers between devices  98.2 us (34%)
  matrix products  18.7 us (6%)
  between operations  16.6 us (6%)
  other arithmetic  14.1 us (5%)
  local copies, waits for them, and re-layouts  9.14 us (3%)
    unnamed x1, blocking collectives  61 us
    psum x1, blocking collectives, on_device(): lax.psum(jnp.sum(own_grad * own_rows * inverse[:, None], axis=0), 'ctx')  57.6 us
    reduce_scatter x1, waiting for transfers between devices, on_device(): lax.psum_scatter(jnp.dot(all_grads, head, preferred_element_type=jnp.floa...  52.7 us
    all_gather x1, waiting for transfers between devices, on_device(): normed_all = lax.all_gather(normed_own, 'ctx', axis=0, tiled=True)  39.7 us
    dot_general x1, matrix products, contract_last(): lax.dot_general(left, right, (((1,), (1,)), ((), ())), preferred_element_...  7.06 us
    dot_general x1, matrix products, on_device(): jnp.dot(all_grads, head, preferred_element_type=jnp.float32)  5.98 us
    psum x1, blocking collectives, on_device(): squares = lax.psum(jnp.sum(own_rows * own_rows, axis=1), 'vocab')  5.89 us
  transfers between devices with their start and end apart: 3, of which 3 were waited for; matrix products, arithmetic and copies ran while one was open for 4% of the time, Pallas kernels for 0%

commit v1 on v0

v1 whole, which is shorter than its diff:
```python
import jax
import jax.numpy as jnp
from jax import lax
from jax.experimental import pallas as pl
from jax.experimental.pallas import tpu as pltpu
from jax.sharding import PartitionSpec as P


EPSILON = 1e-05
LOSS_SCALE = 1024.0
LANES = 128
SUBLANES = 8
MIB = 1 << 20
F32 = jnp.float32
BF16 = jnp.bfloat16


def vmem():
    return pl.BlockSpec(memory_space=pltpu.VMEM)


def smem():
    return pl.BlockSpec(memory_space=pltpu.SMEM)


def anywhere():
    return pl.BlockSpec(memory_space=pl.ANY)


def params(mib):
    return pltpu.CompilerParams(vmem_limit_bytes=mib * MIB)


def cost(bytes_accessed):
    return pl.CostEstimate(flops=0, bytes_accessed=bytes_accessed, transcendentals=0)


def shape(dims, dtype):
    return jax.ShapeDtypeStruct(dims, dtype)


def swap(x, axis, bit):
    return lax.ppermute(x, axis, [(i, i ^ bit) for i in range(lax.axis_size(axis))])


def sum_over(x, axis):
    bit = 1
    while bit < lax.axis_size(axis):
        x = x + swap(x, axis, bit)
        bit *= 2
    return x


def here(blocks):
    ctx = lax.axis_index("ctx")
    return ctx, ctx // blocks, ctx % blocks, ctx % 2


def pick_kernel(select_ref, hidden_ref, own_ref, keep_ref, send_ref):
    slots, width = own_ref.shape
    half = width // 2
    core = lax.axis_index("ctx") % 2
    own = jnp.dot(select_ref[...], hidden_ref[...], preferred_element_type=F32)
    squares = jnp.sum(own * own, axis=1, keepdims=True)
    high = squares.astype(BF16).astype(F32)
    middle = (squares - high).astype(BF16).astype(F32)
    low = squares - high - middle
    lane = lax.broadcasted_iota(jnp.int32, (slots, LANES), 1)
    tail = jnp.where(lane == 0, high, jnp.where(lane == 1, middle, jnp.where(lane == 2, low, 0.0)))
    own = own.astype(BF16)
    own_ref[...] = own
    keep_ref[:, half:] = tail.astype(BF16)
    send_ref[:, half:] = tail.astype(BF16)

    @pl.when(core == 0)
    def _():
        keep_ref[:, :half] = own[:, :half]
        send_ref[:, :half] = own[:, half:]

    @pl.when(core == 1)
    def _():
        keep_ref[:, :half] = own[:, half:]
        send_ref[:, :half] = own[:, :half]


def add_kernel(first_ref, second_ref, out_ref):
    out_ref[...] = first_ref[...] + second_ref[...]


def load_kernel(start, head_ref, dep_ref, out_ref, sem):
    del dep_ref
    copy = pltpu.make_async_copy(head_ref.at[:, pl.ds(start, out_ref.shape[1])], out_ref, sem)
    copy.start()
    copy.wait()


def normalize_kernel(
    blocks, model_width, mine_ref, mine_other_ref, there_ref, there_other_ref, squares_ref,
    there_squares_ref, gain_ref, left_ref, right_ref, scaled_ref, inverse_ref,
):
    slots = mine_ref.shape[0]
    half = mine_ref.shape[1] - LANES
    _, seq, _, core = here(blocks)
    for a_ref, b_ref, s_ref, s in (
        (mine_ref, mine_other_ref, squares_ref, seq),
        (there_ref, there_other_ref, there_squares_ref, 1 - seq),
    ):
        rows = pl.ds(pl.multiple_of(s * slots, slots), slots)
        inverse = lax.rsqrt(s_ref[...] / model_width + EPSILON)
        inverse_ref[rows, :] = inverse
        inverse = inverse[:, :1]
        a = a_ref[:, :half].astype(F32)
        b = b_ref[:, :half].astype(F32)
        for part, part_ref, start in (
            (jnp.where(core == 0, a, b), left_ref, 0),
            (jnp.where(core == 0, b, a), right_ref, half),
        ):
            scaled = part * inverse
            scaled_ref[rows, start : start + half] = scaled
            part_ref[rows, :] = (scaled * gain_ref[:, start : start + half]).astype(BF16)


def targets_kernel(voc, ref, dep_ref, out_ref):
    del dep_ref
    total = out_ref.shape[0]
    slots = total // 2
    place = lax.broadcasted_iota(jnp.int32, out_ref.shape, 0)
    out = jnp.zeros(out_ref.shape, jnp.int32)
    for r in range(total):
        out = jnp.where(place == r, ref[r // slots, r % slots], out)
    out_ref[...] = out - lax.axis_index("ctx") * voc


def stats_kernel(targets_ref, first_ref, second_ref, logits_ref, exps_ref, table_ref):
    total, voc = first_ref.shape
    logits = first_ref[...] + second_ref[...]
    logits_ref[...] = logits
    is_target = lax.broadcasted_iota(jnp.int32, (total, voc), 1) == targets_ref[:, 0:1]
    top = jnp.max(logits, axis=1, keepdims=True)
    away = logits - top
    exps = jnp.exp(away)
    exps_ref[:total, :] = jnp.where(is_target, 0.0, exps).astype(BF16)
    exps_ref[total:, :] = jnp.where(is_target, 1.0, 0.0).astype(BF16)
    entries = (
        top,
        jnp.sum(exps, axis=1, keepdims=True),
        jnp.sum(exps * away, axis=1, keepdims=True),
        jnp.sum(jnp.where(is_target, logits, 0.0), axis=1, keepdims=True),
    )
    lane = lax.broadcasted_iota(jnp.int32, (LANES, LANES), 1)
    table = jnp.zeros((LANES, LANES), F32)
    for k, entry in enumerate(entries):
        entry = jnp.concatenate([entry, jnp.zeros((LANES - total, 1), F32)]) if total < LANES else entry
        table = jnp.where(lane == k, entry, table)
    table_ref[...] = table.T[:SUBLANES, :]


def merged(first, second):
    top = jnp.maximum(first[0:1], second[0:1])
    gap_first = first[0:1] - top
    gap_second = second[0:1] - top
    exp_first = jnp.exp(gap_first)
    exp_second = jnp.exp(gap_second)
    return (
        top,
        first[1:2] * exp_first + second[1:2] * exp_second,
        (first[2:3] + gap_first * first[1:2]) * exp_first
        + (second[2:3] + gap_second * second[1:2]) * exp_second,
        first[3:4] + second[3:4],
    )


def merge_kernel(first_ref, second_ref, out_ref):
    out_ref[...] = jnp.zeros_like(out_ref)
    for k, row in enumerate(merged(first_ref, second_ref)):
        out_ref[k : k + 1, :] = row


def combine_kernel(
    length, model_width, num_ref, den_ref, own_ref, a_ref, b_ref, part_left_ref, part_right_ref,
    scaled_ref, inverse_ref, keep_ref, send_ref, meta_ref, loss_ref, tail_ref, near_ref,
):
    total = inverse_ref.shape[0]
    slots = total // 2
    half = part_left_ref.shape[1]
    core = lax.axis_index("ctx") % 2
    row_top, exp_total, moment, picked = merged(a_ref, b_ref)
    log_total = row_top + jnp.log(exp_total)
    place = lax.broadcasted_iota(jnp.int32, (1, LANES), 1)
    den = jnp.where(place < slots, den_ref[0], den_ref[1]).astype(F32)
    num = jnp.where(place < slots, num_ref[0], num_ref[1]).astype(F32)
    factor = den / (num * (2.0 * length))
    loss_ref[...] = jnp.sum(
        jnp.where(place < total, factor * (log_total - picked), 0.0), axis=1, keepdims=True
    )
    scale = LOSS_SCALE * factor
    inner = scale * (moment / exp_total - (picked - row_top)) / model_width
    spread = scale * jnp.exp(own_ref[0:1, :] - log_total)
    at_target = scale * (jnp.exp(picked - log_total) - 1.0)
    near_ref[...] = jnp.zeros_like(near_ref)
    for k, row in enumerate((log_total, scale, inner, spread, at_target)):
        near_ref[k : k + 1, :] = row
    across = jnp.concatenate([near_ref[...], jnp.zeros((LANES - SUBLANES, LANES), F32)]).T[:total]
    lane = lax.broadcasted_iota(jnp.int32, (total, LANES), 1)
    meta_ref[...] = jnp.where(lane == 2, across / inverse_ref[...], across)
    spread = across[:, 3:4]
    at_target = across[:, 4:5]
    for side, part_ref in enumerate((part_left_ref, part_right_ref)):
        columns = slice(side * half, (side + 1) * half)
        part = spread * part_ref[:total, :] + at_target * part_ref[total:, :]
        gain = jnp.sum(part * scaled_ref[:, columns], axis=0, keepdims=True)
        tail_ref[...] = jnp.zeros_like(tail_ref)
        for j in range(half // LANES):
            tail_ref[j : j + 1, :] = gain[:, j * LANES : (j + 1) * LANES]

        @pl.when(core == side)
        def _():
            keep_ref[:, :half] = part
            keep_ref[:, half:] = tail_ref[...]

        @pl.when(core != side)
        def _():
            send_ref[:, :half] = part.astype(BF16)
            send_ref[:, half:] = tail_ref[...].astype(BF16)


def divide_kernel(blocks, keep_ref, arrived_ref, own_ref, give_ref):
    slots = own_ref.shape[0]
    half = own_ref.shape[1] - LANES
    _, seq, _, _ = here(blocks)
    tail = (keep_ref[:slots, half:] + arrived_ref[:slots, half:].astype(F32)).astype(BF16)
    for ref, s in ((own_ref, seq), (give_ref, 1 - seq)):
        rows = pl.ds(pl.multiple_of(s * slots, slots), slots)
        part = keep_ref[rows, :half] + arrived_ref[rows, :half].astype(F32)
        ref[:, :half] = part.astype(ref.dtype)
        ref[:, half:] = tail.astype(ref.dtype)


def dlogits_kernel(targets_ref, logits_ref, meta_ref, dep_ref, out_ref):
    del dep_ref
    total, voc = logits_ref.shape
    is_target = lax.broadcasted_iota(jnp.int32, (total, voc), 1) == targets_ref[:, 0:1]
    softmax = jnp.exp(logits_ref[...] - meta_ref[:, 0:1])
    out_ref[...] = (
        (meta_ref[:, 1:2] * (softmax - jnp.where(is_target, 1.0, 0.0))).T.astype(BF16)
    )


def head_kernel(dlogits_ref, normed_ref, *rest):
    rest[-1][...] = jnp.dot(
        dlogits_ref[...], normed_ref[...], preferred_element_type=F32
    ).astype(BF16)


def final_kernel(
    blocks, select_ref, mine_ref, other_ref, own_ref, inverse_ref, meta_ref, gain_ref, out_ref,
    grad_gain_ref, block_ref, sems,
):
    chunks, _, step = block_ref.shape
    slots = mine_ref.shape[0]
    half = mine_ref.shape[1] - LANES
    _, seq, _, core = here(blocks)
    rows = pl.ds(pl.multiple_of(seq * slots, slots), slots)
    inverse = inverse_ref[rows, :][:, :1]
    pull = inverse * inverse * inverse * meta_ref[rows, :][:, 2:3]
    copies = []
    for chunk in range(chunks):
        start = chunk * step
        columns = slice(start, start + step)
        inner = slice(start % half, start % half + step)
        dnormed = jnp.where(
            core == start // half,
            mine_ref[:, inner].astype(F32),
            other_ref[:, inner].astype(F32),
        )
        grads = inverse * gain_ref[:, columns] * dnormed - own_ref[:, columns].astype(F32) * pull
        block_ref[chunk] = lax.dot_general(
            select_ref[...],
            grads.astype(BF16),
            (((0,), (0,)), ((), ())),
            preferred_element_type=F32,
        ).astype(BF16)
        copies.append(
            pltpu.make_async_copy(block_ref.at[chunk], out_ref.at[:, columns], sems.at[chunk])
        )
        copies[-1].start()
    a = mine_ref[:, half:].astype(F32)
    b = other_ref[:, half:].astype(F32)
    for start, tail in ((0, jnp.where(core == 0, a, b)), (half, jnp.where(core == 0, b, a))):
        for j in range(half // LANES):
            grad_gain_ref[:, start + j * LANES : start + (j + 1) * LANES] = tail[j : j + 1, :]
    for copy in copies:
        copy.wait()


def device_step(hidden, norm_gain, head, masked_pos, masked_targets, t_num, t_den):
    tok, width = hidden.shape
    voc = head.shape[0]
    count = lax.axis_size("ctx")
    model_width = width * lax.axis_size("vocab")
    blocks = count // 2
    slots = masked_pos.shape[1]
    total = 2 * slots
    half = width // 2
    packed_width = half + LANES
    inner_bits = [1 << b for b in range(1, count.bit_length() - 2)]
    gain_row = norm_gain.reshape(1, width)

    ctx = lax.axis_index("ctx")
    local = masked_pos[ctx // blocks] - ctx % blocks * tok
    select = (jnp.arange(tok, dtype=jnp.int32)[None, :] == local[:, None]).astype(BF16)

    own, keep, send = pl.pallas_call(
        pick_kernel,
        in_specs=[vmem()] * 2,
        out_specs=[vmem()] * 3,
        out_shape=[shape((slots, width), BF16)] + [shape((slots, packed_width), BF16)] * 2,
        compiler_params=params(12),
        name="pick",
    )(select, hidden)

    mine = pl.pallas_call(
        add_kernel,
        in_specs=[vmem()] * 2,
        out_specs=vmem(),
        out_shape=shape((slots, packed_width), BF16),
        compiler_params=params(4),
        cost_estimate=cost(64 * MIB),
        name="add",
    )(keep, swap(send, "ctx", 1))

    def load(start, dep):
        return pl.pallas_call(
            lambda *refs: load_kernel(start, *refs),
            in_specs=[anywhere(), anywhere()],
            out_specs=vmem(),
            out_shape=shape((voc, half), BF16),
            scratch_shapes=[pltpu.SemaphoreType.DMA(())],
            compiler_params=params(46),
            cost_estimate=cost(voc * half * 4),
            name="load",
        )(head, dep)

    loads = []
    for k, bit in enumerate(inner_bits):
        at = k - len(inner_bits) + 2
        before = mine
        mine = before + swap(before, "ctx", bit)
        if at >= 0:
            loads.append(load(half * at, before))
    targets = pl.pallas_call(
        lambda *refs: targets_kernel(voc, *refs),
        in_specs=[smem(), anywhere()],
        out_specs=vmem(),
        out_shape=shape((total, LANES), jnp.int32),
        compiler_params=params(4),
        name="targets",
    )(masked_targets, mine)
    there = swap(mine, "ctx", blocks)

    def squares_of(x):
        part = jnp.sum(x[:, half : half + 3].astype(F32), axis=1, keepdims=True)
        return jnp.broadcast_to(part, (slots, LANES))

    mine_squares = squares_of(mine)
    mine_other = swap(mine, "ctx", 1)
    ways = lax.axis_size("vocab")
    if ways == 2:
        across = lax.ppermute(
            mine_squares,
            ("ctx", "vocab"),
            [(i, i ^ (blocks * ways + 1)) for i in range(count * ways)],
        )
        mine_squares = mine_squares + swap(mine_squares, "vocab", 1)
        there_squares = squares_of(there) + across
    else:
        mine_squares = sum_over(mine_squares, "vocab")
        there_squares = sum_over(squares_of(there), "vocab")
    there_other = swap(there, "ctx", 1)
    left, right, scaled, inverse = pl.pallas_call(
        lambda *refs: normalize_kernel(blocks, model_width, *refs),
        in_specs=[vmem()] * 7,
        out_specs=[vmem()] * 4,
        out_shape=[
            shape((total, half), BF16),
            shape((total, half), BF16),
            shape((total, width), F32),
            shape((total, LANES), F32),
        ],
        compiler_params=params(8),
        name="normalize",
    )(mine, mine_other, there, there_other, mine_squares, there_squares, gain_row)

    partial = sum(
        lax.dot_general(a, b, (((1,), (1,)), ((), ())), preferred_element_type=F32)
        for a, b in zip((left, right), loads)
    )
    bit = 1
    while 2 * bit < lax.axis_size("vocab"):
        partial = partial + swap(partial, "vocab", bit)
        bit *= 2
    logits, exps, table = pl.pallas_call(
        stats_kernel,
        in_specs=[vmem()] * 3,
        out_specs=[vmem()] * 3,
        out_shape=[
            shape((total, voc), F32),
            shape((2 * total, voc), BF16),
            shape((SUBLANES, LANES), F32),
        ],
        compiler_params=params(8),
        name="stats",
    )(targets, partial, swap(partial, "vocab", bit))

    own_table = table

    def merge(a, b):
        return pl.pallas_call(
            merge_kernel,
            in_specs=[vmem()] * 2,
            out_specs=vmem(),
            out_shape=shape((SUBLANES, LANES), F32),
            compiler_params=params(4),
            name="merge",
        )(a, b)

    bits = [1] + inner_bits
    for bit in bits:
        table = merge(table, swap(table, "ctx", bit))
    there_table = swap(table, "ctx", blocks)
    parts = [jnp.dot(exps, block, preferred_element_type=F32) for block in loads]

    keep, send, meta, loss_value = pl.pallas_call(
        lambda *refs: combine_kernel(tok * blocks, model_width, *refs),
        in_specs=[smem(), smem()] + [vmem()] * 7,
        out_specs=[vmem()] * 4,
        out_shape=[
            shape((total, packed_width), F32),
            shape((total, packed_width), BF16),
            shape((total, LANES), F32),
            shape((1, 1), F32),
        ],
        scratch_shapes=[pltpu.VMEM((total, LANES), F32)]
        + [pltpu.VMEM((SUBLANES, LANES), F32)],
        compiler_params=params(10),
        name="combine",
    )(t_num, t_den, own_table, table, there_table, *parts, scaled, inverse)

    steps = 8
    step = width // steps
    grad_head = None

    def head_part(first, last, dep, so_far):
        extra = [dep] + ([] if so_far is None else [so_far])
        return pl.pallas_call(
            head_kernel,
            grid=(last - first,),
            in_specs=[
                pl.BlockSpec((voc, total), lambda i: (0, 0)),
                pl.BlockSpec((total, step), lambda i: (0, first % (steps // 2) + i)),
            ]
            + [anywhere()] * len(extra),
            out_specs=pl.BlockSpec((voc, step), lambda i: (0, first + i)),
            out_shape=shape((voc, width), BF16),
            input_output_aliases={} if so_far is None else {3: 0},
            compiler_params=params(12),
            cost_estimate=cost(2 * voc * step * (last - first)),
            name="head_grad",
        )(dlogits, right if first >= steps // 2 else left, *extra)

    arrived = swap(send, "ctx", 1)
    own_part, give = pl.pallas_call(
        lambda *refs: divide_kernel(blocks, *refs),
        in_specs=[vmem()] * 2,
        out_specs=[vmem()] * 2,
        out_shape=[shape((slots, packed_width), F32), shape((slots, packed_width), BF16)],
        compiler_params=params(6),
        name="divide",
    )(keep, arrived)
    cuts = [0, 4, 6, 8]
    dlogits = pl.pallas_call(
        dlogits_kernel,
        in_specs=[vmem()] * 3 + [anywhere()],
        out_specs=vmem(),
        out_shape=shape((voc, total), BF16),
        compiler_params=params(6),
        name="dlogits",
    )(targets, logits, meta, give)
    grad_head = head_part(cuts[0], cuts[1], give, None)
    sent = (own_part + swap(give, "ctx", blocks).astype(F32)).astype(BF16)
    for k, bit in enumerate(inner_bits):
        at = k - len(inner_bits) + 2
        before = sent
        sent = before + swap(before, "ctx", bit)
        if at >= 0:
            grad_head = head_part(cuts[at + 1], cuts[at + 2], before, grad_head)
    other = swap(sent, "ctx", 1)

    final_step = half // 2
    grad_hidden, grad_gain = pl.pallas_call(
        lambda *refs: final_kernel(blocks, *refs),
        in_specs=[vmem()] * 7,
        out_specs=[anywhere(), vmem()],
        out_shape=[shape((tok, width), BF16), shape((1, width), F32)],
        scratch_shapes=[
            pltpu.VMEM((width // final_step, tok, final_step), BF16),
            pltpu.SemaphoreType.DMA((width // final_step,)),
        ],
        compiler_params=params(12),
        name="final",
    )(select, sent, other, own, inverse, meta, gain_row)
    return (loss_value.reshape(()), grad_hidden, grad_head, grad_gain.reshape(width))


def solution(mesh):
    placed = (P("ctx", "vocab"), P("vocab"), P("ctx", "vocab"), P(), P(), P(), P())
    return jax.shard_map(
        device_step,
        mesh=mesh,
        in_specs=placed,
        out_specs=(P(), P("ctx", "vocab"), P("ctx", "vocab"), P("vocab")),
        check_vma=False,
    )
```

time: 293 us -> 78.5 us (0.27)
  blocking collectives: 136 us -> 0 us
  waiting for transfers between devices: 98.2 us -> 34.1 us
  starting transfers between devices: 0.12 us -> 19.6 us
  Pallas kernels: 0 us -> 16.6 us
  between operations: 16.6 us -> 0.8 us
  matrix products: 18.7 us -> 4.21 us
  other arithmetic: 14.1 us -> 1.23 us
  local copies, waits for them, and re-layouts: 9.14 us -> 1.68 us
    psum x3 -> x0, blocking collectives: 69.1 us -> none  [the longest x1 57.6 us: on_device(): lax.psum(jnp.sum(own_grad * own_rows * inverse[:, None], axis=0), 'ctx')]
    unnamed x1 -> x0, blocking collectives: 61 us -> none
    reduce_scatter x2 -> x0, waiting for transfers between devices: 58.5 us -> none  [the longest x1 52.7 us: on_device(): lax.psum_scatter(jnp.dot(all_grads, head, preferred_element_type=jnp.floa...]
    all_gather x1 -> x0, waiting for transfers between devices: 39.7 us -> none  [on_device(): normed_all = lax.all_gather(normed_own, 'ctx', axis=0, tiled=True)]
    ppermute x0 -> x18, waiting for transfers between devices: none -> 34.1 us  [the longest x17 31.5 us: swap(): lax.ppermute(x, axis, [(i, i ^ bit) for i in range(lax.axis_size(axis))])]
    ppermute x0 -> x18, starting transfers between devices: none -> 19.6 us  [the longest x17 19.6 us: swap(): lax.ppermute(x, axis, [(i, i ^ bit) for i in range(lax.axis_size(axis))])]
    pallas_call x0 -> x17, Pallas kernels: none -> 16.6 us  [the longest x3 6.68 us: head_part(): pl.pallas_call(head_kernel, grid=(last - first,), in_specs=[pl.BlockSpec(...]
    dot_general x3 -> x4, matrix products: 18.7 us -> 4.21 us  [the longest x2 2.55 us: device_step(): lax.dot_general(a, b, (((1,), (1,)), ((), ())), preferred_element_type=F32)]
  transfers between devices with their start and end apart: 3 -> 18, of which waited for: 3 -> 14; matrix products, arithmetic and copies ran while one was open for 4% -> 2% of each run, Pallas kernels for 0% -> 15%
where the time goes in v1:
time: 78.5 us; the launch traced here: 78.2 us
  waiting for transfers between devices  34.1 us (43%)
  starting transfers between devices  19.6 us (25%)
  Pallas kernels  16.6 us (21%)
  matrix products  4.21 us (5%)
  local copies, waits for them, and re-layouts  1.68 us (2%)
  other arithmetic  1.23 us (2%)
  between operations  0.8 us (1%)
    ppermute x17, waiting for transfers between devices, swap(): lax.ppermute(x, axis, [(i, i ^ bit) for i in range(lax.axis_size(axis))])  31.5 us
    ppermute x17, starting transfers between devices, swap(): lax.ppermute(x, axis, [(i, i ^ bit) for i in range(lax.axis_size(axis))])  19.6 us
    pallas_call x3, Pallas kernels, head_part(): pl.pallas_call(head_kernel, grid=(last - first,), in_specs=[pl.BlockSpec(...  6.68 us
    pallas_call x2, Pallas kernels, load(): pl.pallas_call(lambda *refs: load_kernel(start, *refs), in_specs=[anywher...  4.32 us
    ppermute x1, waiting for transfers between devices, device_step(): lax.ppermute(mine_squares, ('ctx', 'vocab'), [(i, i ^ blocks * ways + 1)...  2.64 us
    dot_general x2, matrix products, device_step(): lax.dot_general(a, b, (((1,), (1,)), ((), ())), preferred_element_type=F32)  2.55 us
    pallas_call x1, Pallas kernels, device_step(): pl.pallas_call(lambda *refs: final_kernel(blocks, *refs), in_specs=[vmem(...  2.37 us
    dot_general x2, matrix products, device_step(): jnp.dot(exps, block, preferred_element_type=F32)  1.66 us
  transfers between devices with their start and end apart: 18, of which 14 were waited for; matrix products, arithmetic and copies ran while one was open for 2% of the time, Pallas kernels for 15%

profile of v1, /device:TPU:0, one launch (start us, length us, event | category | flops | bytes accessed | tf_op | source)
XLA Modules:
  0.0 78.2 jit_solution(9684817992437805352)
XLA Ops:
  0.7 0.7 subtract_bitcast_fusion
  1.3 0.1 fusion.select_ref.refs_0_
  1.4 1.6 %copy-done = bf16[256,4096]{1,0:T(8,128)(2,1)S(1)} copy-done((bf16[256,4096]{1,0:T(8,128)(2,1)S(1)}, bf16[256,4096]{1,0:T(8,128)(2,1)}, u32[]{:S(2)}) %copy-start) | copy-done | bytes 2097176
  3.0 0.5 pick.1
  3.5 0.6 collective-permute-start
  4.1 0.9 %collective-permute-done.second_ref = bf16[16,2176]{1,0:T(8,128)(2,1)S(1)} collective-permute-done((bf16[16,2176]{1,0:T(8,128)(2,1)S(1)}, bf16[16,2176]{1,0:T(8,128)(2,1)S(1)}, u32[]{:S(2)}, u32[]{:S(2)}) %collective-permute-start) | collective-permute-done | bytes 69664 | tf_op jit(solution)/shard_map/ppermute | solution.py:43
  5.0 2.8 %collective-permute-start.1 = (bf16[16,2176]{1,0:T(8,128)(2,1)S(1)}, bf16[16,2176]{1,0:T(8,128)(2,1)S(1)}, u32[]{:S(2)}, u32[]{:S(2)}) collective-permute-start(bf16[16,2176]{1,0:T(8,128)(2,1)S(1)} %add.47.refs_1_), channel_id=1, source_target_pairs={{0,4},{2,6},{4,0},{6,2},{8,12},{10,14},{12,8},{14,10},{16,20},{18,... | collective-permute-start | bytes 208904 | tf_op jit(solution)/shard_map/ppermute | solution.py:43
  7.8 2.5 %collective-permute-done.1 = bf16[16,2176]{1,0:T(8,128)(2,1)S(1)} collective-permute-done((bf16[16,2176]{1,0:T(8,128)(2,1)S(1)}, bf16[16,2176]{1,0:T(8,128)(2,1)S(1)}, u32[]{:S(2)}, u32[]{:S(2)}) %collective-permute-start.1) | collective-permute-done | bytes 69664 | tf_op jit(solution)/shard_map/ppermute | solution.py:43
  10.3 2.0 %collective-permute-start.2 = (bf16[16,2176]{1,0:T(8,128)(2,1)S(1)}, bf16[16,2176]{1,0:T(8,128)(2,1)S(1)}, u32[]{:S(2)}, u32[]{:S(2)}) collective-permute-start(bf16[16,2176]{1,0:T(8,128)(2,1)S(1)} %add.35.refs_1_), channel_id=1, source_target_pairs={{0,8},{2,10},{4,12},{6,14},{8,0},{10,2},{12,4},{14,6},{16,24},{18,... | collective-permute-start | bytes 208904 | tf_op jit(solution)/shard_map/ppermute | solution.py:43
  12.3 2.4 %collective-permute-done.2 = bf16[16,2176]{1,0:T(8,128)(2,1)S(1)} collective-permute-done((bf16[16,2176]{1,0:T(8,128)(2,1)S(1)}, bf16[16,2176]{1,0:T(8,128)(2,1)S(1)}, u32[]{:S(2)}, u32[]{:S(2)}) %collective-permute-start.2) | collective-permute-done | bytes 69664 | tf_op jit(solution)/shard_map/ppermute | solution.py:43
  14.7 0.1 convert_reduce_fusion.1
  14.8 0.1 broadcast_in_dim.4
  14.9 1.8 %collective-permute-start.6 = (f32[16,128]{1,0:T(8,128)S(1)}, f32[16,128]{1,0:T(8,128)S(1)}, u32[]{:S(2)}, u32[]{:S(2)}) collective-permute-start(f32[16,128]{1,0:T(8,128)S(1)} %broadcast_in_dim.4), channel_id=1, source_target_pairs={{0,1},{1,0},{2,3},{3,2},{4,5},{5,4},{6,7},{7,6},{8,9},{9,8},{10,11... | collective-permute-start | bytes 24584 | tf_op jit(solution)/shard_map/ppermute | solution.py:43
  16.8 2.2 %load.2 = bf16[988,2048]{1,0:T(8,128)(2,1)S(1)} custom-call(bf16[988,4096]{1,0:T(8,128)(2,1)} %refs_0_.6, bf16[16,2176]{1,0:T(8,128)(2,1)S(1)} %add.47.refs_1_), custom_call_target="tpu_custom_call" | custom-call | bytes 8093696 | tf_op jit(solution)/shard_map/load/pallas_call | solution.py:333
  18.9 0.0 copy-start.1
  18.9 2.2 %load.3 = bf16[988,2048]{1,0:T(8,128)(2,1)S(1)} custom-call(bf16[988,4096]{1,0:T(8,128)(2,1)} %refs_0_.6, bf16[16,2176]{1,0:T(8,128)(2,1)S(1)} %add.35.refs_1_), custom_call_target="tpu_custom_call" | custom-call | bytes 8093696 | tf_op jit(solution)/shard_map/load/pallas_call | solution.py:333
  21.1 2.7 %collective-permute-start.4 = (bf16[16,2176]{1,0:T(8,128)(2,1)S(1)}, bf16[16,2176]{1,0:T(8,128)(2,1)S(1)}, u32[]{:S(2)}, u32[]{:S(2)}) collective-permute-start(bf16[16,2176]{1,0:T(8,128)(2,1)S(1)} %add.36.refs_1_.refs_0_), channel_id=1, source_target_pairs={{0,16},{2,18},{4,20},{6,22},{8,24},{10,26},{12,28},{14,30},{16,0},... | collective-permute-start | bytes 208904 | tf_op jit(solution)/shard_map/ppermute | solution.py:43
  23.8 0.0 collective-permute-start.7
  23.8 0.0 collective-permute-start.3
  23.8 0.0 collective-permute-done.6
  23.8 0.1 broadcast_add_fusion.1.refs_4_
  23.9 2.5 %collective-permute-done.4.refs_2_ = bf16[16,2176]{1,0:T(8,128)(2,1)S(1)} collective-permute-done((bf16[16,2176]{1,0:T(8,128)(2,1)S(1)}, bf16[16,2176]{1,0:T(8,128)(2,1)S(1)}, u32[]{:S(2)}, u32[]{:S(2)}) %collective-permute-start.4) | collective-permute-done | bytes 69664 | tf_op jit(solution)/shard_map/ppermute | solution.py:43
  26.4 0.1 convert_reduce_fusion
  26.5 0.1 collective-permute-start.5
  26.6 2.6 %collective-permute-done.7 = f32[16,128]{1,0:T(8,128)S(1)} collective-permute-done((f32[16,128]{1,0:T(8,128)S(1)}, f32[16,128]{1,0:T(8,128)S(1)}, u32[]{:S(2)}, u32[]{:S(2)}) %collective-permute-start.7) | collective-permute-done | bytes 8224 | tf_op jit(solution)/shard_map/ppermute | solution.py:369
  29.2 0.1 broadcast_add_fusion.refs_5_
  29.3 0.0 collective-permute-done.3.refs_1_
  29.3 0.0 collective-permute-done.5.refs_3_
  29.3 0.0 copy-done.1
  29.3 0.1 normalize.1
  29.4 0.0 copy-start.2
  29.4 1.3 %fusion.1 = f32[32,988]{1,0:T(8,128)S(1)} fusion(bf16[32,2048]{1,0:T(8,128)(2,1)S(1)} %get-tuple-element.25.normed_ref, bf16[988,2048]{1,0:T(8,128)(2,1)S(1)} %load.3), kind=kOutput, calls=%fused_computation.9 | convolution fusion | flops 129499136 | bytes 4304384 | tf_op jit(solution)/shard_map/dot_general | solution.py:395
  30.7 1.3 %convolution_add_fusion.first_ref = f32[32,988]{1,0:T(8,128)S(1)} fusion(f32[32,988]{1,0:T(8,128)S(1)} %fusion.1, bf16[32,2048]{1,0:T(8,128)(2,1)S(1)} %get-tuple-element.24.normed_ref, bf16[988,2048]{1,0:T(8,128)(2,1)S(1)} %load.2), kind=kOutput, calls=%fused_computation | convolution fusion | flops 129530752 | bytes 4430848 | tf_op jit(solution)/shard_map/dot_general | solution.py:395
  32.0 0.5 collective-permute-start.8
  32.5 0.6 targets.1.targets_ref
  33.1 3.9 %collective-permute-done.8.second_ref = f32[32,988]{1,0:T(8,128)S(1)} collective-permute-done((f32[32,988]{1,0:T(8,128)S(1)}, f32[32,988]{1,0:T(8,128)S(1)}, u32[]{:S(2)}, u32[]{:S(2)}) %collective-permute-start.8) | collective-permute-done | bytes 126496 | tf_op jit(solution)/shard_map/ppermute | solution.py:43
  37.0 0.4 stats.1
  37.4 0.0 collective-permute-start.9
  37.4 1.2 %collective-permute-done.9.second_ref = f32[8,128]{1,0:T(8,128)S(1)} collective-permute-done((f32[8,128]{1,0:T(8,128)S(1)}, f32[8,128]{1,0:T(8,128)S(1)}, u32[]{:S(2)}, u32[]{:S(2)}) %collective-permute-start.9) | collective-permute-done | bytes 4128 | tf_op jit(solution)/shard_map/ppermute | solution.py:43
  38.5 1.6 %collective-permute-start.10 = (f32[8,128]{1,0:T(8,128)S(1)}, f32[8,128]{1,0:T(8,128)S(1)}, u32[]{:S(2)}, u32[]{:S(2)}) collective-permute-start(f32[8,128]{1,0:T(8,128)S(1)} %merge.3.first_ref), channel_id=1, source_target_pairs={{0,4},{2,6},{4,0},{6,2},{8,12},{10,14},{12,8},{14,10},{16,20},{18,... | collective-permute-start | bytes 12296 | tf_op jit(solution)/shard_map/ppermute | solution.py:43
  40.1 2.1 %collective-permute-done.10.second_ref = f32[8,128]{1,0:T(8,128)S(1)} collective-permute-done((f32[8,128]{1,0:T(8,128)S(1)}, f32[8,128]{1,0:T(8,128)S(1)}, u32[]{:S(2)}, u32[]{:S(2)}) %collective-permute-start.10) | collective-permute-done | bytes 4128 | tf_op jit(solution)/shard_map/ppermute | solution.py:43
  42.2 1.6 %collective-permute-start.11 = (f32[8,128]{1,0:T(8,128)S(1)}, f32[8,128]{1,0:T(8,128)S(1)}, u32[]{:S(2)}, u32[]{:S(2)}) collective-permute-start(f32[8,128]{1,0:T(8,128)S(1)} %merge.4.first_ref), channel_id=1, source_target_pairs={{0,8},{2,10},{4,12},{6,14},{8,0},{10,2},{12,4},{14,6},{16,24},{18,... | collective-permute-start | bytes 12296 | tf_op jit(solution)/shard_map/ppermute | solution.py:43
  43.9 0.8 %fusion.3.refs_6_ = f32[64,2048]{1,0:T(8,128)S(1)} fusion(bf16[64,988]{1,0:T(8,128)(2,1)S(1)} %get-tuple-element.27, bf16[988,2048]{1,0:T(8,128)(2,1)S(1)} %load.3), kind=kOutput, calls=%fused_computation.11 | convolution fusion | flops 258998272 | bytes 4697600 | tf_op jit(solution)/shard_map/dot_general | solution.py:431
  44.7 1.2 %collective-permute-done.11.second_ref = f32[8,128]{1,0:T(8,128)S(1)} collective-permute-done((f32[8,128]{1,0:T(8,128)S(1)}, f32[8,128]{1,0:T(8,128)S(1)}, u32[]{:S(2)}, u32[]{:S(2)}) %collective-permute-start.11) | collective-permute-done | bytes 4128 | tf_op jit(solution)/shard_map/ppermute | solution.py:43
  45.9 2.0 %collective-permute-start.12 = (f32[8,128]{1,0:T(8,128)S(1)}, f32[8,128]{1,0:T(8,128)S(1)}, u32[]{:S(2)}, u32[]{:S(2)}) collective-permute-start(f32[8,128]{1,0:T(8,128)S(1)} %merge.5.refs_3_), channel_id=1, source_target_pairs={{0,16},{2,18},{4,20},{6,22},{8,24},{10,26},{12,28},{14,30},{16,0},... | collective-permute-start | bytes 12296 | tf_op jit(solution)/shard_map/ppermute | solution.py:43
  48.0 0.8 %fusion.2.refs_5_ = f32[64,2048]{1,0:T(8,128)S(1)} fusion(bf16[64,988]{1,0:T(8,128)(2,1)S(1)} %get-tuple-element.27, bf16[988,2048]{1,0:T(8,128)(2,1)S(1)} %load.2), kind=kOutput, calls=%fused_computation.10 | convolution fusion | flops 258998272 | bytes 4697600 | tf_op jit(solution)/shard_map/dot_general | solution.py:431
  48.8 1.7 %collective-permute-done.12.refs_4_ = f32[8,128]{1,0:T(8,128)S(1)} collective-permute-done((f32[8,128]{1,0:T(8,128)S(1)}, f32[8,128]{1,0:T(8,128)S(1)}, u32[]{:S(2)}, u32[]{:S(2)}) %collective-permute-start.12) | collective-permute-done | bytes 4128 | tf_op jit(solution)/shard_map/ppermute | solution.py:43
  50.5 0.0 copy-done.3
  50.5 1.4 %combine.1 = (f32[32,2176]{1,0:T(8,128)S(1)}, bf16[32,2176]{1,0:T(8,128)(2,1)S(1)}, f32[32,128]{1,0:T(8,128)S(1)}, f32[1,1]{1,0:T(1,128)}) custom-call(s32[2]{0:T(128)S(1)} %copy-done.3, s32[2]{0:T(128)S(1)} %copy-done.4, f32[8,128]{1,0:T(8,128)S(1)} %get-tuple-element.26.first_ref.refs_2_, f32[8,128]{1,0:T(8,128)S(1)} %merge.5.refs_3_, ...), custom_call_target="tpu_custom_call" | custom-call | tf_op jit(solution)/shard_map/combine/pallas_call | solution.py:433
  51.9 0.0 collective-permute-start.13
  51.9 1.4 %collective-permute-done.13.refs_1_ = bf16[32,2176]{1,0:T(8,128)(2,1)S(1)} collective-permute-done((bf16[32,2176]{1,0:T(8,128)(2,1)S(1)}, bf16[32,2176]{1,0:T(8,128)(2,1)S(1)}, u32[]{:S(2)}, u32[]{:S(2)}) %collective-permute-start.13) | collective-permute-done | bytes 139296 | tf_op jit(solution)/shard_map/ppermute | solution.py:43
  53.3 2.0 %collective-permute-start.14 = (bf16[16,2176]{1,0:T(8,128)(2,1)S(1)}, bf16[16,2176]{1,0:T(8,128)(2,1)S(1)}, u32[]{:S(2)}, u32[]{:S(2)}) collective-permute-start(bf16[16,2176]{1,0:T(8,128)(2,1)S(1)} %get-tuple-element.34.dep_ref.rest_0_), channel_id=1, source_target_pairs={{0,16},{2,18},{4,20},{6,22},{8,24},{10,26},{12,28},{14,30},{16,0},... | collective-permute-start | bytes 208904 | tf_op jit(solution)/shard_map/ppermute | solution.py:43
  55.3 4.7 %collective-permute-done.14 = bf16[16,2176]{1,0:T(8,128)(2,1)S(1)} collective-permute-done((bf16[16,2176]{1,0:T(8,128)(2,1)S(1)}, bf16[16,2176]{1,0:T(8,128)(2,1)S(1)}, u32[]{:S(2)}, u32[]{:S(2)}) %collective-permute-start.14) | collective-permute-done | bytes 69664 | tf_op jit(solution)/shard_map/ppermute | solution.py:43
  60.1 1.6 %collective-permute-start.15 = (bf16[16,2176]{1,0:T(8,128)(2,1)S(1)}, bf16[16,2176]{1,0:T(8,128)(2,1)S(1)}, u32[]{:S(2)}, u32[]{:S(2)}) collective-permute-start(bf16[16,2176]{1,0:T(8,128)(2,1)S(1)} %add_convert_fusion.rest_0_), channel_id=1, source_target_pairs={{0,4},{2,6},{4,0},{6,2},{8,12},{10,14},{12,8},{14,10},{16,20},{18,... | collective-permute-start | bytes 208904 | tf_op jit(solution)/shard_map/ppermute | solution.py:43
  61.6 2.8 %collective-permute-done.15 = bf16[16,2176]{1,0:T(8,128)(2,1)S(1)} collective-permute-done((bf16[16,2176]{1,0:T(8,128)(2,1)S(1)}, bf16[16,2176]{1,0:T(8,128)(2,1)S(1)}, u32[]{:S(2)}, u32[]{:S(2)}) %collective-permute-start.15) | collective-permute-done | bytes 69664 | tf_op jit(solution)/shard_map/ppermute | solution.py:43
  64.5 0.2 collective-permute-start.16
  64.6 4.2 %collective-permute-done.16 = bf16[16,2176]{1,0:T(8,128)(2,1)S(1)} collective-permute-done((bf16[16,2176]{1,0:T(8,128)(2,1)S(1)}, bf16[16,2176]{1,0:T(8,128)(2,1)S(1)}, u32[]{:S(2)}, u32[]{:S(2)}) %collective-permute-start.16) | collective-permute-done | bytes 69664 | tf_op jit(solution)/shard_map/ppermute | solution.py:43
  68.9 0.1 collective-permute-start.17
  68.9 0.3 dlogits.1.dlogits_ref
  69.2 3.2 %head_grad.3.rest_1_ = bf16[988,4096]{1,0:T(8,128)(2,1)} custom-call(bf16[988,32]{1,0:T(8,128)(2,1)S(1)} %dlogits.1.dlogits_ref, bf16[32,2048]{1,0:T(8,128)(2,1)S(1)} %get-tuple-element.24.normed_ref, bf16[16,2176]{1,0:T(8,128)(2,1)S(1)} %get-tuple-element.34.dep_ref.rest_0_), custom_call_target="tpu_custom_call" | custom-call | bytes 4046848 | tf_op jit(solution)/shard_map/head_grad/pallas_call | solution.py:455
  72.3 1.8 %head_grad.4.rest_1_ = bf16[988,4096]{1,0:T(8,128)(2,1)} custom-call(bf16[988,32]{1,0:T(8,128)(2,1)S(1)} %dlogits.1.dlogits_ref, bf16[32,2048]{1,0:T(8,128)(2,1)S(1)} %get-tuple-element.25.normed_ref, bf16[16,2176]{1,0:T(8,128)(2,1)S(1)} %add_convert_fusion.rest_0_, bf16[988,4096]{1,0:T(8,128)(2,1)} %head_grad.3.rest_1_), custom_call_target="tpu_custom_call", output_to_operand_aliasing={{}: (3, {})} | custom-call | bytes 2023424 | tf_op jit(solution)/shard_map/head_grad/pallas_call | solution.py:455
  74.1 1.8 %head_grad.5 = bf16[988,4096]{1,0:T(8,128)(2,1)} custom-call(bf16[988,32]{1,0:T(8,128)(2,1)S(1)} %dlogits.1.dlogits_ref, bf16[32,2048]{1,0:T(8,128)(2,1)S(1)} %get-tuple-element.25.normed_ref, bf16[16,2176]{1,0:T(8,128)(2,1)S(1)} %add.41.rest_0_, bf16[988,4096]{1,0:T(8,128)(2,1)} %head_grad.4.rest_1_), custom_call_target="tpu_custom_call", output_to_operand_aliasing={{}: (3, {})} | custom-call | bytes 2023424 | tf_op jit(solution)/shard_map/head_grad/pallas_call | solution.py:455
  75.9 0.0 collective-permute-done.17.refs_2_
  75.9 2.4 %final.1 = (bf16[256,4096]{1,0:T(8,128)(2,1)}, f32[1,4096]{1,0:T(1,128)}) custom-call(bf16[16,256]{1,0:T(8,128)(2,1)S(1)} %fusion.select_ref.refs_0_, bf16[16,2176]{1,0:T(8,128)(2,1)S(1)} %add.42.refs_1_, bf16[16,2176]{1,0:T(8,128)(2,1)S(1)} %collective-permute-done.17.refs_2_, bf16[16,4096]{1,0:T(8,128)(2,1)S(1)} %get-tuple-element.35.refs_3_, ...), custom_call_target="tpu_custom_call" | custom-call | tf_op jit(solution)/shard_map/final/pallas_call | solution.py:500
  (15 shorter events, 0.2 us)
Async XLA Ops:
  1.4 1.6 %copy-start = (bf16[256,4096]{1,0:T(8,128)(2,1)S(1)}, bf16[256,4096]{1,0:T(8,128)(2,1)}, u32[]{:S(2)}) copy-start(bf16[256,4096]{1,0:T(8,128)(2,1)} %hidden_ref.1) | copy-start | bytes 6291460
  3.5 1.5 %collective-permute-start = (bf16[16,2176]{1,0:T(8,128)(2,1)S(1)}, bf16[16,2176]{1,0:T(8,128)(2,1)S(1)}, u32[]{:S(2)}, u32[]{:S(2)}) collective-permute-start(bf16[16,2176]{1,0:T(8,128)(2,1)S(1)} %get-tuple-element.23), channel_id=1, source_target_pairs={{0,2},{2,0},{4,6},{6,4},{8,10},{10,8},{12,14},{14,12},{16,18},{18,... | collective-permute-start | bytes 208904 | tf_op jit(solution)/shard_map/ppermute | solution.py:43
  5.0 5.3 %collective-permute-start.1 = (bf16[16,2176]{1,0:T(8,128)(2,1)S(1)}, bf16[16,2176]{1,0:T(8,128)(2,1)S(1)}, u32[]{:S(2)}, u32[]{:S(2)}) collective-permute-start(bf16[16,2176]{1,0:T(8,128)(2,1)S(1)} %add.47.refs_1_), channel_id=1, source_target_pairs={{0,4},{2,6},{4,0},{6,2},{8,12},{10,14},{12,8},{14,10},{16,20},{18,... | collective-permute-start | bytes 208904 | tf_op jit(solution)/shard_map/ppermute | solution.py:43
  10.3 4.4 %collective-permute-start.2 = (bf16[16,2176]{1,0:T(8,128)(2,1)S(1)}, bf16[16,2176]{1,0:T(8,128)(2,1)S(1)}, u32[]{:S(2)}, u32[]{:S(2)}) collective-permute-start(bf16[16,2176]{1,0:T(8,128)(2,1)S(1)} %add.35.refs_1_), channel_id=1, source_target_pairs={{0,8},{2,10},{4,12},{6,14},{8,0},{10,2},{12,4},{14,6},{16,24},{18,... | collective-permute-start | bytes 208904 | tf_op jit(solution)/shard_map/ppermute | solution.py:43
  14.9 8.9 %collective-permute-start.6 = (f32[16,128]{1,0:T(8,128)S(1)}, f32[16,128]{1,0:T(8,128)S(1)}, u32[]{:S(2)}, u32[]{:S(2)}) collective-permute-start(f32[16,128]{1,0:T(8,128)S(1)} %broadcast_in_dim.4), channel_id=1, source_target_pairs={{0,1},{1,0},{2,3},{3,2},{4,5},{5,4},{6,7},{7,6},{8,9},{9,8},{10,11... | collective-permute-start | bytes 24584 | tf_op jit(solution)/shard_map/ppermute | solution.py:43
  18.9 10.4 %copy-start.1 = (f32[4096]{0:T(1024)S(1)}, f32[4096]{0:T(1024)}, u32[]{:S(2)}) copy-start(f32[4096]{0:T(1024)} %param.8) | copy-start | bytes 49156
  21.1 5.3 %collective-permute-start.4 = (bf16[16,2176]{1,0:T(8,128)(2,1)S(1)}, bf16[16,2176]{1,0:T(8,128)(2,1)S(1)}, u32[]{:S(2)}, u32[]{:S(2)}) collective-permute-start(bf16[16,2176]{1,0:T(8,128)(2,1)S(1)} %add.36.refs_1_.refs_0_), channel_id=1, source_target_pairs={{0,16},{2,18},{4,20},{6,22},{8,24},{10,26},{12,28},{14,30},{16,0},... | collective-permute-start | bytes 208904 | tf_op jit(solution)/shard_map/ppermute | solution.py:43
  23.8 5.4 %collective-permute-start.7 = (f32[16,128]{1,0:T(8,128)S(1)}, f32[16,128]{1,0:T(8,128)S(1)}, u32[]{:S(2)}, u32[]{:S(2)}) collective-permute-start(f32[16,128]{1,0:T(8,128)S(1)} %broadcast_in_dim.4), channel_id=1, source_target_pairs={{0,17},{1,16},{2,19},{3,18},{4,21},{5,20},{6,23},{7,22},{8,25},{9,... | collective-permute-start | bytes 24584 | tf_op jit(solution)/shard_map/ppermute | solution.py:369
  23.8 5.5 %collective-permute-start.3 = (bf16[16,2176]{1,0:T(8,128)(2,1)S(1)}, bf16[16,2176]{1,0:T(8,128)(2,1)S(1)}, u32[]{:S(2)}, u32[]{:S(2)}) collective-permute-start(bf16[16,2176]{1,0:T(8,128)(2,1)S(1)} %add.36.refs_1_.refs_0_), channel_id=1, source_target_pairs={{0,2},{2,0},{4,6},{6,4},{8,10},{10,8},{12,14},{14,12},{16,18},{18,... | collective-permute-start | bytes 208904 | tf_op jit(solution)/shard_map/ppermute | solution.py:43
  26.5 2.8 %collective-permute-start.5 = (bf16[16,2176]{1,0:T(8,128)(2,1)S(1)}, bf16[16,2176]{1,0:T(8,128)(2,1)S(1)}, u32[]{:S(2)}, u32[]{:S(2)}) collective-permute-start(bf16[16,2176]{1,0:T(8,128)(2,1)S(1)} %collective-permute-done.4.refs_2_), channel_id=1, source_target_pairs={{0,2},{2,0},{4,6},{6,4},{8,10},{10,8},{12,14},{14,12},{16,18},{18,... | collective-permute-start | bytes 208904 | tf_op jit(solution)/shard_map/ppermute | solution.py:43
  29.4 3.1 %copy-start.2 = (s32[2,16]{1,0:T(2,128)S(1)}, s32[2,16]{1,0:T(2,128)}, u32[]{:S(2)}) copy-start(s32[2,16]{1,0:T(2,128)} %refs_0_.4) | copy-start | bytes 388
  32.0 5.0 %collective-permute-start.8 = (f32[32,988]{1,0:T(8,128)S(1)}, f32[32,988]{1,0:T(8,128)S(1)}, u32[]{:S(2)}, u32[]{:S(2)}) collective-permute-start(f32[32,988]{1,0:T(8,128)S(1)} %convolution_add_fusion.first_ref), channel_id=1, source_target_pairs={{0,1},{1,0},{2,3},{3,2},{4,5},{5,4},{6,7},{7,6},{8,9},{9,8},{10,11... | collective-permute-start | bytes 379400 | tf_op jit(solution)/shard_map/ppermute | solution.py:43
  37.4 1.2 %collective-permute-start.9 = (f32[8,128]{1,0:T(8,128)S(1)}, f32[8,128]{1,0:T(8,128)S(1)}, u32[]{:S(2)}, u32[]{:S(2)}) collective-permute-start(f32[8,128]{1,0:T(8,128)S(1)} %get-tuple-element.26.first_ref.refs_2_), channel_id=1, source_target_pairs={{0,2},{2,0},{4,6},{6,4},{8,10},{10,8},{12,14},{14,12},{16,18},{18,... | collective-permute-start | bytes 12296 | tf_op jit(solution)/shard_map/ppermute | solution.py:43
  38.5 3.7 %collective-permute-start.10 = (f32[8,128]{1,0:T(8,128)S(1)}, f32[8,128]{1,0:T(8,128)S(1)}, u32[]{:S(2)}, u32[]{:S(2)}) collective-permute-start(f32[8,128]{1,0:T(8,128)S(1)} %merge.3.first_ref), channel_id=1, source_target_pairs={{0,4},{2,6},{4,0},{6,2},{8,12},{10,14},{12,8},{14,10},{16,20},{18,... | collective-permute-start | bytes 12296 | tf_op jit(solution)/shard_map/ppermute | solution.py:43
  42.2 3.7 %collective-permute-start.11 = (f32[8,128]{1,0:T(8,128)S(1)}, f32[8,128]{1,0:T(8,128)S(1)}, u32[]{:S(2)}, u32[]{:S(2)}) collective-permute-start(f32[8,128]{1,0:T(8,128)S(1)} %merge.4.first_ref), channel_id=1, source_target_pairs={{0,8},{2,10},{4,12},{6,14},{8,0},{10,2},{12,4},{14,6},{16,24},{18,... | collective-permute-start | bytes 12296 | tf_op jit(solution)/shard_map/ppermute | solution.py:43
  43.9 6.6 %copy-start.3 = (s32[2]{0:T(128)S(1)}, s32[2]{0:T(128)}, u32[]{:S(2)}) copy-start(s32[2]{0:T(128)} %refs_0_.7) | copy-start | bytes 28
  43.9 6.6 %copy-start.4 = (s32[2]{0:T(128)S(1)}, s32[2]{0:T(128)}, u32[]{:S(2)}) copy-start(s32[2]{0:T(128)} %refs_1_.1) | copy-start | bytes 28
  45.9 4.6 %collective-permute-start.12 = (f32[8,128]{1,0:T(8,128)S(1)}, f32[8,128]{1,0:T(8,128)S(1)}, u32[]{:S(2)}, u32[]{:S(2)}) collective-permute-start(f32[8,128]{1,0:T(8,128)S(1)} %merge.5.refs_3_), channel_id=1, source_target_pairs={{0,16},{2,18},{4,20},{6,22},{8,24},{10,26},{12,28},{14,30},{16,0},... | collective-permute-start | bytes 12296 | tf_op jit(solution)/shard_map/ppermute | solution.py:43
  51.9 1.4 %collective-permute-start.13 = (bf16[32,2176]{1,0:T(8,128)(2,1)S(1)}, bf16[32,2176]{1,0:T(8,128)(2,1)S(1)}, u32[]{:S(2)}, u32[]{:S(2)}) collective-permute-start(bf16[32,2176]{1,0:T(8,128)(2,1)S(1)} %get-tuple-element.32), channel_id=1, source_target_pairs={{0,2},{2,0},{4,6},{6,4},{8,10},{10,8},{12,14},{14,12},{16,18},{18,... | collective-permute-start | bytes 417800 | tf_op jit(solution)/shard_map/ppermute | solution.py:43
  53.3 6.8 %collective-permute-start.14 = (bf16[16,2176]{1,0:T(8,128)(2,1)S(1)}, bf16[16,2176]{1,0:T(8,128)(2,1)S(1)}, u32[]{:S(2)}, u32[]{:S(2)}) collective-permute-start(bf16[16,2176]{1,0:T(8,128)(2,1)S(1)} %get-tuple-element.34.dep_ref.rest_0_), channel_id=1, source_target_pairs={{0,16},{2,18},{4,20},{6,22},{8,24},{10,26},{12,28},{14,30},{16,0},... | collective-permute-start | bytes 208904 | tf_op jit(solution)/shard_map/ppermute | solution.py:43
  60.1 4.4 %collective-permute-start.15 = (bf16[16,2176]{1,0:T(8,128)(2,1)S(1)}, bf16[16,2176]{1,0:T(8,128)(2,1)S(1)}, u32[]{:S(2)}, u32[]{:S(2)}) collective-permute-start(bf16[16,2176]{1,0:T(8,128)(2,1)S(1)} %add_convert_fusion.rest_0_), channel_id=1, source_target_pairs={{0,4},{2,6},{4,0},{6,2},{8,12},{10,14},{12,8},{14,10},{16,20},{18,... | collective-permute-start | bytes 208904 | tf_op jit(solution)/shard_map/ppermute | solution.py:43
  64.5 4.4 %collective-permute-start.16 = (bf16[16,2176]{1,0:T(8,128)(2,1)S(1)}, bf16[16,2176]{1,0:T(8,128)(2,1)S(1)}, u32[]{:S(2)}, u32[]{:S(2)}) collective-permute-start(bf16[16,2176]{1,0:T(8,128)(2,1)S(1)} %add.41.rest_0_), channel_id=1, source_target_pairs={{0,8},{2,10},{4,12},{6,14},{8,0},{10,2},{12,4},{14,6},{16,24},{18,... | collective-permute-start | bytes 208904 | tf_op jit(solution)/shard_map/ppermute | solution.py:43
  68.9 7.0 %collective-permute-start.17 = (bf16[16,2176]{1,0:T(8,128)(2,1)S(1)}, bf16[16,2176]{1,0:T(8,128)(2,1)S(1)}, u32[]{:S(2)}, u32[]{:S(2)}) collective-permute-start(bf16[16,2176]{1,0:T(8,128)(2,1)S(1)} %add.42.refs_1_), channel_id=1, source_target_pairs={{0,2},{2,0},{4,6},{6,4},{8,10},{10,8},{12,14},{14,12},{16,18},{18,... | collective-permute-start | bytes 208904 | tf_op jit(solution)/shard_map/ppermute | solution.py:43

commit v2 on v1

v2 whole, which is shorter than its diff:
```python
import jax
import jax.numpy as jnp
from jax import lax
from jax.experimental import pallas as pl
from jax.experimental.pallas import tpu as pltpu
from jax.sharding import PartitionSpec as P


EPSILON = 1e-05
LOSS_SCALE = 1024.0
LANES = 128
SUBLANES = 8
MIB = 1 << 20
F32 = jnp.float32
BF16 = jnp.bfloat16


def vmem():
    return pl.BlockSpec(memory_space=pltpu.VMEM)


def smem():
    return pl.BlockSpec(memory_space=pltpu.SMEM)


def anywhere():
    return pl.BlockSpec(memory_space=pl.ANY)


def params(mib):
    return pltpu.CompilerParams(vmem_limit_bytes=mib * MIB)


def cost(bytes_accessed):
    return pl.CostEstimate(flops=0, bytes_accessed=bytes_accessed, transcendentals=0)


def shape(dims, dtype):
    return jax.ShapeDtypeStruct(dims, dtype)


def swap(x, axis, bit):
    return lax.ppermute(x, axis, [(i, i ^ bit) for i in range(lax.axis_size(axis))])


def sum_over(x, axis):
    bit = 1
    while bit < lax.axis_size(axis):
        x = x + swap(x, axis, bit)
        bit *= 2
    return x


def here(blocks):
    ctx = lax.axis_index("ctx")
    return ctx, ctx // blocks, ctx % blocks, ctx % 2


def three_parts(x):
    high = x.astype(BF16).astype(F32)
    middle = (x - high).astype(BF16).astype(F32)
    low = x - high - middle
    lane = lax.broadcasted_iota(jnp.int32, (x.shape[0], LANES), 1)
    tail = jnp.where(lane == 0, high, jnp.where(lane == 1, middle, jnp.where(lane == 2, low, 0.0)))
    return tail.astype(BF16)


def whole(tail):
    return jnp.sum(tail.astype(F32), axis=1, keepdims=True)


def pick_kernel(rows_ref, own_ref, keep_ref, send_ref, squares_ref):
    half = rows_ref.shape[1] // 2
    core = lax.axis_index("ctx") % 2
    rows = rows_ref[...]
    squares = jnp.sum(rows * rows, axis=1, keepdims=True)
    squares_ref[...] = jnp.broadcast_to(squares, squares_ref.shape)
    tail = three_parts(squares)
    own = rows.astype(BF16)
    own_ref[...] = own
    keep_ref[:, half:] = tail
    send_ref[:, half:] = tail

    @pl.when(core == 0)
    def _():
        keep_ref[:, :half] = own[:, :half]
        send_ref[:, :half] = own[:, half:]

    @pl.when(core == 1)
    def _():
        keep_ref[:, :half] = own[:, half:]
        send_ref[:, :half] = own[:, :half]


def add_kernel(first_ref, second_ref, out_ref, squares_ref):
    half = out_ref.shape[1] - LANES
    out_ref[:, :half] = first_ref[:, :half] + second_ref[:, :half]
    squares = whole(first_ref[:, half:]) + whole(second_ref[:, half:])
    out_ref[:, half:] = three_parts(squares)
    squares_ref[...] = jnp.broadcast_to(squares, squares_ref.shape)


def settle_kernel(first_ref, second_ref, squares_ref, up_ref, across_ref, out_ref):
    half = out_ref.shape[1] - LANES
    out_ref[:, :half] = first_ref[:, :half] + second_ref[:, :half]
    here_squares = squares_ref[:, 0:1] + whole(second_ref[:, half:])
    out_ref[:, half:] = three_parts(here_squares + (up_ref[:, 0:1] + across_ref[:, 0:1]))


def join_kernel(*refs):
    a, b, c, d = (ref[...].astype(F32) for ref in refs[:4])
    refs[4][...] = ((a + b) + (c + d)).astype(refs[4].dtype)


def retail_kernel(first_ref, squares_ref, out_ref):
    half = out_ref.shape[1] - LANES
    out_ref[:, :half] = first_ref[:, :half]
    out_ref[:, half:] = three_parts(squares_ref[:, 0:1])


def load_kernel(side, head_ref, dep_ref, out_ref, sem):
    del dep_ref
    half = out_ref.shape[1]
    start = pl.multiple_of((lax.axis_index("ctx") + side) % 2 * half, LANES)
    copy = pltpu.make_async_copy(head_ref.at[:, pl.ds(start, half)], out_ref, sem)
    copy.start()
    copy.wait()


def normalize_kernel(
    blocks, model_width, side, mine_ref, there_ref, gain_ref, *rest
):
    slots = mine_ref.shape[0]
    half = mine_ref.shape[1] - LANES
    _, seq, _, core = here(blocks)
    normed_ref, scaled_ref = rest[:2]
    gain = gain_ref[:, pl.ds(pl.multiple_of((core + side) % 2 * half, LANES), half)]
    for ref, s in ((mine_ref, seq), (there_ref, 1 - seq)):
        rows = pl.ds(pl.multiple_of(s * slots, slots), slots)
        inverse = lax.rsqrt(whole(ref[:, half:]) / model_width + EPSILON)
        scaled = ref[:, :half].astype(F32) * inverse
        scaled_ref[rows, :] = scaled
        normed_ref[rows, :] = (scaled * gain).astype(BF16)
        if len(rest) == 3:
            rest[2][rows, :] = jnp.broadcast_to(inverse, (slots, LANES))


def targets_kernel(voc, ref, dep_ref, out_ref):
    del dep_ref
    total = out_ref.shape[0]
    slots = total // 2
    place = lax.broadcasted_iota(jnp.int32, out_ref.shape, 0)
    out = jnp.zeros(out_ref.shape, jnp.int32)
    for r in range(total):
        out = jnp.where(place == r, ref[r // slots, r % slots], out)
    out_ref[...] = out - lax.axis_index("ctx") * voc


def stats_kernel(targets_ref, first_ref, second_ref, logits_ref, exps_ref, table_ref):
    total, voc = first_ref.shape
    logits = first_ref[...] + second_ref[...]
    logits_ref[...] = logits
    is_target = lax.broadcasted_iota(jnp.int32, (total, voc), 1) == targets_ref[:, 0:1]
    top = jnp.max(logits, axis=1, keepdims=True)
    away = logits - top
    exps = jnp.exp(away)
    exps_ref[:total, :] = jnp.where(is_target, 0.0, exps).astype(BF16)
    exps_ref[total:, :] = jnp.where(is_target, 1.0, 0.0).astype(BF16)
    entries = (
        top,
        jnp.sum(exps, axis=1, keepdims=True),
        jnp.sum(exps * away, axis=1, keepdims=True),
        jnp.sum(jnp.where(is_target, logits, 0.0), axis=1, keepdims=True),
    )
    lane = lax.broadcasted_iota(jnp.int32, (LANES, LANES), 1)
    table = jnp.zeros((LANES, LANES), F32)
    for k, entry in enumerate(entries):
        entry = jnp.concatenate([entry, jnp.zeros((LANES - total, 1), F32)]) if total < LANES else entry
        table = jnp.where(lane == k, entry, table)
    table_ref[...] = table.T[:SUBLANES, :]


def merged(first, second):
    top = jnp.maximum(first[0:1], second[0:1])
    gap_first = first[0:1] - top
    gap_second = second[0:1] - top
    exp_first = jnp.exp(gap_first)
    exp_second = jnp.exp(gap_second)
    return (
        top,
        first[1:2] * exp_first + second[1:2] * exp_second,
        (first[2:3] + gap_first * first[1:2]) * exp_first
        + (second[2:3] + gap_second * second[1:2]) * exp_second,
        first[3:4] + second[3:4],
    )


def merge_kernel(first_ref, second_ref, out_ref):
    out_ref[...] = jnp.zeros_like(out_ref)
    for k, row in enumerate(merged(first_ref, second_ref)):
        out_ref[k : k + 1, :] = row


def merge_four_kernel(a_ref, b_ref, c_ref, d_ref, out_ref, near_ref, far_ref):
    merge_kernel(a_ref, b_ref, near_ref)
    merge_kernel(c_ref, d_ref, far_ref)
    merge_kernel(near_ref, far_ref, out_ref)


def scaled_part(spread, at_target, part_ref, scaled_ref, out_ref, tail_ref):
    total, half = scaled_ref.shape
    part = spread * part_ref[:total, :] + at_target * part_ref[total:, :]
    gain = jnp.sum(part * scaled_ref[...], axis=0, keepdims=True)
    tail_ref[...] = jnp.zeros_like(tail_ref)
    for j in range(half // LANES):
        tail_ref[j : j + 1, :] = gain[:, j * LANES : (j + 1) * LANES]
    out_ref[:, :half] = part.astype(out_ref.dtype)
    out_ref[:, half:] = tail_ref[...].astype(out_ref.dtype)


def send_kernel(
    length, model_width, num_ref, den_ref, own_ref, a_ref, b_ref, part_ref, scaled_ref,
    inverse_ref, send_ref, meta_ref, loss_ref, tail_ref, rows_ref,
):
    total = inverse_ref.shape[0]
    slots = total // 2
    row_top, exp_total, moment, picked = merged(a_ref, b_ref)
    log_total = row_top + jnp.log(exp_total)
    place = lax.broadcasted_iota(jnp.int32, (1, LANES), 1)
    den = jnp.where(place < slots, den_ref[0], den_ref[1]).astype(F32)
    num = jnp.where(place < slots, num_ref[0], num_ref[1]).astype(F32)
    factor = den / (num * (2.0 * length))
    scale = LOSS_SCALE * factor
    inner = scale * (moment / exp_total - (picked - row_top)) / model_width
    spread = scale * jnp.exp(own_ref[0:1, :] - log_total)
    at_target = scale * (jnp.exp(picked - log_total) - 1.0)
    rows_ref[...] = jnp.zeros_like(rows_ref)
    for k, row in enumerate((log_total, scale, inner, spread, at_target)):
        rows_ref[k : k + 1, :] = row
    across = jnp.concatenate([rows_ref[...], jnp.zeros((LANES - SUBLANES, LANES), F32)]).T[:total]
    scaled_part(across[:, 3:4], across[:, 4:5], part_ref, scaled_ref, send_ref, tail_ref)
    lane = lax.broadcasted_iota(jnp.int32, (total, LANES), 1)
    meta_ref[...] = jnp.where(lane == 2, across / inverse_ref[...], across)
    loss_ref[...] = jnp.sum(
        jnp.where(place < total, factor * (log_total - picked), 0.0), axis=1, keepdims=True
    )


def keep_kernel(meta_ref, part_ref, scaled_ref, keep_ref, tail_ref):
    scaled_part(meta_ref[:, 3:4], meta_ref[:, 4:5], part_ref, scaled_ref, keep_ref, tail_ref)


def divide_kernel(blocks, keep_ref, arrived_ref, own_ref, give_ref):
    slots = own_ref.shape[0]
    half = own_ref.shape[1] - LANES
    _, seq, _, _ = here(blocks)
    tail = (keep_ref[:slots, half:] + arrived_ref[:slots, half:].astype(F32)).astype(BF16)
    for ref, s in ((own_ref, seq), (give_ref, 1 - seq)):
        rows = pl.ds(pl.multiple_of(s * slots, slots), slots)
        part = keep_ref[rows, :half] + arrived_ref[rows, :half].astype(F32)
        ref[:, :half] = part.astype(ref.dtype)
        ref[:, half:] = tail.astype(ref.dtype)


def dlogits_kernel(
    targets_ref, logits_ref, meta_ref, own_ref, other_ref, dep_ref, out_ref, normed_ref
):
    del dep_ref
    total, voc = logits_ref.shape
    is_target = lax.broadcasted_iota(jnp.int32, (total, voc), 1) == targets_ref[:, 0:1]
    softmax = jnp.exp(logits_ref[...] - meta_ref[:, 0:1])
    out_ref[...] = (
        (meta_ref[:, 1:2] * (softmax - jnp.where(is_target, 1.0, 0.0))).T.astype(BF16)
    )
    half = own_ref.shape[1]
    core = lax.axis_index("ctx") % 2
    for side, ref in enumerate((own_ref, other_ref)):
        normed_ref[:, pl.ds(pl.multiple_of((core + side) % 2 * half, LANES), half)] = ref[...]


def head_kernel(dlogits_ref, normed_ref, *rest):
    rest[-1][...] = jnp.dot(
        dlogits_ref[...], normed_ref[...], preferred_element_type=F32
    ).astype(BF16)


def final_kernel(
    blocks, side, select_ref, part_ref, own_ref, inverse_ref, meta_ref, gain_ref, *rest
):
    mine_ref, out_ref, grad_gain_ref, tails_ref = (None, rest[0], None, None)
    if side == 1:
        mine_ref, _, out_ref, grad_gain_ref, tails_ref = rest[:5]
    block_ref, sems = rest[-2:]
    chunks, _, step = block_ref.shape
    slots = part_ref.shape[0]
    half = chunks * step
    _, seq, _, core = here(blocks)
    rows = pl.ds(pl.multiple_of(seq * slots, slots), slots)
    inverse = inverse_ref[rows, :][:, :1]
    pull = inverse * inverse * inverse * meta_ref[rows, :][:, 2:3]
    copies = []
    for chunk in range(chunks):
        start = (core + side) % 2 * half + chunk * step
        columns = pl.ds(pl.multiple_of(start, LANES), step)
        grads = inverse * gain_ref[:, columns] * part_ref[
            :, chunk * step : (chunk + 1) * step
        ].astype(F32) - own_ref[:, columns].astype(F32) * pull
        block_ref[chunk] = lax.dot_general(
            select_ref[...],
            grads.astype(BF16),
            (((0,), (0,)), ((), ())),
            preferred_element_type=F32,
        ).astype(BF16)
        copies.append(
            pltpu.make_async_copy(block_ref.at[chunk], out_ref.at[:, columns], sems.at[chunk])
        )
        copies[-1].start()
    if side == 1:
        a = mine_ref[:, half:].astype(F32)
        b = part_ref[:, half:].astype(F32)
        for start, tail in ((0, jnp.where(core == 0, a, b)), (half, jnp.where(core == 0, b, a))):
            for j in range(half // LANES):
                at = start + j * LANES
                tails_ref[:, at : at + LANES] = tail[j : j + 1, :]
        copies.append(pltpu.make_async_copy(tails_ref, grad_gain_ref, sems.at[chunks]))
        copies[-1].start()
    for copy in copies:
        copy.wait()


def device_step(hidden, norm_gain, head, masked_pos, masked_targets, t_num, t_den):
    tok, width = hidden.shape
    voc = head.shape[0]
    count = lax.axis_size("ctx")
    model_width = width * lax.axis_size("vocab")
    blocks = count // 2
    slots = masked_pos.shape[1]
    total = 2 * slots
    half = width // 2
    packed_width = half + LANES
    inner_bits = [1 << b for b in range(1, count.bit_length() - 2)]
    gain_row = norm_gain.reshape(1, width)

    ctx = lax.axis_index("ctx")
    local = masked_pos[ctx // blocks] - ctx % blocks * tok
    select = (jnp.arange(tok, dtype=jnp.int32)[None, :] == local[:, None]).astype(BF16)

    own, keep, send, squares = pl.pallas_call(
        pick_kernel,
        in_specs=[vmem()],
        out_specs=[vmem()] * 4,
        out_shape=[shape((slots, width), BF16)]
        + [shape((slots, packed_width), BF16)] * 2
        + [shape((slots, LANES), F32)],
        compiler_params=params(6),
        name="pick",
    )(jnp.dot(select, hidden, preferred_element_type=F32))

    ways = lax.axis_size("vocab")

    def load(side, dep):
        return pl.pallas_call(
            lambda *refs: load_kernel(side, *refs),
            in_specs=[anywhere(), anywhere()],
            out_specs=vmem(),
            out_shape=shape((voc, half), BF16),
            scratch_shapes=[pltpu.SemaphoreType.DMA(())],
            compiler_params=params(46),
            cost_estimate=cost(voc * half * 4),
            name="load",
        )(head, dep)

    arrived = swap(send, "ctx", 1)
    loads = [load(0, keep)]
    if ways == 2:
        across = lax.ppermute(
            squares,
            ("ctx", "vocab"),
            [(i, i ^ (ways + 1)) for i in range(count * ways)],
        )
        mine = pl.pallas_call(
            settle_kernel,
            in_specs=[vmem()] * 5,
            out_specs=vmem(),
            out_shape=shape((slots, packed_width), BF16),
            compiler_params=params(4),
            name="settle",
        )(keep, arrived, squares, swap(squares, "vocab", 1), across)
    else:
        mine, squares = pl.pallas_call(
            add_kernel,
            in_specs=[vmem()] * 2,
            out_specs=[vmem()] * 2,
            out_shape=[shape((slots, packed_width), BF16), shape((slots, LANES), F32)],
            compiler_params=params(4),
            name="add",
        )(keep, arrived)
        mine = pl.pallas_call(
            retail_kernel,
            in_specs=[vmem()] * 2,
            out_specs=vmem(),
            out_shape=shape((slots, packed_width), BF16),
            compiler_params=params(4),
            name="retail",
        )(mine, sum_over(squares, "vocab"))

    def around(x):
        first, second = inner_bits[-2:]
        bits = (first, second, first + second)
        return [swap(x, "ctx", bit) for bit in bits]

    def join(x, others):
        return pl.pallas_call(
            join_kernel,
            in_specs=[vmem()] * 4,
            out_specs=vmem(),
            out_shape=shape(x.shape, x.dtype),
            compiler_params=params(4),
            name="join",
        )(x, *others)

    for bit in inner_bits[:-2]:
        mine = mine + swap(mine, "ctx", bit)
    before = mine
    mine = join(before, around(before))
    loads.append(load(1, before))
    there = swap(mine, "ctx", blocks)
    mine_other = swap(mine, "ctx", 1)
    there_other = swap(there, "ctx", 1)

    def normalize(side, a, b):
        extra = [shape((total, LANES), F32)] if side == 0 else []
        return pl.pallas_call(
            lambda *refs: normalize_kernel(blocks, model_width, side, *refs),
            in_specs=[vmem()] * 3,
            out_specs=[vmem()] * (2 + len(extra)),
            out_shape=[shape((total, half), BF16), shape((total, half), F32)] + extra,
            compiler_params=params(6),
            name="normalize",
        )(a, b, gain_row)

    def contract(a, b):
        return lax.dot_general(a, b, (((1,), (1,)), ((), ())), preferred_element_type=F32)

    normed, scaled, inverse = normalize(0, mine, there)
    partial = contract(normed, loads[0])
    normed_other, scaled_other = normalize(1, mine_other, there_other)
    partial = partial + contract(normed_other, loads[1])
    bit = 1
    while 2 * bit < lax.axis_size("vocab"):
        partial = partial + swap(partial, "vocab", bit)
        bit *= 2
    targets = pl.pallas_call(
        lambda *refs: targets_kernel(voc, *refs),
        in_specs=[smem(), anywhere()],
        out_specs=vmem(),
        out_shape=shape((total, LANES), jnp.int32),
        compiler_params=params(4),
        name="targets",
    )(masked_targets, partial)
    logits, exps, table = pl.pallas_call(
        stats_kernel,
        in_specs=[vmem()] * 3,
        out_specs=[vmem()] * 3,
        out_shape=[
            shape((total, voc), F32),
            shape((2 * total, voc), BF16),
            shape((SUBLANES, LANES), F32),
        ],
        compiler_params=params(8),
        name="stats",
    )(targets, partial, swap(partial, "vocab", bit))

    own_table = table

    def merge(a, b):
        return pl.pallas_call(
            merge_kernel,
            in_specs=[vmem()] * 2,
            out_specs=vmem(),
            out_shape=shape((SUBLANES, LANES), F32),
            compiler_params=params(4),
            name="merge",
        )(a, b)

    for bit in [1] + inner_bits[:-2]:
        table = merge(table, swap(table, "ctx", bit))
    near = [table] + around(table)
    table = pl.pallas_call(
        merge_four_kernel,
        in_specs=[vmem()] * 4,
        out_specs=vmem(),
        out_shape=shape((SUBLANES, LANES), F32),
        scratch_shapes=[pltpu.VMEM((SUBLANES, LANES), F32)] * 2,
        compiler_params=params(4),
        name="merge_four",
    )(*near)
    there_table = swap(table, "ctx", blocks)
    part = jnp.dot(exps, loads[0], preferred_element_type=F32)
    part_other = jnp.dot(exps, loads[1], preferred_element_type=F32)
    send, meta, loss_value = pl.pallas_call(
        lambda *refs: send_kernel(tok * blocks, model_width, *refs),
        in_specs=[smem(), smem()] + [vmem()] * 6,
        out_specs=[vmem()] * 3,
        out_shape=[
            shape((total, packed_width), BF16),
            shape((total, LANES), F32),
            shape((1, 1), F32),
        ],
        scratch_shapes=[pltpu.VMEM((total, LANES), F32), pltpu.VMEM((SUBLANES, LANES), F32)],
        compiler_params=params(8),
        name="send_part",
    )(t_num, t_den, own_table, table, there_table, part_other, scaled_other, inverse)
    keep = pl.pallas_call(
        keep_kernel,
        in_specs=[vmem()] * 3,
        out_specs=vmem(),
        out_shape=shape((total, packed_width), F32),
        scratch_shapes=[pltpu.VMEM((total, LANES), F32)],
        compiler_params=params(8),
        name="keep_part",
    )(meta, part, scaled)

    steps = 8
    step = width // steps
    grad_head = None

    def head_part(first, last, dep, so_far):
        extra = [dep] + ([] if so_far is None else [so_far])
        return pl.pallas_call(
            head_kernel,
            grid=(last - first,),
            in_specs=[
                pl.BlockSpec((voc, total), lambda i: (0, 0)),
                pl.BlockSpec((total, step), lambda i: (0, first + i)),
            ]
            + [anywhere()] * len(extra),
            out_specs=pl.BlockSpec((voc, step), lambda i: (0, first + i)),
            out_shape=shape((voc, width), BF16),
            input_output_aliases={} if so_far is None else {3: 0},
            compiler_params=params(12),
            cost_estimate=cost(2 * voc * step * (last - first)),
            name="head_grad",
        )(dlogits, normed, *extra)

    arrived = swap(send, "ctx", 1)
    own_part, give = pl.pallas_call(
        lambda *refs: divide_kernel(blocks, *refs),
        in_specs=[vmem()] * 2,
        out_specs=[vmem()] * 2,
        out_shape=[shape((slots, packed_width), F32), shape((slots, packed_width), BF16)],
        compiler_params=params(6),
        name="divide",
    )(keep, arrived)
    dlogits, normed = pl.pallas_call(
        dlogits_kernel,
        in_specs=[vmem()] * 5 + [anywhere()],
        out_specs=[vmem()] * 2,
        out_shape=[shape((voc, total), BF16), shape((total, width), BF16)],
        compiler_params=params(6),
        name="dlogits",
    )(targets, logits, meta, normed, normed_other, send)
    middle = steps // 2
    grad_head = head_part(0, middle, give, None)
    sent = (own_part + swap(give, "ctx", blocks).astype(F32)).astype(BF16)
    for bit in inner_bits[:-2]:
        sent = sent + swap(sent, "ctx", bit)
    grad_head = head_part(middle, steps, sent, grad_head)
    sent = join(sent, around(sent))
    other = swap(sent, "ctx", 1)

    def finish(side, part, *extra):
        chunks = 4
        return pl.pallas_call(
            lambda *refs: final_kernel(blocks, side, *refs),
            in_specs=[vmem()] * 6 + ([vmem(), anywhere()] if side else []),
            out_specs=[anywhere()] * (1 + side),
            out_shape=[shape((tok, width), BF16)] + ([shape((1, width), F32)] if side else []),
            input_output_aliases={7: 0} if side else {},
            scratch_shapes=[pltpu.VMEM((1, width), F32)] * side
            + [
                pltpu.VMEM((chunks, tok, half // chunks), BF16),
                pltpu.SemaphoreType.DMA((chunks + side,)),
            ],
            compiler_params=params(8),
            name="final",
        )(select, part, own, inverse, meta, gain_row, *extra)

    (grad_hidden,) = finish(0, sent)
    grad_hidden, grad_gain = finish(1, other, sent, grad_hidden)
    return (loss_value.reshape(()), grad_hidden, grad_head, grad_gain.reshape(width))


def solution(mesh):
    placed = (P("ctx", "vocab"), P("vocab"), P("ctx", "vocab"), P(), P(), P(), P())
    return jax.shard_map(
        device_step,
        mesh=mesh,
        in_specs=placed,
        out_specs=(P(), P("ctx", "vocab"), P("ctx", "vocab"), P("vocab")),
        check_vma=False,
    )
```

time: 78.5 us -> 71.5 us (0.911)
  waiting for transfers between devices: 34.1 us -> 26.9 us
  starting transfers between devices: 19.6 us -> 20.7 us
  local copies, waits for them, and re-layouts: 1.68 us -> 0.77 us
    ppermute x17 -> x20, waiting for transfers between devices: 31.5 us -> 25.4 us  [swap(): lax.ppermute(x, axis, [(i, i ^ bit) for i in range(lax.axis_size(axis))])]
    ppermute x1, waiting for transfers between devices: 2.64 us -> 1.45 us  [device_step(): lax.ppermute(squares, ('ctx', 'vocab'), [(i, i ^ ways + 1) for i in range...]
    ppermute x17 -> x20, starting transfers between devices: 19.6 us -> 20.7 us  [swap(): lax.ppermute(x, axis, [(i, i ^ bit) for i in range(lax.axis_size(axis))])]
    unnamed x10, local copies, waits for them, and re-layouts: 1.61 us -> 0.77 us
    pallas_call x8 -> x14, Pallas kernels: 8.95 us -> 9.37 us  [the longest x2 4.33 us: load(): pl.pallas_call(lambda *refs: load_kernel(side, *refs), in_specs=[anywhere...]
    pallas_call x3 -> x2, Pallas kernels: 6.68 us -> 6.28 us  [head_part(): pl.pallas_call(head_kernel, grid=(last - first,), in_specs=[pl.BlockSpec(...]
    dot_general x4 -> x5, matrix products: 4.21 us -> 4.57 us  [the longest x2 2.52 us: contract(): lax.dot_general(a, b, (((1,), (1,)), ((), ())), preferred_element_type=F32)]
  transfers between devices with their start and end apart: 18 -> 21, of which waited for: 14 -> 16; matrix products, arithmetic and copies ran while one was open for 2% -> 4% of each run, Pallas kernels for 15% -> 18%
where the time goes in v2:
time: 71.5 us; the launch traced here: 71.3 us
  waiting for transfers between devices  26.9 us (38%)
  starting transfers between devices  20.7 us (29%)
  Pallas kernels  16.6 us (23%)
  matrix products  4.57 us (6%)
  other arithmetic  0.92 us (1%)
  between operations  0.85 us (1%)
  local copies, waits for them, and re-layouts  0.77 us (1%)
    ppermute x20, waiting for transfers between devices, swap(): lax.ppermute(x, axis, [(i, i ^ bit) for i in range(lax.axis_size(axis))])  25.4 us
    ppermute x20, starting transfers between devices, swap(): lax.ppermute(x, axis, [(i, i ^ bit) for i in range(lax.axis_size(axis))])  20.7 us
    pallas_call x2, Pallas kernels, head_part(): pl.pallas_call(head_kernel, grid=(last - first,), in_specs=[pl.BlockSpec(...  6.28 us
    pallas_call x2, Pallas kernels, load(): pl.pallas_call(lambda *refs: load_kernel(side, *refs), in_specs=[anywhere...  4.33 us
    pallas_call x2, Pallas kernels, finish(): pl.pallas_call(lambda *refs: final_kernel(blocks, side, *refs), in_specs=...  2.71 us
    dot_general x2, matrix products, contract(): lax.dot_general(a, b, (((1,), (1,)), ((), ())), preferred_element_type=F32)  2.52 us
    ppermute x1, waiting for transfers between devices, device_step(): lax.ppermute(squares, ('ctx', 'vocab'), [(i, i ^ ways + 1) for i in range...  1.45 us
  transfers between devices with their start and end apart: 21, of which 16 were waited for; matrix products, arithmetic and copies ran while one was open for 4% of the time, Pallas kernels for 18%

profile of v2, /device:TPU:0, one launch (start us, length us, event | category | flops | bytes accessed | tf_op | source)
XLA Modules:
  0.0 71.3 jit_solution(13641545598460374963)
XLA Ops:
  0.6 0.0 copy-start
  0.7 0.8 %subtract_bitcast_fusion = s32[16]{0:T(128)S(1)} fusion(s32[2,16]{1,0:T(2,128)} %param.10, s32[]{:T(128)S(6)} %select_n.15, s32[]{:T(128)S(6)} %mul.3), kind=kLoop, calls=%fused_computation.6 | loop fusion | flops 16 | bytes 136 | tf_op jit(solution)/shard_map/sub | solution.py:345
  1.5 0.7 %copy-done = bf16[256,4096]{1,0:T(8,128)(2,1)S(1)} copy-done((bf16[256,4096]{1,0:T(8,128)(2,1)S(1)}, bf16[256,4096]{1,0:T(8,128)(2,1)}, u32[]{:S(2)}) %copy-start) | copy-done | bytes 2097176
  2.2 0.4 fusion.1.rows_ref
  2.7 0.1 pick.1
  2.8 0.6 collective-permute-start
  3.4 2.5 %collective-permute-start.1 = (f32[16,128]{1,0:T(8,128)S(1)}, f32[16,128]{1,0:T(8,128)S(1)}, u32[]{:S(2)}, u32[]{:S(2)}) collective-permute-start(f32[16,128]{1,0:T(8,128)S(1)} %get-tuple-element.27.squares_ref), channel_id=1, source_target_pairs={{0,1},{1,0},{2,3},{3,2},{4,5},{5,4},{6,7},{7,6},{8,9},{9,8},{10,11... | collective-permute-start | bytes 24584 | tf_op jit(solution)/shard_map/ppermute | solution.py:43
  5.9 0.0 collective-permute-start.2
  5.9 1.6 %collective-permute-done.1.up_ref = f32[16,128]{1,0:T(8,128)S(1)} collective-permute-done((f32[16,128]{1,0:T(8,128)S(1)}, f32[16,128]{1,0:T(8,128)S(1)}, u32[]{:S(2)}, u32[]{:S(2)}) %collective-permute-start.1) | collective-permute-done | bytes 8224 | tf_op jit(solution)/shard_map/ppermute | solution.py:43
  7.5 1.4 %collective-permute-done.2.across_ref = f32[16,128]{1,0:T(8,128)S(1)} collective-permute-done((f32[16,128]{1,0:T(8,128)S(1)}, f32[16,128]{1,0:T(8,128)S(1)}, u32[]{:S(2)}, u32[]{:S(2)}) %collective-permute-start.2) | collective-permute-done | bytes 8224 | tf_op jit(solution)/shard_map/ppermute | solution.py:376
  9.0 0.2 settle.1.refs_0_.refs_1_
  9.1 1.5 %collective-permute-start.3 = (bf16[16,2176]{1,0:T(8,128)(2,1)S(1)}, bf16[16,2176]{1,0:T(8,128)(2,1)S(1)}, u32[]{:S(2)}, u32[]{:S(2)}) collective-permute-start(bf16[16,2176]{1,0:T(8,128)(2,1)S(1)} %settle.1.refs_0_.refs_1_), channel_id=1, source_target_pairs={{0,4},{2,6},{4,0},{6,2},{8,12},{10,14},{12,8},{14,10},{16,20},{18,... | collective-permute-start | bytes 208904 | tf_op jit(solution)/shard_map/ppermute | solution.py:43
  10.6 1.6 %collective-permute-start.4 = (bf16[16,2176]{1,0:T(8,128)(2,1)S(1)}, bf16[16,2176]{1,0:T(8,128)(2,1)S(1)}, u32[]{:S(2)}, u32[]{:S(2)}) collective-permute-start(bf16[16,2176]{1,0:T(8,128)(2,1)S(1)} %settle.1.refs_0_.refs_1_), channel_id=1, source_target_pairs={{0,8},{2,10},{4,12},{6,14},{8,0},{10,2},{12,4},{14,6},{16,24},{18,... | collective-permute-start | bytes 208904 | tf_op jit(solution)/shard_map/ppermute | solution.py:43
  12.2 0.4 collective-permute-start.5
  12.6 0.8 %collective-permute-done.3.refs_1_ = bf16[16,2176]{1,0:T(8,128)(2,1)S(1)} collective-permute-done((bf16[16,2176]{1,0:T(8,128)(2,1)S(1)}, bf16[16,2176]{1,0:T(8,128)(2,1)S(1)}, u32[]{:S(2)}, u32[]{:S(2)}) %collective-permute-start.3) | collective-permute-done | bytes 69664 | tf_op jit(solution)/shard_map/ppermute | solution.py:43
  13.5 2.1 %collective-permute-done.4.refs_2_ = bf16[16,2176]{1,0:T(8,128)(2,1)S(1)} collective-permute-done((bf16[16,2176]{1,0:T(8,128)(2,1)S(1)}, bf16[16,2176]{1,0:T(8,128)(2,1)S(1)}, u32[]{:S(2)}, u32[]{:S(2)}) %collective-permute-start.4) | collective-permute-done | bytes 69664 | tf_op jit(solution)/shard_map/ppermute | solution.py:43
  15.5 1.9 %collective-permute-done.5.refs_3_ = bf16[16,2176]{1,0:T(8,128)(2,1)S(1)} collective-permute-done((bf16[16,2176]{1,0:T(8,128)(2,1)S(1)}, bf16[16,2176]{1,0:T(8,128)(2,1)S(1)}, u32[]{:S(2)}, u32[]{:S(2)}) %collective-permute-start.5) | collective-permute-done | bytes 69664 | tf_op jit(solution)/shard_map/ppermute | solution.py:43
  17.5 2.7 %collective-permute-start.6 = (bf16[16,2176]{1,0:T(8,128)(2,1)S(1)}, bf16[16,2176]{1,0:T(8,128)(2,1)S(1)}, u32[]{:S(2)}, u32[]{:S(2)}) collective-permute-start(bf16[16,2176]{1,0:T(8,128)(2,1)S(1)} %join.2.refs_0_), channel_id=1, source_target_pairs={{0,16},{2,18},{4,20},{6,22},{8,24},{10,26},{12,28},{14,30},{16,0},... | collective-permute-start | bytes 208904 | tf_op jit(solution)/shard_map/ppermute | solution.py:43
  20.1 2.2 %load.2 = bf16[988,2048]{1,0:T(8,128)(2,1)S(1)} custom-call(bf16[988,4096]{1,0:T(8,128)(2,1)} %refs_0_.5, bf16[16,2176]{1,0:T(8,128)(2,1)S(1)} %get-tuple-element.25.first_ref.refs_1_), custom_call_target="tpu_custom_call" | custom-call | bytes 8093696 | tf_op jit(solution)/shard_map/load/pallas_call | solution.py:362
  22.3 0.0 copy-start.1
  22.3 2.2 %load.3 = bf16[988,2048]{1,0:T(8,128)(2,1)S(1)} custom-call(bf16[988,4096]{1,0:T(8,128)(2,1)} %refs_0_.5, bf16[16,2176]{1,0:T(8,128)(2,1)S(1)} %settle.1.refs_0_.refs_1_), custom_call_target="tpu_custom_call" | custom-call | bytes 8093696 | tf_op jit(solution)/shard_map/load/pallas_call | solution.py:362
  24.5 0.1 collective-permute-start.7
  24.6 0.5 collective-permute-start.8
  25.1 0.1 normalize.2
  25.2 0.0 copy-start.2
  25.2 1.3 %fusion.3 = f32[32,988]{1,0:T(8,128)S(1)} fusion(bf16[32,2048]{1,0:T(8,128)(2,1)S(1)} %get-tuple-element.28.own_ref, bf16[988,2048]{1,0:T(8,128)(2,1)S(1)} %load.2), kind=kOutput, calls=%fused_computation.7 | convolution fusion | flops 129499136 | bytes 4304384 | tf_op jit(solution)/shard_map/dot_general | solution.py:443
  26.5 0.0 collective-permute-done.8.refs_1_
  26.5 0.1 normalize.3
  26.6 0.0 copy-start.3
  26.7 0.0 copy-start.4
  26.7 1.3 %convolution_add_fusion.refs_1_.first_ref = f32[32,988]{1,0:T(8,128)S(1)} fusion(f32[32,988]{1,0:T(8,128)S(1)} %fusion.3, bf16[32,2048]{1,0:T(8,128)(2,1)S(1)} %get-tuple-element.29.other_ref, bf16[988,2048]{1,0:T(8,128)(2,1)S(1)} %load.3), kind=kOutput, calls=%fused_computation | convolution fusion | flops 129530752 | bytes 4430848 | tf_op jit(solution)/shard_map/dot_general | solution.py:443
  27.9 0.6 collective-permute-start.9
  28.6 0.6 targets.1.targets_ref
  29.1 4.3 %collective-permute-done.9.second_ref = f32[32,988]{1,0:T(8,128)S(1)} collective-permute-done((f32[32,988]{1,0:T(8,128)S(1)}, f32[32,988]{1,0:T(8,128)S(1)}, u32[]{:S(2)}, u32[]{:S(2)}) %collective-permute-start.9) | collective-permute-done | bytes 126496 | tf_op jit(solution)/shard_map/ppermute | solution.py:43
  33.5 0.4 stats.1
  33.8 0.0 collective-permute-start.10
  33.8 1.2 %collective-permute-done.10.second_ref = f32[8,128]{1,0:T(8,128)S(1)} collective-permute-done((f32[8,128]{1,0:T(8,128)S(1)}, f32[8,128]{1,0:T(8,128)S(1)}, u32[]{:S(2)}, u32[]{:S(2)}) %collective-permute-start.10) | collective-permute-done | bytes 4128 | tf_op jit(solution)/shard_map/ppermute | solution.py:43
  35.0 0.6 collective-permute-start.11
  35.6 1.2 %collective-permute-start.12 = (f32[8,128]{1,0:T(8,128)S(1)}, f32[8,128]{1,0:T(8,128)S(1)}, u32[]{:S(2)}, u32[]{:S(2)}) collective-permute-start(f32[8,128]{1,0:T(8,128)S(1)} %merge.1.a_ref), channel_id=1, source_target_pairs={{0,8},{2,10},{4,12},{6,14},{8,0},{10,2},{12,4},{14,6},{16,24},{18,... | collective-permute-start | bytes 12296 | tf_op jit(solution)/shard_map/ppermute | solution.py:43
  36.8 1.8 %collective-permute-start.13 = (f32[8,128]{1,0:T(8,128)S(1)}, f32[8,128]{1,0:T(8,128)S(1)}, u32[]{:S(2)}, u32[]{:S(2)}) collective-permute-start(f32[8,128]{1,0:T(8,128)S(1)} %merge.1.a_ref), channel_id=1, source_target_pairs={{0,12},{2,14},{4,8},{6,10},{8,4},{10,6},{12,0},{14,2},{16,28},{18,... | collective-permute-start | bytes 12296 | tf_op jit(solution)/shard_map/ppermute | solution.py:43
  38.6 0.1 collective-permute-done.11.b_ref
  38.7 0.5 collective-permute-done.12.c_ref
  39.2 2.1 %collective-permute-done.13.d_ref = f32[8,128]{1,0:T(8,128)S(1)} collective-permute-done((f32[8,128]{1,0:T(8,128)S(1)}, f32[8,128]{1,0:T(8,128)S(1)}, u32[]{:S(2)}, u32[]{:S(2)}) %collective-permute-start.13) | collective-permute-done | bytes 4128 | tf_op jit(solution)/shard_map/ppermute | solution.py:43
  41.3 1.5 %collective-permute-start.14 = (f32[8,128]{1,0:T(8,128)S(1)}, f32[8,128]{1,0:T(8,128)S(1)}, u32[]{:S(2)}, u32[]{:S(2)}) collective-permute-start(f32[8,128]{1,0:T(8,128)S(1)} %merge_four.1.refs_3_), channel_id=1, source_target_pairs={{0,16},{2,18},{4,20},{6,22},{8,24},{10,26},{12,28},{14,30},{16,0},... | collective-permute-start | bytes 12296 | tf_op jit(solution)/shard_map/ppermute | solution.py:43
  42.8 0.8 %fusion.4.refs_5_ = f32[64,2048]{1,0:T(8,128)S(1)} fusion(bf16[64,988]{1,0:T(8,128)(2,1)S(1)} %get-tuple-element.31, bf16[988,2048]{1,0:T(8,128)(2,1)S(1)} %load.3), kind=kOutput, calls=%fused_computation.8 | convolution fusion | flops 258998272 | bytes 4697600 | tf_op jit(solution)/shard_map/dot_general | solution.py:500
  43.6 2.2 %collective-permute-done.14.refs_4_ = f32[8,128]{1,0:T(8,128)S(1)} collective-permute-done((f32[8,128]{1,0:T(8,128)S(1)}, f32[8,128]{1,0:T(8,128)S(1)}, u32[]{:S(2)}, u32[]{:S(2)}) %collective-permute-start.14) | collective-permute-done | bytes 4128 | tf_op jit(solution)/shard_map/ppermute | solution.py:43
  45.9 1.3 %send_part.1 = (bf16[32,2176]{1,0:T(8,128)(2,1)S(1)}, f32[32,128]{1,0:T(8,128)S(1)}, f32[1,1]{1,0:T(1,128)}) custom-call(s32[2]{0:T(128)S(1)} %copy-done.3, s32[2]{0:T(128)S(1)} %copy-done.4, f32[8,128]{1,0:T(8,128)S(1)} %get-tuple-element.30.first_ref.refs_2_, f32[8,128]{1,0:T(8,128)S(1)} %merge_four.1.refs_3_, ...), custom_call_target="tpu_custom_call" | custom-call | tf_op jit(solution)/shard_map/send_part/pallas_call | solution.py:501
  47.1 0.8 %fusion.5.part_ref = f32[64,2048]{1,0:T(8,128)S(1)} fusion(bf16[64,988]{1,0:T(8,128)(2,1)S(1)} %get-tuple-element.31, bf16[988,2048]{1,0:T(8,128)(2,1)S(1)} %load.2), kind=kOutput, calls=%fused_computation.9 | convolution fusion | flops 258998272 | bytes 4697600 | tf_op jit(solution)/shard_map/dot_general | solution.py:499
  48.0 0.1 keep_part.1.refs_0_
  48.1 0.4 collective-permute-done.15.refs_1_
  48.5 1.5 %collective-permute-start.16 = (bf16[16,2176]{1,0:T(8,128)(2,1)S(1)}, bf16[16,2176]{1,0:T(8,128)(2,1)S(1)}, u32[]{:S(2)}, u32[]{:S(2)}) collective-permute-start(bf16[16,2176]{1,0:T(8,128)(2,1)S(1)} %get-tuple-element.39.rest_0_), channel_id=1, source_target_pairs={{0,16},{2,18},{4,20},{6,22},{8,24},{10,26},{12,28},{14,30},{16,0},... | collective-permute-start | bytes 208904 | tf_op jit(solution)/shard_map/ppermute | solution.py:43
  50.0 5.2 %collective-permute-done.16 = bf16[16,2176]{1,0:T(8,128)(2,1)S(1)} collective-permute-done((bf16[16,2176]{1,0:T(8,128)(2,1)S(1)}, bf16[16,2176]{1,0:T(8,128)(2,1)S(1)}, u32[]{:S(2)}, u32[]{:S(2)}) %collective-permute-start.16) | collective-permute-done | bytes 69664 | tf_op jit(solution)/shard_map/ppermute | solution.py:43
  55.3 1.0 %collective-permute-start.17 = (bf16[16,2176]{1,0:T(8,128)(2,1)S(1)}, bf16[16,2176]{1,0:T(8,128)(2,1)S(1)}, u32[]{:S(2)}, u32[]{:S(2)}) collective-permute-start(bf16[16,2176]{1,0:T(8,128)(2,1)S(1)} %add_convert_fusion.refs_0_.rest_0_), channel_id=1, source_target_pairs={{0,4},{2,6},{4,0},{6,2},{8,12},{10,14},{12,8},{14,10},{16,20},{18,... | collective-permute-start | bytes 208904 | tf_op jit(solution)/shard_map/ppermute | solution.py:43
  56.3 2.5 %collective-permute-start.19 = (bf16[16,2176]{1,0:T(8,128)(2,1)S(1)}, bf16[16,2176]{1,0:T(8,128)(2,1)S(1)}, u32[]{:S(2)}, u32[]{:S(2)}) collective-permute-start(bf16[16,2176]{1,0:T(8,128)(2,1)S(1)} %add_convert_fusion.refs_0_.rest_0_), channel_id=1, source_target_pairs={{0,12},{2,14},{4,8},{6,10},{8,4},{10,6},{12,0},{14,2},{16,28},{18,... | collective-permute-start | bytes 208904 | tf_op jit(solution)/shard_map/ppermute | solution.py:43
  58.8 0.8 %collective-permute-done.17.refs_1_ = bf16[16,2176]{1,0:T(8,128)(2,1)S(1)} collective-permute-done((bf16[16,2176]{1,0:T(8,128)(2,1)S(1)}, bf16[16,2176]{1,0:T(8,128)(2,1)S(1)}, u32[]{:S(2)}, u32[]{:S(2)}) %collective-permute-start.17) | collective-permute-done | bytes 69664 | tf_op jit(solution)/shard_map/ppermute | solution.py:43
  59.6 0.9 %collective-permute-done.18.refs_2_ = bf16[16,2176]{1,0:T(8,128)(2,1)S(1)} collective-permute-done((bf16[16,2176]{1,0:T(8,128)(2,1)S(1)}, bf16[16,2176]{1,0:T(8,128)(2,1)S(1)}, u32[]{:S(2)}, u32[]{:S(2)}) %collective-permute-start.18) | collective-permute-done | bytes 69664 | tf_op jit(solution)/shard_map/ppermute | solution.py:43
  60.6 1.2 %collective-permute-done.19.refs_3_ = bf16[16,2176]{1,0:T(8,128)(2,1)S(1)} collective-permute-done((bf16[16,2176]{1,0:T(8,128)(2,1)S(1)}, bf16[16,2176]{1,0:T(8,128)(2,1)S(1)}, u32[]{:S(2)}, u32[]{:S(2)}) %collective-permute-start.19) | collective-permute-done | bytes 69664 | tf_op jit(solution)/shard_map/ppermute | solution.py:43
  61.9 0.1 collective-permute-start.20
  62.0 0.1 fusion.refs_0_
  62.0 0.3 dlogits.1
  62.3 3.2 %head_grad.2.rest_1_ = bf16[988,4096]{1,0:T(8,128)(2,1)} custom-call(bf16[988,32]{1,0:T(8,128)(2,1)S(1)} %get-tuple-element.43.dlogits_ref, bf16[32,4096]{1,0:T(8,128)(2,1)S(1)} %get-tuple-element.44.normed_ref, bf16[16,2176]{1,0:T(8,128)(2,1)S(1)} %get-tuple-element.39.rest_0_), custom_call_target="tpu_custom_call" | custom-call | bytes 4046848 | tf_op jit(solution)/shard_map/head_grad/pallas_call | solution.py:530
  65.5 3.1 %head_grad.3 = bf16[988,4096]{1,0:T(8,128)(2,1)} custom-call(bf16[988,32]{1,0:T(8,128)(2,1)S(1)} %get-tuple-element.43.dlogits_ref, bf16[32,4096]{1,0:T(8,128)(2,1)S(1)} %get-tuple-element.44.normed_ref, bf16[16,2176]{1,0:T(8,128)(2,1)S(1)} %add_convert_fusion.refs_0_.rest_0_, bf16[988,4096]{1,0:T(8,128)(2,1)} %head_grad.2.rest_1_), custom_call_target="tpu_custom_call", output_to_operand_aliasing={{}: (3, {})} | custom-call | bytes 4046848 | tf_op jit(solution)/shard_map/head_grad/pallas_call | solution.py:530
  68.6 1.3 %final.2.refs_7_ = bf16[256,4096]{1,0:T(8,128)(2,1)} custom-call(bf16[16,256]{1,0:T(8,128)(2,1)S(1)} %fusion.refs_0_, bf16[16,2176]{1,0:T(8,128)(2,1)S(1)} %join.3.refs_1_.refs_6_, bf16[16,4096]{1,0:T(8,128)(2,1)S(1)} %get-tuple-element.40.refs_2_, f32[32,128]{1,0:T(8,128)S(1)} %get-tuple-element.33.refs_7_.refs_3_, ...), custom_call_target="tpu_custom_call" | custom-call | tf_op jit(solution)/shard_map/final/pallas_call | solution.py:574
  69.9 1.4 %final.3 = (bf16[256,4096]{1,0:T(8,128)(2,1)}, f32[1,4096]{1,0:T(1,128)}) custom-call(bf16[16,256]{1,0:T(8,128)(2,1)S(1)} %fusion.refs_0_, bf16[16,2176]{1,0:T(8,128)(2,1)S(1)} %collective-permute-done.20.refs_1_, bf16[16,4096]{1,0:T(8,128)(2,1)S(1)} %get-tuple-element.40.refs_2_, ...), custom_call_target="tpu_custom_call", output_to_operand_aliasing={{0}: (7, {})} | custom-call | tf_op jit(solution)/shard_map/final/pallas_call | solution.py:574
  (16 shorter events, 0.2 us)
Async XLA Ops:
  0.6 1.6 %copy-start = (bf16[256,4096]{1,0:T(8,128)(2,1)S(1)}, bf16[256,4096]{1,0:T(8,128)(2,1)}, u32[]{:S(2)}) copy-start(bf16[256,4096]{1,0:T(8,128)(2,1)} %param.7) | copy-start | bytes 6291460
  2.8 6.2 %collective-permute-start = (bf16[16,2176]{1,0:T(8,128)(2,1)S(1)}, bf16[16,2176]{1,0:T(8,128)(2,1)S(1)}, u32[]{:S(2)}, u32[]{:S(2)}) collective-permute-start(bf16[16,2176]{1,0:T(8,128)(2,1)S(1)} %get-tuple-element.26), channel_id=1, source_target_pairs={{0,2},{2,0},{4,6},{6,4},{8,10},{10,8},{12,14},{14,12},{16,18},{18,... | collective-permute-start | bytes 208904 | tf_op jit(solution)/shard_map/ppermute | solution.py:43
  3.4 4.2 %collective-permute-start.1 = (f32[16,128]{1,0:T(8,128)S(1)}, f32[16,128]{1,0:T(8,128)S(1)}, u32[]{:S(2)}, u32[]{:S(2)}) collective-permute-start(f32[16,128]{1,0:T(8,128)S(1)} %get-tuple-element.27.squares_ref), channel_id=1, source_target_pairs={{0,1},{1,0},{2,3},{3,2},{4,5},{5,4},{6,7},{7,6},{8,9},{9,8},{10,11... | collective-permute-start | bytes 24584 | tf_op jit(solution)/shard_map/ppermute | solution.py:43
  5.9 3.1 %collective-permute-start.2 = (f32[16,128]{1,0:T(8,128)S(1)}, f32[16,128]{1,0:T(8,128)S(1)}, u32[]{:S(2)}, u32[]{:S(2)}) collective-permute-start(f32[16,128]{1,0:T(8,128)S(1)} %get-tuple-element.27.squares_ref), channel_id=1, source_target_pairs={{0,3},{1,2},{2,1},{3,0},{4,7},{5,6},{6,5},{7,4},{8,11},{9,10},{10,... | collective-permute-start | bytes 24584 | tf_op jit(solution)/shard_map/ppermute | solution.py:376
  9.1 4.3 %collective-permute-start.3 = (bf16[16,2176]{1,0:T(8,128)(2,1)S(1)}, bf16[16,2176]{1,0:T(8,128)(2,1)S(1)}, u32[]{:S(2)}, u32[]{:S(2)}) collective-permute-start(bf16[16,2176]{1,0:T(8,128)(2,1)S(1)} %settle.1.refs_0_.refs_1_), channel_id=1, source_target_pairs={{0,4},{2,6},{4,0},{6,2},{8,12},{10,14},{12,8},{14,10},{16,20},{18,... | collective-permute-start | bytes 208904 | tf_op jit(solution)/shard_map/ppermute | solution.py:43
  10.6 4.9 %collective-permute-start.4 = (bf16[16,2176]{1,0:T(8,128)(2,1)S(1)}, bf16[16,2176]{1,0:T(8,128)(2,1)S(1)}, u32[]{:S(2)}, u32[]{:S(2)}) collective-permute-start(bf16[16,2176]{1,0:T(8,128)(2,1)S(1)} %settle.1.refs_0_.refs_1_), channel_id=1, source_target_pairs={{0,8},{2,10},{4,12},{6,14},{8,0},{10,2},{12,4},{14,6},{16,24},{18,... | collective-permute-start | bytes 208904 | tf_op jit(solution)/shard_map/ppermute | solution.py:43
  12.2 5.2 %collective-permute-start.5 = (bf16[16,2176]{1,0:T(8,128)(2,1)S(1)}, bf16[16,2176]{1,0:T(8,128)(2,1)S(1)}, u32[]{:S(2)}, u32[]{:S(2)}) collective-permute-start(bf16[16,2176]{1,0:T(8,128)(2,1)S(1)} %settle.1.refs_0_.refs_1_), channel_id=1, source_target_pairs={{0,12},{2,14},{4,8},{6,10},{8,4},{10,6},{12,0},{14,2},{16,28},{18,... | collective-permute-start | bytes 208904 | tf_op jit(solution)/shard_map/ppermute | solution.py:43
  17.5 7.1 %collective-permute-start.6 = (bf16[16,2176]{1,0:T(8,128)(2,1)S(1)}, bf16[16,2176]{1,0:T(8,128)(2,1)S(1)}, u32[]{:S(2)}, u32[]{:S(2)}) collective-permute-start(bf16[16,2176]{1,0:T(8,128)(2,1)S(1)} %join.2.refs_0_), channel_id=1, source_target_pairs={{0,16},{2,18},{4,20},{6,22},{8,24},{10,26},{12,28},{14,30},{16,0},... | collective-permute-start | bytes 208904 | tf_op jit(solution)/shard_map/ppermute | solution.py:43
  22.3 2.8 %copy-start.1 = (f32[4096]{0:T(1024)S(1)}, f32[4096]{0:T(1024)}, u32[]{:S(2)}) copy-start(f32[4096]{0:T(1024)} %param.8) | copy-start | bytes 49156
  24.5 2.0 %collective-permute-start.7 = (bf16[16,2176]{1,0:T(8,128)(2,1)S(1)}, bf16[16,2176]{1,0:T(8,128)(2,1)S(1)}, u32[]{:S(2)}, u32[]{:S(2)}) collective-permute-start(bf16[16,2176]{1,0:T(8,128)(2,1)S(1)} %join.2.refs_0_), channel_id=1, source_target_pairs={{0,2},{2,0},{4,6},{6,4},{8,10},{10,8},{12,14},{14,12},{16,18},{18,... | collective-permute-start | bytes 208904 | tf_op jit(solution)/shard_map/ppermute | solution.py:43
  24.6 1.9 %collective-permute-start.8 = (bf16[16,2176]{1,0:T(8,128)(2,1)S(1)}, bf16[16,2176]{1,0:T(8,128)(2,1)S(1)}, u32[]{:S(2)}, u32[]{:S(2)}) collective-permute-start(bf16[16,2176]{1,0:T(8,128)(2,1)S(1)} %collective-permute-done.6.refs_1_), channel_id=1, source_target_pairs={{0,2},{2,0},{4,6},{6,4},{8,10},{10,8},{12,14},{14,12},{16,18},{18,... | collective-permute-start | bytes 208904 | tf_op jit(solution)/shard_map/ppermute | solution.py:43
  25.2 3.4 %copy-start.2 = (s32[2,16]{1,0:T(2,128)S(1)}, s32[2,16]{1,0:T(2,128)}, u32[]{:S(2)}) copy-start(s32[2,16]{1,0:T(2,128)} %refs_0_.6) | copy-start | bytes 388
  26.6 19.2 %copy-start.3 = (s32[2]{0:T(128)S(1)}, s32[2]{0:T(128)}, u32[]{:S(2)}) copy-start(s32[2]{0:T(128)} %refs_0_.7) | copy-start | bytes 28
  26.7 19.2 %copy-start.4 = (s32[2]{0:T(128)S(1)}, s32[2]{0:T(128)}, u32[]{:S(2)}) copy-start(s32[2]{0:T(128)} %refs_1_.1) | copy-start | bytes 28
  27.9 5.5 %collective-permute-start.9 = (f32[32,988]{1,0:T(8,128)S(1)}, f32[32,988]{1,0:T(8,128)S(1)}, u32[]{:S(2)}, u32[]{:S(2)}) collective-permute-start(f32[32,988]{1,0:T(8,128)S(1)} %convolution_add_fusion.refs_1_.first_ref), channel_id=1, source_target_pairs={{0,1},{1,0},{2,3},{3,2},{4,5},{5,4},{6,7},{7,6},{8,9},{9,8},{10,11... | collective-permute-start | bytes 379400 | tf_op jit(solution)/shard_map/ppermute | solution.py:43
  33.8 1.2 %collective-permute-start.10 = (f32[8,128]{1,0:T(8,128)S(1)}, f32[8,128]{1,0:T(8,128)S(1)}, u32[]{:S(2)}, u32[]{:S(2)}) collective-permute-start(f32[8,128]{1,0:T(8,128)S(1)} %get-tuple-element.30.first_ref.refs_2_), channel_id=1, source_target_pairs={{0,2},{2,0},{4,6},{6,4},{8,10},{10,8},{12,14},{14,12},{16,18},{18,... | collective-permute-start | bytes 12296 | tf_op jit(solution)/shard_map/ppermute | solution.py:43
  35.0 3.7 %collective-permute-start.11 = (f32[8,128]{1,0:T(8,128)S(1)}, f32[8,128]{1,0:T(8,128)S(1)}, u32[]{:S(2)}, u32[]{:S(2)}) collective-permute-start(f32[8,128]{1,0:T(8,128)S(1)} %merge.1.a_ref), channel_id=1, source_target_pairs={{0,4},{2,6},{4,0},{6,2},{8,12},{10,14},{12,8},{14,10},{16,20},{18,... | collective-permute-start | bytes 12296 | tf_op jit(solution)/shard_map/ppermute | solution.py:43
  35.6 3.6 %collective-permute-start.12 = (f32[8,128]{1,0:T(8,128)S(1)}, f32[8,128]{1,0:T(8,128)S(1)}, u32[]{:S(2)}, u32[]{:S(2)}) collective-permute-start(f32[8,128]{1,0:T(8,128)S(1)} %merge.1.a_ref), channel_id=1, source_target_pairs={{0,8},{2,10},{4,12},{6,14},{8,0},{10,2},{12,4},{14,6},{16,24},{18,... | collective-permute-start | bytes 12296 | tf_op jit(solution)/shard_map/ppermute | solution.py:43
  36.8 4.5 %collective-permute-start.13 = (f32[8,128]{1,0:T(8,128)S(1)}, f32[8,128]{1,0:T(8,128)S(1)}, u32[]{:S(2)}, u32[]{:S(2)}) collective-permute-start(f32[8,128]{1,0:T(8,128)S(1)} %merge.1.a_ref), channel_id=1, source_target_pairs={{0,12},{2,14},{4,8},{6,10},{8,4},{10,6},{12,0},{14,2},{16,28},{18,... | collective-permute-start | bytes 12296 | tf_op jit(solution)/shard_map/ppermute | solution.py:43
  41.3 4.6 %collective-permute-start.14 = (f32[8,128]{1,0:T(8,128)S(1)}, f32[8,128]{1,0:T(8,128)S(1)}, u32[]{:S(2)}, u32[]{:S(2)}) collective-permute-start(f32[8,128]{1,0:T(8,128)S(1)} %merge_four.1.refs_3_), channel_id=1, source_target_pairs={{0,16},{2,18},{4,20},{6,22},{8,24},{10,26},{12,28},{14,30},{16,0},... | collective-permute-start | bytes 12296 | tf_op jit(solution)/shard_map/ppermute | solution.py:43
  47.1 1.4 %collective-permute-start.15 = (bf16[32,2176]{1,0:T(8,128)(2,1)S(1)}, bf16[32,2176]{1,0:T(8,128)(2,1)S(1)}, u32[]{:S(2)}, u32[]{:S(2)}) collective-permute-start(bf16[32,2176]{1,0:T(8,128)(2,1)S(1)} %get-tuple-element.37.dep_ref), channel_id=1, source_target_pairs={{0,2},{2,0},{4,6},{6,4},{8,10},{10,8},{12,14},{14,12},{16,18},{18,... | collective-permute-start | bytes 417800 | tf_op jit(solution)/shard_map/ppermute | solution.py:43
  48.5 6.7 %collective-permute-start.16 = (bf16[16,2176]{1,0:T(8,128)(2,1)S(1)}, bf16[16,2176]{1,0:T(8,128)(2,1)S(1)}, u32[]{:S(2)}, u32[]{:S(2)}) collective-permute-start(bf16[16,2176]{1,0:T(8,128)(2,1)S(1)} %get-tuple-element.39.rest_0_), channel_id=1, source_target_pairs={{0,16},{2,18},{4,20},{6,22},{8,24},{10,26},{12,28},{14,30},{16,0},... | collective-permute-start | bytes 208904 | tf_op jit(solution)/shard_map/ppermute | solution.py:43
  55.3 4.4 %collective-permute-start.17 = (bf16[16,2176]{1,0:T(8,128)(2,1)S(1)}, bf16[16,2176]{1,0:T(8,128)(2,1)S(1)}, u32[]{:S(2)}, u32[]{:S(2)}) collective-permute-start(bf16[16,2176]{1,0:T(8,128)(2,1)S(1)} %add_convert_fusion.refs_0_.rest_0_), channel_id=1, source_target_pairs={{0,4},{2,6},{4,0},{6,2},{8,12},{10,14},{12,8},{14,10},{16,20},{18,... | collective-permute-start | bytes 208904 | tf_op jit(solution)/shard_map/ppermute | solution.py:43
  56.3 4.3 %collective-permute-start.18 = (bf16[16,2176]{1,0:T(8,128)(2,1)S(1)}, bf16[16,2176]{1,0:T(8,128)(2,1)S(1)}, u32[]{:S(2)}, u32[]{:S(2)}) collective-permute-start(bf16[16,2176]{1,0:T(8,128)(2,1)S(1)} %add_convert_fusion.refs_0_.rest_0_), channel_id=1, source_target_pairs={{0,8},{2,10},{4,12},{6,14},{8,0},{10,2},{12,4},{14,6},{16,24},{18,... | collective-permute-start | bytes 208904 | tf_op jit(solution)/shard_map/ppermute | solution.py:43
  56.3 5.6 %collective-permute-start.19 = (bf16[16,2176]{1,0:T(8,128)(2,1)S(1)}, bf16[16,2176]{1,0:T(8,128)(2,1)S(1)}, u32[]{:S(2)}, u32[]{:S(2)}) collective-permute-start(bf16[16,2176]{1,0:T(8,128)(2,1)S(1)} %add_convert_fusion.refs_0_.rest_0_), channel_id=1, source_target_pairs={{0,12},{2,14},{4,8},{6,10},{8,4},{10,6},{12,0},{14,2},{16,28},{18,... | collective-permute-start | bytes 208904 | tf_op jit(solution)/shard_map/ppermute | solution.py:43
  61.9 8.0 %collective-permute-start.20 = (bf16[16,2176]{1,0:T(8,128)(2,1)S(1)}, bf16[16,2176]{1,0:T(8,128)(2,1)S(1)}, u32[]{:S(2)}, u32[]{:S(2)}) collective-permute-start(bf16[16,2176]{1,0:T(8,128)(2,1)S(1)} %join.3.refs_1_.refs_6_), channel_id=1, source_target_pairs={{0,2},{2,0},{4,6},{6,4},{8,10},{10,8},{12,14},{14,12},{16,18},{18,... | collective-permute-start | bytes 208904 | tf_op jit(solution)/shard_map/ppermute | solution.py:43

commit v3 on v2

--- a/solution.py
+++ b/solution.py
@@ -207,23 +207,14 @@
     merge_kernel(near_ref, far_ref, out_ref)
 
 
-def scaled_part(spread, at_target, part_ref, scaled_ref, out_ref, tail_ref):
+def gradient_kernel(
+    blocks, length, model_width, num_ref, den_ref, own_ref, peer_ref, a_ref, b_ref, part_ref,
+    peer_part_ref, scaled_ref, inverse_ref, mine_ref, give_ref, meta_ref, loss_ref, rows_ref,
+    part_scratch, tail_ref,
+):
     total, half = scaled_ref.shape
-    part = spread * part_ref[:total, :] + at_target * part_ref[total:, :]
-    gain = jnp.sum(part * scaled_ref[...], axis=0, keepdims=True)
-    tail_ref[...] = jnp.zeros_like(tail_ref)
-    for j in range(half // LANES):
-        tail_ref[j : j + 1, :] = gain[:, j * LANES : (j + 1) * LANES]
-    out_ref[:, :half] = part.astype(out_ref.dtype)
-    out_ref[:, half:] = tail_ref[...].astype(out_ref.dtype)
-
-
-def send_kernel(
-    length, model_width, num_ref, den_ref, own_ref, a_ref, b_ref, part_ref, scaled_ref,
-    inverse_ref, send_ref, meta_ref, loss_ref, tail_ref, rows_ref,
-):
-    total = inverse_ref.shape[0]
     slots = total // 2
+    _, seq, _, _ = here(blocks)
     row_top, exp_total, moment, picked = merged(a_ref, b_ref)
     log_total = row_top + jnp.log(exp_total)
     place = lax.broadcasted_iota(jnp.int32, (1, LANES), 1)
@@ -232,34 +223,39 @@
     factor = den / (num * (2.0 * length))
     scale = LOSS_SCALE * factor
     inner = scale * (moment / exp_total - (picked - row_top)) / model_width
-    spread = scale * jnp.exp(own_ref[0:1, :] - log_total)
-    at_target = scale * (jnp.exp(picked - log_total) - 1.0)
     rows_ref[...] = jnp.zeros_like(rows_ref)
-    for k, row in enumerate((log_total, scale, inner, spread, at_target)):
+    for k, row in enumerate(
+        (
+            log_total,
+            scale,
+            inner,
+            scale * jnp.exp(own_ref[0:1, :] - log_total),
+            scale * jnp.exp(peer_ref[0:1, :] - log_total),
+            scale * (jnp.exp(picked - log_total) - 1.0),
+        )
+    ):
         rows_ref[k : k + 1, :] = row
     across = jnp.concatenate([rows_ref[...], jnp.zeros((LANES - SUBLANES, LANES), F32)]).T[:total]
-    scaled_part(across[:, 3:4], across[:, 4:5], part_ref, scaled_ref, send_ref, tail_ref)
+    part = (
+        across[:, 3:4] * part_ref[:total, :]
+        + across[:, 4:5] * peer_part_ref[:total, :].astype(F32)
+        + across[:, 5:6] * (part_ref[total:, :] + peer_part_ref[total:, :].astype(F32))
+    )
+    part_scratch[...] = part
+    gain = jnp.sum(part * scaled_ref[...], axis=0, keepdims=True)
+    tail_ref[...] = jnp.zeros_like(tail_ref)
+    for j in range(half // LANES):
+        tail_ref[j : j + 1, :] = gain[:, j * LANES : (j + 1) * LANES]
+    tail = tail_ref[...].astype(BF16)
+    for ref, s in ((mine_ref, seq), (give_ref, 1 - seq)):
+        rows = pl.ds(pl.multiple_of(s * slots, slots), slots)
+        ref[:, :half] = part_scratch[rows, :].astype(ref.dtype)
+        ref[:, half:] = tail.astype(ref.dtype)
     lane = lax.broadcasted_iota(jnp.int32, (total, LANES), 1)
     meta_ref[...] = jnp.where(lane == 2, across / inverse_ref[...], across)
     loss_ref[...] = jnp.sum(
         jnp.where(place < total, factor * (log_total - picked), 0.0), axis=1, keepdims=True
     )
-
-
-def keep_kernel(meta_ref, part_ref, scaled_ref, keep_ref, tail_ref):
-    scaled_part(meta_ref[:, 3:4], meta_ref[:, 4:5], part_ref, scaled_ref, keep_ref, tail_ref)
-
-
-def divide_kernel(blocks, keep_ref, arrived_ref, own_ref, give_ref):
-    slots = own_ref.shape[0]
-    half = own_ref.shape[1] - LANES
-    _, seq, _, _ = here(blocks)
-    tail = (keep_ref[:slots, half:] + arrived_ref[:slots, half:].astype(F32)).astype(BF16)
-    for ref, s in ((own_ref, seq), (give_ref, 1 - seq)):
-        rows = pl.ds(pl.multiple_of(s * slots, slots), slots)
-        part = keep_ref[rows, :half] + arrived_ref[rows, :half].astype(F32)
-        ref[:, :half] = part.astype(ref.dtype)
-        ref[:, half:] = tail.astype(ref.dtype)
 
 
 def dlogits_kernel(
@@ -444,7 +440,7 @@
 
     normed, scaled, inverse = normalize(0, mine, there)
     partial = contract(normed, loads[0])
-    normed_other, scaled_other = normalize(1, mine_other, there_other)
+    normed_other, _ = normalize(1, mine_other, there_other)
     partial = partial + contract(normed_other, loads[1])
     bit = 1
     while 2 * bit < lax.axis_size("vocab"):
@@ -483,7 +479,9 @@
             name="merge",
         )(a, b)
 
-    for bit in [1] + inner_bits[:-2]:
+    peer_table = swap(table, "ctx", 1)
+    table = merge(table, peer_table)
+    for bit in inner_bits[:-2]:
         table = merge(table, swap(table, "ctx", bit))
     near = [table] + around(table)
     table = pl.pallas_call(
@@ -496,32 +494,29 @@
         name="merge_four",
     )(*near)
     there_table = swap(table, "ctx", blocks)
+    part_other = jnp.dot(exps, loads[1], preferred_element_type=F32).astype(BF16)
     part = jnp.dot(exps, loads[0], preferred_element_type=F32)
-    part_other = jnp.dot(exps, loads[1], preferred_element_type=F32)
-    send, meta, loss_value = pl.pallas_call(
-        lambda *refs: send_kernel(tok * blocks, model_width, *refs),
-        in_specs=[smem(), smem()] + [vmem()] * 6,
-        out_specs=[vmem()] * 3,
+    peer_part = swap(part_other, "ctx", 1)
+    own_part, give, meta, loss_value = pl.pallas_call(
+        lambda *refs: gradient_kernel(blocks, tok * blocks, model_width, *refs),
+        in_specs=[smem(), smem()] + [vmem()] * 8,
+        out_specs=[vmem()] * 4,
         out_shape=[
-            shape((total, packed_width), BF16),
+            shape((slots, packed_width), F32),
+            shape((slots, packed_width), BF16),
             shape((total, LANES), F32),
             shape((1, 1), F32),
         ],
-        scratch_shapes=[pltpu.VMEM((total, LANES), F32), pltpu.VMEM((SUBLANES, LANES), F32)],
+        scratch_shapes=[
+            pltpu.VMEM((SUBLANES, LANES), F32),
+            pltpu.VMEM((total, half), F32),
+            pltpu.VMEM((slots, LANES), F32),
+        ],
         compiler_params=params(8),
-        name="send_part",
-    )(t_num, t_den, own_table, table, there_table, part_other, scaled_other, inverse)
-    keep = pl.pallas_call(
-        keep_kernel,
-        in_specs=[vmem()] * 3,
-        out_specs=vmem(),
-        out_shape=shape((total, packed_width), F32),
-        scratch_shapes=[pltpu.VMEM((total, LANES), F32)],
-        compiler_params=params(8),
-        name="keep_part",
-    )(meta, part, scaled)
-
-    steps = 8
+        name="gradient",
+    )(t_num, t_den, own_table, peer_table, table, there_table, part, peer_part, scaled, inverse)
+
+    steps = 4
     step = width // steps
     grad_head = None
 
@@ -543,15 +538,6 @@
             name="head_grad",
         )(dlogits, normed, *extra)
 
-    arrived = swap(send, "ctx", 1)
-    own_part, give = pl.pallas_call(
-        lambda *refs: divide_kernel(blocks, *refs),
-        in_specs=[vmem()] * 2,
-        out_specs=[vmem()] * 2,
-        out_shape=[shape((slots, packed_width), F32), shape((slots, packed_width), BF16)],
-        compiler_params=params(6),
-        name="divide",
-    )(keep, arrived)
     dlogits, normed = pl.pallas_call(
         dlogits_kernel,
         in_specs=[vmem()] * 5 + [anywhere()],
@@ -559,8 +545,8 @@
         out_shape=[shape((voc, total), BF16), shape((total, width), BF16)],
         compiler_params=params(6),
         name="dlogits",
-    )(targets, logits, meta, normed, normed_other, send)
-    middle = steps // 2
+    )(targets, logits, meta, normed, normed_other, give)
+    middle = 2
     grad_head = head_part(0, middle, give, None)
     sent = (own_part + swap(give, "ctx", blocks).astype(F32)).astype(BF16)
     for bit in inner_bits[:-2]:

time: 71.5 us -> 69.8 us (0.976)
  waiting for transfers between devices: 26.9 us -> 25.5 us
    ppermute x20, waiting for transfers between devices: 25.4 us -> 24.1 us  [swap(): lax.ppermute(x, axis, [(i, i ^ bit) for i in range(lax.axis_size(axis))])]
    pallas_call x2, Pallas kernels: 6.28 us -> 5.3 us  [head_part(): pl.pallas_call(head_kernel, grid=(last - first,), in_specs=[pl.BlockSpec(...]
    pallas_call x3 -> x1, Pallas kernels: 1.45 us -> 1.33 us  [device_step(): pl.pallas_call(lambda *refs: gradient_kernel(blocks, tok * blocks, model_...]
  transfers between devices with their start and end apart: 21 -> 21, of which waited for: 16 -> 13; matrix products, arithmetic and copies ran while one was open for 4% -> 4% of each run, Pallas kernels for 18% -> 17%
where the time goes in v3:
time: 69.8 us; the launch traced here: 69.5 us
  waiting for transfers between devices  25.5 us (37%)
  starting transfers between devices  20.7 us (30%)
  Pallas kernels  16.2 us (23%)
  matrix products  4.57 us (7%)
  other arithmetic  0.93 us (1%)
  between operations  0.85 us (1%)
  local copies, waits for them, and re-layouts  0.77 us (1%)
    ppermute x20, waiting for transfers between devices, swap(): lax.ppermute(x, axis, [(i, i ^ bit) for i in range(lax.axis_size(axis))])  24.1 us
    ppermute x20, starting transfers between devices, swap(): lax.ppermute(x, axis, [(i, i ^ bit) for i in range(lax.axis_size(axis))])  20.7 us
    pallas_call x2, Pallas kernels, head_part(): pl.pallas_call(head_kernel, grid=(last - first,), in_specs=[pl.BlockSpec(...  5.3 us
    pallas_call x2, Pallas kernels, load(): pl.pallas_call(lambda *refs: load_kernel(side, *refs), in_specs=[anywhere...  4.33 us
    pallas_call x2, Pallas kernels, finish(): pl.pallas_call(lambda *refs: final_kernel(blocks, side, *refs), in_specs=...  2.71 us
    dot_general x2, matrix products, contract(): lax.dot_general(a, b, (((1,), (1,)), ((), ())), preferred_element_type=F32)  2.51 us
    ppermute x1, waiting for transfers between devices, device_step(): lax.ppermute(squares, ('ctx', 'vocab'), [(i, i ^ ways + 1) for i in range...  1.45 us
  transfers between devices with their start and end apart: 21, of which 13 were waited for; matrix products, arithmetic and copies ran while one was open for 4% of the time, Pallas kernels for 17%

profile of v3, /device:TPU:0, one launch (start us, length us, event | category | flops | bytes accessed | tf_op | source)
XLA Modules:
  0.0 69.5 jit_solution(879539832978061145)
XLA Ops:
  0.6 0.0 copy-start
  0.7 0.8 %subtract_bitcast_fusion = s32[16]{0:T(128)S(1)} fusion(s32[2,16]{1,0:T(2,128)} %param.10, s32[]{:T(128)S(6)} %select_n.15, s32[]{:T(128)S(6)} %mul.3), kind=kLoop, calls=%fused_computation.7 | loop fusion | flops 16 | bytes 136 | tf_op jit(solution)/shard_map/sub | solution.py:341
  1.5 0.7 %copy-done = bf16[256,4096]{1,0:T(8,128)(2,1)S(1)} copy-done((bf16[256,4096]{1,0:T(8,128)(2,1)S(1)}, bf16[256,4096]{1,0:T(8,128)(2,1)}, u32[]{:S(2)}) %copy-start) | copy-done | bytes 2097176
  2.2 0.4 fusion.1.rows_ref
  2.7 0.1 pick.1
  2.8 0.6 collective-permute-start
  3.4 2.5 %collective-permute-start.1 = (f32[16,128]{1,0:T(8,128)S(1)}, f32[16,128]{1,0:T(8,128)S(1)}, u32[]{:S(2)}, u32[]{:S(2)}) collective-permute-start(f32[16,128]{1,0:T(8,128)S(1)} %get-tuple-element.25.squares_ref), channel_id=1, source_target_pairs={{0,1},{1,0},{2,3},{3,2},{4,5},{5,4},{6,7},{7,6},{8,9},{9,8},{10,11... | collective-permute-start | bytes 24584 | tf_op jit(solution)/shard_map/ppermute | solution.py:43
  5.9 0.0 collective-permute-start.2
  5.9 1.6 %collective-permute-done.1.up_ref = f32[16,128]{1,0:T(8,128)S(1)} collective-permute-done((f32[16,128]{1,0:T(8,128)S(1)}, f32[16,128]{1,0:T(8,128)S(1)}, u32[]{:S(2)}, u32[]{:S(2)}) %collective-permute-start.1) | collective-permute-done | bytes 8224 | tf_op jit(solution)/shard_map/ppermute | solution.py:43
  7.5 1.4 %collective-permute-done.2.across_ref = f32[16,128]{1,0:T(8,128)S(1)} collective-permute-done((f32[16,128]{1,0:T(8,128)S(1)}, f32[16,128]{1,0:T(8,128)S(1)}, u32[]{:S(2)}, u32[]{:S(2)}) %collective-permute-start.2) | collective-permute-done | bytes 8224 | tf_op jit(solution)/shard_map/ppermute | solution.py:372
  9.0 0.2 settle.1.refs_0_.refs_1_
  9.1 1.5 %collective-permute-start.3 = (bf16[16,2176]{1,0:T(8,128)(2,1)S(1)}, bf16[16,2176]{1,0:T(8,128)(2,1)S(1)}, u32[]{:S(2)}, u32[]{:S(2)}) collective-permute-start(bf16[16,2176]{1,0:T(8,128)(2,1)S(1)} %settle.1.refs_0_.refs_1_), channel_id=1, source_target_pairs={{0,4},{2,6},{4,0},{6,2},{8,12},{10,14},{12,8},{14,10},{16,20},{18,... | collective-permute-start | bytes 208904 | tf_op jit(solution)/shard_map/ppermute | solution.py:43
  10.6 1.6 %collective-permute-start.4 = (bf16[16,2176]{1,0:T(8,128)(2,1)S(1)}, bf16[16,2176]{1,0:T(8,128)(2,1)S(1)}, u32[]{:S(2)}, u32[]{:S(2)}) collective-permute-start(bf16[16,2176]{1,0:T(8,128)(2,1)S(1)} %settle.1.refs_0_.refs_1_), channel_id=1, source_target_pairs={{0,8},{2,10},{4,12},{6,14},{8,0},{10,2},{12,4},{14,6},{16,24},{18,... | collective-permute-start | bytes 208904 | tf_op jit(solution)/shard_map/ppermute | solution.py:43
  12.2 0.4 collective-permute-start.5
  12.6 0.8 %collective-permute-done.3.refs_1_ = bf16[16,2176]{1,0:T(8,128)(2,1)S(1)} collective-permute-done((bf16[16,2176]{1,0:T(8,128)(2,1)S(1)}, bf16[16,2176]{1,0:T(8,128)(2,1)S(1)}, u32[]{:S(2)}, u32[]{:S(2)}) %collective-permute-start.3) | collective-permute-done | bytes 69664 | tf_op jit(solution)/shard_map/ppermute | solution.py:43
  13.5 2.1 %collective-permute-done.4.refs_2_ = bf16[16,2176]{1,0:T(8,128)(2,1)S(1)} collective-permute-done((bf16[16,2176]{1,0:T(8,128)(2,1)S(1)}, bf16[16,2176]{1,0:T(8,128)(2,1)S(1)}, u32[]{:S(2)}, u32[]{:S(2)}) %collective-permute-start.4) | collective-permute-done | bytes 69664 | tf_op jit(solution)/shard_map/ppermute | solution.py:43
  15.5 1.9 %collective-permute-done.5.refs_3_ = bf16[16,2176]{1,0:T(8,128)(2,1)S(1)} collective-permute-done((bf16[16,2176]{1,0:T(8,128)(2,1)S(1)}, bf16[16,2176]{1,0:T(8,128)(2,1)S(1)}, u32[]{:S(2)}, u32[]{:S(2)}) %collective-permute-start.5) | collective-permute-done | bytes 69664 | tf_op jit(solution)/shard_map/ppermute | solution.py:43
  17.5 2.7 %collective-permute-start.6 = (bf16[16,2176]{1,0:T(8,128)(2,1)S(1)}, bf16[16,2176]{1,0:T(8,128)(2,1)S(1)}, u32[]{:S(2)}, u32[]{:S(2)}) collective-permute-start(bf16[16,2176]{1,0:T(8,128)(2,1)S(1)} %join.2.refs_0_), channel_id=1, source_target_pairs={{0,16},{2,18},{4,20},{6,22},{8,24},{10,26},{12,28},{14,30},{16,0},... | collective-permute-start | bytes 208904 | tf_op jit(solution)/shard_map/ppermute | solution.py:43
  20.1 2.2 %load.2 = bf16[988,2048]{1,0:T(8,128)(2,1)S(1)} custom-call(bf16[988,4096]{1,0:T(8,128)(2,1)} %refs_0_.5, bf16[16,2176]{1,0:T(8,128)(2,1)S(1)} %get-tuple-element.23.first_ref.refs_1_), custom_call_target="tpu_custom_call" | custom-call | bytes 8093696 | tf_op jit(solution)/shard_map/load/pallas_call | solution.py:358
  22.3 0.0 copy-start.1
  22.3 2.2 %load.3 = bf16[988,2048]{1,0:T(8,128)(2,1)S(1)} custom-call(bf16[988,4096]{1,0:T(8,128)(2,1)} %refs_0_.5, bf16[16,2176]{1,0:T(8,128)(2,1)S(1)} %settle.1.refs_0_.refs_1_), custom_call_target="tpu_custom_call" | custom-call | bytes 8093696 | tf_op jit(solution)/shard_map/load/pallas_call | solution.py:358
  24.5 0.1 collective-permute-start.7
  24.6 0.0 collective-permute-done.6.refs_1_
  24.6 0.5 collective-permute-start.8
  25.1 0.1 normalize.2
  25.2 0.0 copy-start.2
  25.2 1.3 %fusion.3 = f32[32,988]{1,0:T(8,128)S(1)} fusion(bf16[32,2048]{1,0:T(8,128)(2,1)S(1)} %get-tuple-element.26.own_ref, bf16[988,2048]{1,0:T(8,128)(2,1)S(1)} %load.2), kind=kOutput, calls=%fused_computation.8 | convolution fusion | flops 129499136 | bytes 4304384 | tf_op jit(solution)/shard_map/dot_general | solution.py:439
  26.5 0.0 collective-permute-done.8.refs_1_
  26.5 0.8 %normalize.3 = (bf16[32,2048]{1,0:T(8,128)(2,1)S(1)}, f32[32,2048]{1,0:T(8,128)}) custom-call(bf16[16,2176]{1,0:T(8,128)(2,1)S(1)} %collective-permute-done.7.refs_0_, bf16[16,2176]{1,0:T(8,128)(2,1)S(1)} %collective-permute-done.8.refs_1_, f32[1,4096]{1,0:T(1,128)S(1)} %bitcast.15), custom_call_target="tpu_custom_call" | custom-call | tf_op jit(solution)/shard_map/normalize/pallas_call | solution.py:429
  27.3 1.3 %convolution_add_fusion.refs_1_.first_ref = f32[32,988]{1,0:T(8,128)S(1)} fusion(f32[32,988]{1,0:T(8,128)S(1)} %fusion.3, bf16[32,2048]{1,0:T(8,128)(2,1)S(1)} %get-tuple-element.27.other_ref, bf16[988,2048]{1,0:T(8,128)(2,1)S(1)} %load.3), kind=kOutput, calls=%fused_computation.1 | convolution fusion | flops 129530752 | bytes 4430848 | tf_op jit(solution)/shard_map/dot_general | solution.py:439
  28.6 0.6 collective-permute-start.9
  29.2 0.6 targets.1.targets_ref
  29.8 4.3 %collective-permute-done.9.second_ref = f32[32,988]{1,0:T(8,128)S(1)} collective-permute-done((f32[32,988]{1,0:T(8,128)S(1)}, f32[32,988]{1,0:T(8,128)S(1)}, u32[]{:S(2)}, u32[]{:S(2)}) %collective-permute-start.9) | collective-permute-done | bytes 126496 | tf_op jit(solution)/shard_map/ppermute | solution.py:43
  34.1 0.4 stats.1
  34.5 0.0 collective-permute-start.10
  34.5 1.2 %collective-permute-done.10.second_ref.refs_3_ = f32[8,128]{1,0:T(8,128)S(1)} collective-permute-done((f32[8,128]{1,0:T(8,128)S(1)}, f32[8,128]{1,0:T(8,128)S(1)}, u32[]{:S(2)}, u32[]{:S(2)}) %collective-permute-start.10) | collective-permute-done | bytes 4128 | tf_op jit(solution)/shard_map/ppermute | solution.py:43
  35.7 0.6 collective-permute-start.11
  36.3 1.2 %collective-permute-start.12 = (f32[8,128]{1,0:T(8,128)S(1)}, f32[8,128]{1,0:T(8,128)S(1)}, u32[]{:S(2)}, u32[]{:S(2)}) collective-permute-start(f32[8,128]{1,0:T(8,128)S(1)} %merge.1.a_ref), channel_id=1, source_target_pairs={{0,8},{2,10},{4,12},{6,14},{8,0},{10,2},{12,4},{14,6},{16,24},{18,... | collective-permute-start | bytes 12296 | tf_op jit(solution)/shard_map/ppermute | solution.py:43
  37.4 1.8 %collective-permute-start.13 = (f32[8,128]{1,0:T(8,128)S(1)}, f32[8,128]{1,0:T(8,128)S(1)}, u32[]{:S(2)}, u32[]{:S(2)}) collective-permute-start(f32[8,128]{1,0:T(8,128)S(1)} %merge.1.a_ref), channel_id=1, source_target_pairs={{0,12},{2,14},{4,8},{6,10},{8,4},{10,6},{12,0},{14,2},{16,28},{18,... | collective-permute-start | bytes 12296 | tf_op jit(solution)/shard_map/ppermute | solution.py:43
  39.2 0.8 %convolution_convert_fusion = bf16[64,2048]{1,0:T(8,128)(2,1)S(1)} fusion(bf16[64,988]{1,0:T(8,128)(2,1)S(1)} %get-tuple-element.29, bf16[988,2048]{1,0:T(8,128)(2,1)S(1)} %load.3), kind=kOutput, calls=%fused_computation | convolution fusion | flops 259129344 | bytes 4435456 | tf_op jit(solution)/shard_map/dot_general | solution.py:497
  40.1 0.1 collective-permute-start.15
  40.1 0.0 collective-permute-done.11.b_ref
  40.1 0.0 collective-permute-done.12.c_ref
  40.2 1.8 %collective-permute-done.13.d_ref = f32[8,128]{1,0:T(8,128)S(1)} collective-permute-done((f32[8,128]{1,0:T(8,128)S(1)}, f32[8,128]{1,0:T(8,128)S(1)}, u32[]{:S(2)}, u32[]{:S(2)}) %collective-permute-start.13) | collective-permute-done | bytes 4128 | tf_op jit(solution)/shard_map/ppermute | solution.py:43
  42.0 1.5 %collective-permute-start.14 = (f32[8,128]{1,0:T(8,128)S(1)}, f32[8,128]{1,0:T(8,128)S(1)}, u32[]{:S(2)}, u32[]{:S(2)}) collective-permute-start(f32[8,128]{1,0:T(8,128)S(1)} %merge_four.1.refs_4_), channel_id=1, source_target_pairs={{0,16},{2,18},{4,20},{6,22},{8,24},{10,26},{12,28},{14,30},{16,0},... | collective-permute-start | bytes 12296 | tf_op jit(solution)/shard_map/ppermute | solution.py:43
  43.5 0.8 %fusion.4.refs_6_ = f32[64,2048]{1,0:T(8,128)S(1)} fusion(bf16[64,988]{1,0:T(8,128)(2,1)S(1)} %get-tuple-element.29, bf16[988,2048]{1,0:T(8,128)(2,1)S(1)} %load.2), kind=kOutput, calls=%fused_computation.9 | convolution fusion | flops 258998272 | bytes 4697600 | tf_op jit(solution)/shard_map/dot_general | solution.py:498
  44.3 2.2 %collective-permute-done.14.refs_5_ = f32[8,128]{1,0:T(8,128)S(1)} collective-permute-done((f32[8,128]{1,0:T(8,128)S(1)}, f32[8,128]{1,0:T(8,128)S(1)}, u32[]{:S(2)}, u32[]{:S(2)}) %collective-permute-start.14) | collective-permute-done | bytes 4128 | tf_op jit(solution)/shard_map/ppermute | solution.py:43
  46.5 0.0 collective-permute-done.15.refs_7_
  46.5 1.3 %gradient.1 = (f32[16,2176]{1,0:T(8,128)S(1)}, bf16[16,2176]{1,0:T(8,128)(2,1)S(1)}, f32[32,128]{1,0:T(8,128)S(1)}, f32[1,1]{1,0:T(1,128)}) custom-call(s32[2]{0:T(128)S(1)} %copy-done.3, s32[2]{0:T(128)S(1)} %copy-done.4, f32[8,128]{1,0:T(8,128)S(1)} %get-tuple-element.28.first_ref.refs_2_, f32[8,128]{1,0:T(8,128)S(1)} %collective-permute-done.10.second_ref.refs_3_, ...), custom_call_target="tpu_custom_call" | custom-call | tf_op jit(solution)/shard_map/gradient/pallas_call | solution.py:500
  47.9 1.4 %collective-permute-start.16 = (bf16[16,2176]{1,0:T(8,128)(2,1)S(1)}, bf16[16,2176]{1,0:T(8,128)(2,1)S(1)}, u32[]{:S(2)}, u32[]{:S(2)}) collective-permute-start(bf16[16,2176]{1,0:T(8,128)(2,1)S(1)} %get-tuple-element.34.dep_ref.rest_0_), channel_id=1, source_target_pairs={{0,16},{2,18},{4,20},{6,22},{8,24},{10,26},{12,28},{14,30},{16,0},... | collective-permute-start | bytes 208904 | tf_op jit(solution)/shard_map/ppermute | solution.py:43
  49.3 4.6 %collective-permute-done.16 = bf16[16,2176]{1,0:T(8,128)(2,1)S(1)} collective-permute-done((bf16[16,2176]{1,0:T(8,128)(2,1)S(1)}, bf16[16,2176]{1,0:T(8,128)(2,1)S(1)}, u32[]{:S(2)}, u32[]{:S(2)}) %collective-permute-start.16) | collective-permute-done | bytes 69664 | tf_op jit(solution)/shard_map/ppermute | solution.py:43
  54.0 0.1 collective-permute-start.17
  54.1 1.8 %collective-permute-start.18 = (bf16[16,2176]{1,0:T(8,128)(2,1)S(1)}, bf16[16,2176]{1,0:T(8,128)(2,1)S(1)}, u32[]{:S(2)}, u32[]{:S(2)}) collective-permute-start(bf16[16,2176]{1,0:T(8,128)(2,1)S(1)} %add_convert_fusion.refs_0_.rest_0_), channel_id=1, source_target_pairs={{0,8},{2,10},{4,12},{6,14},{8,0},{10,2},{12,4},{14,6},{16,24},{18,... | collective-permute-start | bytes 208904 | tf_op jit(solution)/shard_map/ppermute | solution.py:43
  55.8 1.7 %collective-permute-start.19 = (bf16[16,2176]{1,0:T(8,128)(2,1)S(1)}, bf16[16,2176]{1,0:T(8,128)(2,1)S(1)}, u32[]{:S(2)}, u32[]{:S(2)}) collective-permute-start(bf16[16,2176]{1,0:T(8,128)(2,1)S(1)} %add_convert_fusion.refs_0_.rest_0_), channel_id=1, source_target_pairs={{0,12},{2,14},{4,8},{6,10},{8,4},{10,6},{12,0},{14,2},{16,28},{18,... | collective-permute-start | bytes 208904 | tf_op jit(solution)/shard_map/ppermute | solution.py:43
  57.5 0.8 %collective-permute-done.17.refs_1_ = bf16[16,2176]{1,0:T(8,128)(2,1)S(1)} collective-permute-done((bf16[16,2176]{1,0:T(8,128)(2,1)S(1)}, bf16[16,2176]{1,0:T(8,128)(2,1)S(1)}, u32[]{:S(2)}, u32[]{:S(2)}) %collective-permute-start.17) | collective-permute-done | bytes 69664 | tf_op jit(solution)/shard_map/ppermute | solution.py:43
  58.3 0.1 collective-permute-done.18.refs_2_
  58.4 2.6 %collective-permute-done.19.refs_3_ = bf16[16,2176]{1,0:T(8,128)(2,1)S(1)} collective-permute-done((bf16[16,2176]{1,0:T(8,128)(2,1)S(1)}, bf16[16,2176]{1,0:T(8,128)(2,1)S(1)}, u32[]{:S(2)}, u32[]{:S(2)}) %collective-permute-start.19) | collective-permute-done | bytes 69664 | tf_op jit(solution)/shard_map/ppermute | solution.py:43
  61.1 0.1 collective-permute-start.20
  61.2 0.1 fusion.refs_0_
  61.3 0.3 dlogits.1
  61.5 2.7 %head_grad.2.rest_1_ = bf16[988,4096]{1,0:T(8,128)(2,1)} custom-call(bf16[988,32]{1,0:T(8,128)(2,1)S(1)} %get-tuple-element.39.dlogits_ref, bf16[32,4096]{1,0:T(8,128)(2,1)S(1)} %get-tuple-element.40.normed_ref, bf16[16,2176]{1,0:T(8,128)(2,1)S(1)} %get-tuple-element.34.dep_ref.rest_0_), custom_call_target="tpu_custom_call" | custom-call | bytes 4046848 | tf_op jit(solution)/shard_map/head_grad/pallas_call | solution.py:525
  64.2 2.6 %head_grad.3 = bf16[988,4096]{1,0:T(8,128)(2,1)} custom-call(bf16[988,32]{1,0:T(8,128)(2,1)S(1)} %get-tuple-element.39.dlogits_ref, bf16[32,4096]{1,0:T(8,128)(2,1)S(1)} %get-tuple-element.40.normed_ref, bf16[16,2176]{1,0:T(8,128)(2,1)S(1)} %add_convert_fusion.refs_0_.rest_0_, bf16[988,4096]{1,0:T(8,128)(2,1)} %head_grad.2.rest_1_), custom_call_target="tpu_custom_call", output_to_operand_aliasing={{}: (3, {})} | custom-call | bytes 4046848 | tf_op jit(solution)/shard_map/head_grad/pallas_call | solution.py:525
  66.8 1.3 %final.2.refs_7_ = bf16[256,4096]{1,0:T(8,128)(2,1)} custom-call(bf16[16,256]{1,0:T(8,128)(2,1)S(1)} %fusion.refs_0_, bf16[16,2176]{1,0:T(8,128)(2,1)S(1)} %join.3.refs_1_.refs_6_, bf16[16,4096]{1,0:T(8,128)(2,1)S(1)} %get-tuple-element.35.refs_2_, f32[32,128]{1,0:T(8,128)S(1)} %get-tuple-element.31.refs_9_.refs_3_, ...), custom_call_target="tpu_custom_call" | custom-call | tf_op jit(solution)/shard_map/final/pallas_call | solution.py:560
  68.2 1.4 %final.3 = (bf16[256,4096]{1,0:T(8,128)(2,1)}, f32[1,4096]{1,0:T(1,128)}) custom-call(bf16[16,256]{1,0:T(8,128)(2,1)S(1)} %fusion.refs_0_, bf16[16,2176]{1,0:T(8,128)(2,1)S(1)} %collective-permute-done.20.refs_1_, bf16[16,4096]{1,0:T(8,128)(2,1)S(1)} %get-tuple-element.35.refs_2_, ...), custom_call_target="tpu_custom_call", output_to_operand_aliasing={{0}: (7, {})} | custom-call | tf_op jit(solution)/shard_map/final/pallas_call | solution.py:560
  (14 shorter events, 0.2 us)
Async XLA Ops:
  0.6 1.6 %copy-start = (bf16[256,4096]{1,0:T(8,128)(2,1)S(1)}, bf16[256,4096]{1,0:T(8,128)(2,1)}, u32[]{:S(2)}) copy-start(bf16[256,4096]{1,0:T(8,128)(2,1)} %param.7) | copy-start | bytes 6291460
  2.8 6.2 %collective-permute-start = (bf16[16,2176]{1,0:T(8,128)(2,1)S(1)}, bf16[16,2176]{1,0:T(8,128)(2,1)S(1)}, u32[]{:S(2)}, u32[]{:S(2)}) collective-permute-start(bf16[16,2176]{1,0:T(8,128)(2,1)S(1)} %get-tuple-element.24), channel_id=1, source_target_pairs={{0,2},{2,0},{4,6},{6,4},{8,10},{10,8},{12,14},{14,12},{16,18},{18,... | collective-permute-start | bytes 208904 | tf_op jit(solution)/shard_map/ppermute | solution.py:43
  3.4 4.2 %collective-permute-start.1 = (f32[16,128]{1,0:T(8,128)S(1)}, f32[16,128]{1,0:T(8,128)S(1)}, u32[]{:S(2)}, u32[]{:S(2)}) collective-permute-start(f32[16,128]{1,0:T(8,128)S(1)} %get-tuple-element.25.squares_ref), channel_id=1, source_target_pairs={{0,1},{1,0},{2,3},{3,2},{4,5},{5,4},{6,7},{7,6},{8,9},{9,8},{10,11... | collective-permute-start | bytes 24584 | tf_op jit(solution)/shard_map/ppermute | solution.py:43
  5.9 3.1 %collective-permute-start.2 = (f32[16,128]{1,0:T(8,128)S(1)}, f32[16,128]{1,0:T(8,128)S(1)}, u32[]{:S(2)}, u32[]{:S(2)}) collective-permute-start(f32[16,128]{1,0:T(8,128)S(1)} %get-tuple-element.25.squares_ref), channel_id=1, source_target_pairs={{0,3},{1,2},{2,1},{3,0},{4,7},{5,6},{6,5},{7,4},{8,11},{9,10},{10,... | collective-permute-start | bytes 24584 | tf_op jit(solution)/shard_map/ppermute | solution.py:372
  9.1 4.3 %collective-permute-start.3 = (bf16[16,2176]{1,0:T(8,128)(2,1)S(1)}, bf16[16,2176]{1,0:T(8,128)(2,1)S(1)}, u32[]{:S(2)}, u32[]{:S(2)}) collective-permute-start(bf16[16,2176]{1,0:T(8,128)(2,1)S(1)} %settle.1.refs_0_.refs_1_), channel_id=1, source_target_pairs={{0,4},{2,6},{4,0},{6,2},{8,12},{10,14},{12,8},{14,10},{16,20},{18,... | collective-permute-start | bytes 208904 | tf_op jit(solution)/shard_map/ppermute | solution.py:43
  10.6 4.9 %collective-permute-start.4 = (bf16[16,2176]{1,0:T(8,128)(2,1)S(1)}, bf16[16,2176]{1,0:T(8,128)(2,1)S(1)}, u32[]{:S(2)}, u32[]{:S(2)}) collective-permute-start(bf16[16,2176]{1,0:T(8,128)(2,1)S(1)} %settle.1.refs_0_.refs_1_), channel_id=1, source_target_pairs={{0,8},{2,10},{4,12},{6,14},{8,0},{10,2},{12,4},{14,6},{16,24},{18,... | collective-permute-start | bytes 208904 | tf_op jit(solution)/shard_map/ppermute | solution.py:43
  12.2 5.2 %collective-permute-start.5 = (bf16[16,2176]{1,0:T(8,128)(2,1)S(1)}, bf16[16,2176]{1,0:T(8,128)(2,1)S(1)}, u32[]{:S(2)}, u32[]{:S(2)}) collective-permute-start(bf16[16,2176]{1,0:T(8,128)(2,1)S(1)} %settle.1.refs_0_.refs_1_), channel_id=1, source_target_pairs={{0,12},{2,14},{4,8},{6,10},{8,4},{10,6},{12,0},{14,2},{16,28},{18,... | collective-permute-start | bytes 208904 | tf_op jit(solution)/shard_map/ppermute | solution.py:43
  17.5 7.1 %collective-permute-start.6 = (bf16[16,2176]{1,0:T(8,128)(2,1)S(1)}, bf16[16,2176]{1,0:T(8,128)(2,1)S(1)}, u32[]{:S(2)}, u32[]{:S(2)}) collective-permute-start(bf16[16,2176]{1,0:T(8,128)(2,1)S(1)} %join.2.refs_0_), channel_id=1, source_target_pairs={{0,16},{2,18},{4,20},{6,22},{8,24},{10,26},{12,28},{14,30},{16,0},... | collective-permute-start | bytes 208904 | tf_op jit(solution)/shard_map/ppermute | solution.py:43
  22.3 2.8 %copy-start.1 = (f32[4096]{0:T(1024)S(1)}, f32[4096]{0:T(1024)}, u32[]{:S(2)}) copy-start(f32[4096]{0:T(1024)} %param.8) | copy-start | bytes 49156
  24.5 2.0 %collective-permute-start.7 = (bf16[16,2176]{1,0:T(8,128)(2,1)S(1)}, bf16[16,2176]{1,0:T(8,128)(2,1)S(1)}, u32[]{:S(2)}, u32[]{:S(2)}) collective-permute-start(bf16[16,2176]{1,0:T(8,128)(2,1)S(1)} %join.2.refs_0_), channel_id=1, source_target_pairs={{0,2},{2,0},{4,6},{6,4},{8,10},{10,8},{12,14},{14,12},{16,18},{18,... | collective-permute-start | bytes 208904 | tf_op jit(solution)/shard_map/ppermute | solution.py:43
  24.6 1.9 %collective-permute-start.8 = (bf16[16,2176]{1,0:T(8,128)(2,1)S(1)}, bf16[16,2176]{1,0:T(8,128)(2,1)S(1)}, u32[]{:S(2)}, u32[]{:S(2)}) collective-permute-start(bf16[16,2176]{1,0:T(8,128)(2,1)S(1)} %collective-permute-done.6.refs_1_), channel_id=1, source_target_pairs={{0,2},{2,0},{4,6},{6,4},{8,10},{10,8},{12,14},{14,12},{16,18},{18,... | collective-permute-start | bytes 208904 | tf_op jit(solution)/shard_map/ppermute | solution.py:43
  25.2 4.0 %copy-start.2 = (s32[2,16]{1,0:T(2,128)S(1)}, s32[2,16]{1,0:T(2,128)}, u32[]{:S(2)}) copy-start(s32[2,16]{1,0:T(2,128)} %refs_0_.6) | copy-start | bytes 388
  28.6 5.5 %collective-permute-start.9 = (f32[32,988]{1,0:T(8,128)S(1)}, f32[32,988]{1,0:T(8,128)S(1)}, u32[]{:S(2)}, u32[]{:S(2)}) collective-permute-start(f32[32,988]{1,0:T(8,128)S(1)} %convolution_add_fusion.refs_1_.first_ref), channel_id=1, source_target_pairs={{0,1},{1,0},{2,3},{3,2},{4,5},{5,4},{6,7},{7,6},{8,9},{9,8},{10,11... | collective-permute-start | bytes 379400 | tf_op jit(solution)/shard_map/ppermute | solution.py:43
  34.5 1.2 %collective-permute-start.10 = (f32[8,128]{1,0:T(8,128)S(1)}, f32[8,128]{1,0:T(8,128)S(1)}, u32[]{:S(2)}, u32[]{:S(2)}) collective-permute-start(f32[8,128]{1,0:T(8,128)S(1)} %get-tuple-element.28.first_ref.refs_2_), channel_id=1, source_target_pairs={{0,2},{2,0},{4,6},{6,4},{8,10},{10,8},{12,14},{14,12},{16,18},{18,... | collective-permute-start | bytes 12296 | tf_op jit(solution)/shard_map/ppermute | solution.py:43
  35.7 4.5 %collective-permute-start.11 = (f32[8,128]{1,0:T(8,128)S(1)}, f32[8,128]{1,0:T(8,128)S(1)}, u32[]{:S(2)}, u32[]{:S(2)}) collective-permute-start(f32[8,128]{1,0:T(8,128)S(1)} %merge.1.a_ref), channel_id=1, source_target_pairs={{0,4},{2,6},{4,0},{6,2},{8,12},{10,14},{12,8},{14,10},{16,20},{18,... | collective-permute-start | bytes 12296 | tf_op jit(solution)/shard_map/ppermute | solution.py:43
  36.3 3.9 %collective-permute-start.12 = (f32[8,128]{1,0:T(8,128)S(1)}, f32[8,128]{1,0:T(8,128)S(1)}, u32[]{:S(2)}, u32[]{:S(2)}) collective-permute-start(f32[8,128]{1,0:T(8,128)S(1)} %merge.1.a_ref), channel_id=1, source_target_pairs={{0,8},{2,10},{4,12},{6,14},{8,0},{10,2},{12,4},{14,6},{16,24},{18,... | collective-permute-start | bytes 12296 | tf_op jit(solution)/shard_map/ppermute | solution.py:43
  37.4 4.5 %collective-permute-start.13 = (f32[8,128]{1,0:T(8,128)S(1)}, f32[8,128]{1,0:T(8,128)S(1)}, u32[]{:S(2)}, u32[]{:S(2)}) collective-permute-start(f32[8,128]{1,0:T(8,128)S(1)} %merge.1.a_ref), channel_id=1, source_target_pairs={{0,12},{2,14},{4,8},{6,10},{8,4},{10,6},{12,0},{14,2},{16,28},{18,... | collective-permute-start | bytes 12296 | tf_op jit(solution)/shard_map/ppermute | solution.py:43
  39.2 7.3 %copy-start.3 = (s32[2]{0:T(128)S(1)}, s32[2]{0:T(128)}, u32[]{:S(2)}) copy-start(s32[2]{0:T(128)} %refs_0_.7) | copy-start | bytes 28
  39.2 7.3 %copy-start.4 = (s32[2]{0:T(128)S(1)}, s32[2]{0:T(128)}, u32[]{:S(2)}) copy-start(s32[2]{0:T(128)} %refs_1_.1) | copy-start | bytes 28
  40.1 6.5 %collective-permute-start.15 = (bf16[64,2048]{1,0:T(8,128)(2,1)S(1)}, bf16[64,2048]{1,0:T(8,128)(2,1)S(1)}, u32[]{:S(2)}, u32[]{:S(2)}) collective-permute-start(bf16[64,2048]{1,0:T(8,128)(2,1)S(1)} %convolution_convert_fusion), channel_id=1, source_target_pairs={{0,2},{2,0},{4,6},{6,4},{8,10},{10,8},{12,14},{14,12},{16,18},{18,... | collective-permute-start | bytes 786440 | tf_op jit(solution)/shard_map/ppermute | solution.py:43
  42.0 4.6 %collective-permute-start.14 = (f32[8,128]{1,0:T(8,128)S(1)}, f32[8,128]{1,0:T(8,128)S(1)}, u32[]{:S(2)}, u32[]{:S(2)}) collective-permute-start(f32[8,128]{1,0:T(8,128)S(1)} %merge_four.1.refs_4_), channel_id=1, source_target_pairs={{0,16},{2,18},{4,20},{6,22},{8,24},{10,26},{12,28},{14,30},{16,0},... | collective-permute-start | bytes 12296 | tf_op jit(solution)/shard_map/ppermute | solution.py:43
  47.9 6.1 %collective-permute-start.16 = (bf16[16,2176]{1,0:T(8,128)(2,1)S(1)}, bf16[16,2176]{1,0:T(8,128)(2,1)S(1)}, u32[]{:S(2)}, u32[]{:S(2)}) collective-permute-start(bf16[16,2176]{1,0:T(8,128)(2,1)S(1)} %get-tuple-element.34.dep_ref.rest_0_), channel_id=1, source_target_pairs={{0,16},{2,18},{4,20},{6,22},{8,24},{10,26},{12,28},{14,30},{16,0},... | collective-permute-start | bytes 208904 | tf_op jit(solution)/shard_map/ppermute | solution.py:43
  54.0 4.4 %collective-permute-start.17 = (bf16[16,2176]{1,0:T(8,128)(2,1)S(1)}, bf16[16,2176]{1,0:T(8,128)(2,1)S(1)}, u32[]{:S(2)}, u32[]{:S(2)}) collective-permute-start(bf16[16,2176]{1,0:T(8,128)(2,1)S(1)} %add_convert_fusion.refs_0_.rest_0_), channel_id=1, source_target_pairs={{0,4},{2,6},{4,0},{6,2},{8,12},{10,14},{12,8},{14,10},{16,20},{18,... | collective-permute-start | bytes 208904 | tf_op jit(solution)/shard_map/ppermute | solution.py:43
  54.1 4.4 %collective-permute-start.18 = (bf16[16,2176]{1,0:T(8,128)(2,1)S(1)}, bf16[16,2176]{1,0:T(8,128)(2,1)S(1)}, u32[]{:S(2)}, u32[]{:S(2)}) collective-permute-start(bf16[16,2176]{1,0:T(8,128)(2,1)S(1)} %add_convert_fusion.refs_0_.rest_0_), channel_id=1, source_target_pairs={{0,8},{2,10},{4,12},{6,14},{8,0},{10,2},{12,4},{14,6},{16,24},{18,... | collective-permute-start | bytes 208904 | tf_op jit(solution)/shard_map/ppermute | solution.py:43
  55.8 5.2 %collective-permute-start.19 = (bf16[16,2176]{1,0:T(8,128)(2,1)S(1)}, bf16[16,2176]{1,0:T(8,128)(2,1)S(1)}, u32[]{:S(2)}, u32[]{:S(2)}) collective-permute-start(bf16[16,2176]{1,0:T(8,128)(2,1)S(1)} %add_convert_fusion.refs_0_.rest_0_), channel_id=1, source_target_pairs={{0,12},{2,14},{4,8},{6,10},{8,4},{10,6},{12,0},{14,2},{16,28},{18,... | collective-permute-start | bytes 208904 | tf_op jit(solution)/shard_map/ppermute | solution.py:43
  61.1 7.1 %collective-permute-start.20 = (bf16[16,2176]{1,0:T(8,128)(2,1)S(1)}, bf16[16,2176]{1,0:T(8,128)(2,1)S(1)}, u32[]{:S(2)}, u32[]{:S(2)}) collective-permute-start(bf16[16,2176]{1,0:T(8,128)(2,1)S(1)} %join.3.refs_1_.refs_6_), channel_id=1, source_target_pairs={{0,2},{2,0},{4,6},{6,4},{8,10},{10,8},{12,14},{14,12},{16,18},{18,... | collective-permute-start | bytes 208904 | tf_op jit(solution)/shard_map/ppermute | solution.py:43

commit v4 on v3

--- a/solution.py
+++ b/solution.py
@@ -133,15 +133,15 @@
     slots = mine_ref.shape[0]
     half = mine_ref.shape[1] - LANES
     _, seq, _, core = here(blocks)
-    normed_ref, scaled_ref = rest[:2]
+    normed_ref = rest[0]
     gain = gain_ref[:, pl.ds(pl.multiple_of((core + side) % 2 * half, LANES), half)]
     for ref, s in ((mine_ref, seq), (there_ref, 1 - seq)):
         rows = pl.ds(pl.multiple_of(s * slots, slots), slots)
         inverse = lax.rsqrt(whole(ref[:, half:]) / model_width + EPSILON)
         scaled = ref[:, :half].astype(F32) * inverse
-        scaled_ref[rows, :] = scaled
         normed_ref[rows, :] = (scaled * gain).astype(BF16)
-        if len(rest) == 3:
+        if side == 0:
+            rest[1][rows, :] = scaled
             rest[2][rows, :] = jnp.broadcast_to(inverse, (slots, LANES))
 
 
@@ -209,7 +209,7 @@
 
 def gradient_kernel(
     blocks, length, model_width, num_ref, den_ref, own_ref, peer_ref, a_ref, b_ref, part_ref,
-    peer_part_ref, scaled_ref, inverse_ref, mine_ref, give_ref, meta_ref, loss_ref, rows_ref,
+    peer_part_ref, scaled_ref, inverse_ref, mine_ref, give_ref, meta_ref, rows_ref,
     part_scratch, tail_ref,
 ):
     total, half = scaled_ref.shape
@@ -252,10 +252,11 @@
         ref[:, :half] = part_scratch[rows, :].astype(ref.dtype)
         ref[:, half:] = tail.astype(ref.dtype)
     lane = lax.broadcasted_iota(jnp.int32, (total, LANES), 1)
-    meta_ref[...] = jnp.where(lane == 2, across / inverse_ref[...], across)
-    loss_ref[...] = jnp.sum(
+    loss = jnp.sum(
         jnp.where(place < total, factor * (log_total - picked), 0.0), axis=1, keepdims=True
     )
+    meta = jnp.where(lane == 2, across / inverse_ref[...], across)
+    meta_ref[...] = jnp.where(lane == 6, loss, meta)
 
 
 def dlogits_kernel(
@@ -272,6 +273,11 @@
     core = lax.axis_index("ctx") % 2
     for side, ref in enumerate((own_ref, other_ref)):
         normed_ref[:, pl.ds(pl.multiple_of((core + side) % 2 * half, LANES), half)] = ref[...]
+
+
+def loss_kernel(meta_ref, dep_ref, loss_ref):
+    del dep_ref
+    loss_ref[...] = meta_ref[0:1, 6:7]
 
 
 def head_kernel(dlogits_ref, normed_ref, *rest):
@@ -419,18 +425,18 @@
         mine = mine + swap(mine, "ctx", bit)
     before = mine
     mine = join(before, around(before))
-    loads.append(load(1, before))
+    loads.append(load(1, mine))
     there = swap(mine, "ctx", blocks)
     mine_other = swap(mine, "ctx", 1)
     there_other = swap(there, "ctx", 1)
 
     def normalize(side, a, b):
-        extra = [shape((total, LANES), F32)] if side == 0 else []
+        extra = [] if side else [shape((total, half), F32), shape((total, LANES), F32)]
         return pl.pallas_call(
             lambda *refs: normalize_kernel(blocks, model_width, side, *refs),
             in_specs=[vmem()] * 3,
-            out_specs=[vmem()] * (2 + len(extra)),
-            out_shape=[shape((total, half), BF16), shape((total, half), F32)] + extra,
+            out_specs=[vmem()] * (1 + len(extra)),
+            out_shape=[shape((total, half), BF16)] + extra,
             compiler_params=params(6),
             name="normalize",
         )(a, b, gain_row)
@@ -440,7 +446,7 @@
 
     normed, scaled, inverse = normalize(0, mine, there)
     partial = contract(normed, loads[0])
-    normed_other, _ = normalize(1, mine_other, there_other)
+    (normed_other,) = normalize(1, mine_other, there_other)
     partial = partial + contract(normed_other, loads[1])
     bit = 1
     while 2 * bit < lax.axis_size("vocab"):
@@ -497,15 +503,14 @@
     part_other = jnp.dot(exps, loads[1], preferred_element_type=F32).astype(BF16)
     part = jnp.dot(exps, loads[0], preferred_element_type=F32)
     peer_part = swap(part_other, "ctx", 1)
-    own_part, give, meta, loss_value = pl.pallas_call(
+    own_part, give, meta = pl.pallas_call(
         lambda *refs: gradient_kernel(blocks, tok * blocks, model_width, *refs),
         in_specs=[smem(), smem()] + [vmem()] * 8,
-        out_specs=[vmem()] * 4,
+        out_specs=[vmem()] * 3,
         out_shape=[
             shape((slots, packed_width), F32),
             shape((slots, packed_width), BF16),
             shape((total, LANES), F32),
-            shape((1, 1), F32),
         ],
         scratch_shapes=[
             pltpu.VMEM((SUBLANES, LANES), F32),
@@ -552,6 +557,14 @@
     for bit in inner_bits[:-2]:
         sent = sent + swap(sent, "ctx", bit)
     grad_head = head_part(middle, steps, sent, grad_head)
+    loss_value = pl.pallas_call(
+        loss_kernel,
+        in_specs=[vmem(), anywhere()],
+        out_specs=vmem(),
+        out_shape=shape((1, 1), F32),
+        compiler_params=params(4),
+        name="loss",
+    )(meta, sent)
     sent = join(sent, around(sent))
     other = swap(sent, "ctx", 1)
 

time: 69.8 us -> 69.2 us (level)
    pallas_call x2, Pallas kernels: 0.94 us -> 0.24 us  [normalize(): pl.pallas_call(lambda *refs: normalize_kernel(blocks, model_width, side,...]
  transfers between devices with their start and end apart: 21 -> 21, of which waited for: 13 -> 13; matrix products, arithmetic and copies ran while one was open for 4% -> 4% of each run, Pallas kernels for 17% -> 18%
where the time goes in v4:
time: 69.2 us; the launch traced here: 69 us
  waiting for transfers between devices  25.5 us (37%)
  starting transfers between devices  20.8 us (30%)
  Pallas kernels  15.6 us (23%)
  matrix products  4.58 us (7%)
  other arithmetic  0.92 us (1%)
  between operations  0.87 us (1%)
  local copies, waits for them, and re-layouts  0.77 us (1%)
    ppermute x20, waiting for transfers between devices, swap(): lax.ppermute(x, axis, [(i, i ^ bit) for i in range(lax.axis_size(axis))])  24.1 us
    ppermute x20, starting transfers between devices, swap(): lax.ppermute(x, axis, [(i, i ^ bit) for i in range(lax.axis_size(axis))])  20.7 us
    pallas_call x2, Pallas kernels, head_part(): pl.pallas_call(head_kernel, grid=(last - first,), in_specs=[pl.BlockSpec(...  5.31 us
    pallas_call x2, Pallas kernels, load(): pl.pallas_call(lambda *refs: load_kernel(side, *refs), in_specs=[anywhere...  4.33 us
    pallas_call x2, Pallas kernels, finish(): pl.pallas_call(lambda *refs: final_kernel(blocks, side, *refs), in_specs=...  2.72 us
    dot_general x2, matrix products, contract(): lax.dot_general(a, b, (((1,), (1,)), ((), ())), preferred_element_type=F32)  2.52 us
    ppermute x1, waiting for transfers between devices, device_step(): lax.ppermute(squares, ('ctx', 'vocab'), [(i, i ^ ways + 1) for i in range...  1.45 us
  transfers between devices with their start and end apart: 21, of which 13 were waited for; matrix products, arithmetic and copies ran while one was open for 4% of the time, Pallas kernels for 18%

profile of v4, /device:TPU:0, one launch (start us, length us, event | category | flops | bytes accessed | tf_op | source)
XLA Modules:
  0.0 69.0 jit_solution(17228326590701584356)
XLA Ops:
  0.6 0.0 copy-start
  0.7 0.8 %subtract_bitcast_fusion = s32[16]{0:T(128)S(1)} fusion(s32[2,16]{1,0:T(2,128)} %param.10, s32[]{:T(128)S(6)} %select_n.15, s32[]{:T(128)S(6)} %mul.3), kind=kLoop, calls=%fused_computation.7 | loop fusion | flops 16 | bytes 136 | tf_op jit(solution)/shard_map/sub | solution.py:347
  1.5 0.7 %copy-done = bf16[256,4096]{1,0:T(8,128)(2,1)S(1)} copy-done((bf16[256,4096]{1,0:T(8,128)(2,1)S(1)}, bf16[256,4096]{1,0:T(8,128)(2,1)}, u32[]{:S(2)}) %copy-start) | copy-done | bytes 2097176
  2.2 0.4 fusion.1.rows_ref
  2.7 0.1 pick.1
  2.8 0.6 collective-permute-start
  3.4 2.5 %collective-permute-start.1 = (f32[16,128]{1,0:T(8,128)S(1)}, f32[16,128]{1,0:T(8,128)S(1)}, u32[]{:S(2)}, u32[]{:S(2)}) collective-permute-start(f32[16,128]{1,0:T(8,128)S(1)} %get-tuple-element.23.squares_ref), channel_id=1, source_target_pairs={{0,1},{1,0},{2,3},{3,2},{4,5},{5,4},{6,7},{7,6},{8,9},{9,8},{10,11... | collective-permute-start | bytes 24584 | tf_op jit(solution)/shard_map/ppermute | solution.py:43
  5.9 0.0 collective-permute-start.2
  5.9 1.6 %collective-permute-done.1.up_ref = f32[16,128]{1,0:T(8,128)S(1)} collective-permute-done((f32[16,128]{1,0:T(8,128)S(1)}, f32[16,128]{1,0:T(8,128)S(1)}, u32[]{:S(2)}, u32[]{:S(2)}) %collective-permute-start.1) | collective-permute-done | bytes 8224 | tf_op jit(solution)/shard_map/ppermute | solution.py:43
  7.5 1.4 %collective-permute-done.2.across_ref = f32[16,128]{1,0:T(8,128)S(1)} collective-permute-done((f32[16,128]{1,0:T(8,128)S(1)}, f32[16,128]{1,0:T(8,128)S(1)}, u32[]{:S(2)}, u32[]{:S(2)}) %collective-permute-start.2) | collective-permute-done | bytes 8224 | tf_op jit(solution)/shard_map/ppermute | solution.py:378
  9.0 0.2 settle.1.refs_0_
  9.1 1.5 %collective-permute-start.3 = (bf16[16,2176]{1,0:T(8,128)(2,1)S(1)}, bf16[16,2176]{1,0:T(8,128)(2,1)S(1)}, u32[]{:S(2)}, u32[]{:S(2)}) collective-permute-start(bf16[16,2176]{1,0:T(8,128)(2,1)S(1)} %settle.1.refs_0_), channel_id=1, source_target_pairs={{0,4},{2,6},{4,0},{6,2},{8,12},{10,14},{12,8},{14,10},{16,20},{18,... | collective-permute-start | bytes 208904 | tf_op jit(solution)/shard_map/ppermute | solution.py:43
  10.6 1.6 %collective-permute-start.4 = (bf16[16,2176]{1,0:T(8,128)(2,1)S(1)}, bf16[16,2176]{1,0:T(8,128)(2,1)S(1)}, u32[]{:S(2)}, u32[]{:S(2)}) collective-permute-start(bf16[16,2176]{1,0:T(8,128)(2,1)S(1)} %settle.1.refs_0_), channel_id=1, source_target_pairs={{0,8},{2,10},{4,12},{6,14},{8,0},{10,2},{12,4},{14,6},{16,24},{18,... | collective-permute-start | bytes 208904 | tf_op jit(solution)/shard_map/ppermute | solution.py:43
  12.2 0.4 collective-permute-start.5
  12.6 0.8 %collective-permute-done.3.refs_1_ = bf16[16,2176]{1,0:T(8,128)(2,1)S(1)} collective-permute-done((bf16[16,2176]{1,0:T(8,128)(2,1)S(1)}, bf16[16,2176]{1,0:T(8,128)(2,1)S(1)}, u32[]{:S(2)}, u32[]{:S(2)}) %collective-permute-start.3) | collective-permute-done | bytes 69664 | tf_op jit(solution)/shard_map/ppermute | solution.py:43
  13.5 2.1 %collective-permute-done.4.refs_2_ = bf16[16,2176]{1,0:T(8,128)(2,1)S(1)} collective-permute-done((bf16[16,2176]{1,0:T(8,128)(2,1)S(1)}, bf16[16,2176]{1,0:T(8,128)(2,1)S(1)}, u32[]{:S(2)}, u32[]{:S(2)}) %collective-permute-start.4) | collective-permute-done | bytes 69664 | tf_op jit(solution)/shard_map/ppermute | solution.py:43
  15.5 1.9 %collective-permute-done.5.refs_3_ = bf16[16,2176]{1,0:T(8,128)(2,1)S(1)} collective-permute-done((bf16[16,2176]{1,0:T(8,128)(2,1)S(1)}, bf16[16,2176]{1,0:T(8,128)(2,1)S(1)}, u32[]{:S(2)}, u32[]{:S(2)}) %collective-permute-start.5) | collective-permute-done | bytes 69664 | tf_op jit(solution)/shard_map/ppermute | solution.py:43
  17.5 2.7 %collective-permute-start.6 = (bf16[16,2176]{1,0:T(8,128)(2,1)S(1)}, bf16[16,2176]{1,0:T(8,128)(2,1)S(1)}, u32[]{:S(2)}, u32[]{:S(2)}) collective-permute-start(bf16[16,2176]{1,0:T(8,128)(2,1)S(1)} %join.2.refs_0_.refs_1_), channel_id=1, source_target_pairs={{0,16},{2,18},{4,20},{6,22},{8,24},{10,26},{12,28},{14,30},{16,0},... | collective-permute-start | bytes 208904 | tf_op jit(solution)/shard_map/ppermute | solution.py:43
  20.1 2.2 %load.2 = bf16[988,2048]{1,0:T(8,128)(2,1)S(1)} custom-call(bf16[988,4096]{1,0:T(8,128)(2,1)} %refs_0_.5, bf16[16,2176]{1,0:T(8,128)(2,1)S(1)} %get-tuple-element.21.first_ref.refs_1_), custom_call_target="tpu_custom_call" | custom-call | bytes 8093696 | tf_op jit(solution)/shard_map/load/pallas_call | solution.py:364
  22.3 0.0 copy-start.1
  22.3 2.2 %load.3 = bf16[988,2048]{1,0:T(8,128)(2,1)S(1)} custom-call(bf16[988,4096]{1,0:T(8,128)(2,1)} %refs_0_.5, bf16[16,2176]{1,0:T(8,128)(2,1)S(1)} %join.2.refs_0_.refs_1_), custom_call_target="tpu_custom_call" | custom-call | bytes 8093696 | tf_op jit(solution)/shard_map/load/pallas_call | solution.py:364
  24.5 0.1 collective-permute-start.7
  24.6 0.5 collective-permute-start.8
  25.1 0.1 normalize.2
  25.2 0.0 copy-start.2
  25.2 1.3 %fusion.3 = f32[32,988]{1,0:T(8,128)S(1)} fusion(bf16[32,2048]{1,0:T(8,128)(2,1)S(1)} %get-tuple-element.24.own_ref, bf16[988,2048]{1,0:T(8,128)(2,1)S(1)} %load.2), kind=kOutput, calls=%fused_computation.8 | convolution fusion | flops 129499136 | bytes 4304384 | tf_op jit(solution)/shard_map/dot_general | solution.py:445
  26.5 0.0 collective-permute-done.8.refs_1_
  26.5 0.1 normalize.3.other_ref
  26.6 1.3 %convolution_add_fusion.refs_1_.first_ref = f32[32,988]{1,0:T(8,128)S(1)} fusion(f32[32,988]{1,0:T(8,128)S(1)} %fusion.3, bf16[32,2048]{1,0:T(8,128)(2,1)S(1)} %normalize.3.other_ref, bf16[988,2048]{1,0:T(8,128)(2,1)S(1)} %load.3), kind=kOutput, calls=%fused_computation.1 | convolution fusion | flops 129530752 | bytes 4430848 | tf_op jit(solution)/shard_map/dot_general | solution.py:445
  27.9 0.6 collective-permute-start.9
  28.5 0.6 targets.1.targets_ref
  29.1 4.3 %collective-permute-done.9.second_ref = f32[32,988]{1,0:T(8,128)S(1)} collective-permute-done((f32[32,988]{1,0:T(8,128)S(1)}, f32[32,988]{1,0:T(8,128)S(1)}, u32[]{:S(2)}, u32[]{:S(2)}) %collective-permute-start.9) | collective-permute-done | bytes 126496 | tf_op jit(solution)/shard_map/ppermute | solution.py:43
  33.4 0.4 stats.1
  33.8 0.0 collective-permute-start.10
  33.8 1.2 %collective-permute-done.10.second_ref.refs_3_ = f32[8,128]{1,0:T(8,128)S(1)} collective-permute-done((f32[8,128]{1,0:T(8,128)S(1)}, f32[8,128]{1,0:T(8,128)S(1)}, u32[]{:S(2)}, u32[]{:S(2)}) %collective-permute-start.10) | collective-permute-done | bytes 4128 | tf_op jit(solution)/shard_map/ppermute | solution.py:43
  35.0 0.6 collective-permute-start.11
  35.6 1.2 %collective-permute-start.12 = (f32[8,128]{1,0:T(8,128)S(1)}, f32[8,128]{1,0:T(8,128)S(1)}, u32[]{:S(2)}, u32[]{:S(2)}) collective-permute-start(f32[8,128]{1,0:T(8,128)S(1)} %merge.1.a_ref), channel_id=1, source_target_pairs={{0,8},{2,10},{4,12},{6,14},{8,0},{10,2},{12,4},{14,6},{16,24},{18,... | collective-permute-start | bytes 12296 | tf_op jit(solution)/shard_map/ppermute | solution.py:43
  36.7 1.8 %collective-permute-start.13 = (f32[8,128]{1,0:T(8,128)S(1)}, f32[8,128]{1,0:T(8,128)S(1)}, u32[]{:S(2)}, u32[]{:S(2)}) collective-permute-start(f32[8,128]{1,0:T(8,128)S(1)} %merge.1.a_ref), channel_id=1, source_target_pairs={{0,12},{2,14},{4,8},{6,10},{8,4},{10,6},{12,0},{14,2},{16,28},{18,... | collective-permute-start | bytes 12296 | tf_op jit(solution)/shard_map/ppermute | solution.py:43
  38.5 0.8 %convolution_convert_fusion = bf16[64,2048]{1,0:T(8,128)(2,1)S(1)} fusion(bf16[64,988]{1,0:T(8,128)(2,1)S(1)} %get-tuple-element.26, bf16[988,2048]{1,0:T(8,128)(2,1)S(1)} %load.3), kind=kOutput, calls=%fused_computation | convolution fusion | flops 259129344 | bytes 4435456 | tf_op jit(solution)/shard_map/dot_general | solution.py:503
  39.4 0.1 collective-permute-start.15
  39.4 0.0 collective-permute-done.12.c_ref
  39.5 1.8 %collective-permute-done.13.d_ref = f32[8,128]{1,0:T(8,128)S(1)} collective-permute-done((f32[8,128]{1,0:T(8,128)S(1)}, f32[8,128]{1,0:T(8,128)S(1)}, u32[]{:S(2)}, u32[]{:S(2)}) %collective-permute-start.13) | collective-permute-done | bytes 4128 | tf_op jit(solution)/shard_map/ppermute | solution.py:43
  41.3 1.5 %collective-permute-start.14 = (f32[8,128]{1,0:T(8,128)S(1)}, f32[8,128]{1,0:T(8,128)S(1)}, u32[]{:S(2)}, u32[]{:S(2)}) collective-permute-start(f32[8,128]{1,0:T(8,128)S(1)} %merge_four.1.refs_4_), channel_id=1, source_target_pairs={{0,16},{2,18},{4,20},{6,22},{8,24},{10,26},{12,28},{14,30},{16,0},... | collective-permute-start | bytes 12296 | tf_op jit(solution)/shard_map/ppermute | solution.py:43
  42.8 0.8 %fusion.4.refs_6_ = f32[64,2048]{1,0:T(8,128)S(1)} fusion(bf16[64,988]{1,0:T(8,128)(2,1)S(1)} %get-tuple-element.26, bf16[988,2048]{1,0:T(8,128)(2,1)S(1)} %load.2), kind=kOutput, calls=%fused_computation.9 | convolution fusion | flops 258998272 | bytes 4697600 | tf_op jit(solution)/shard_map/dot_general | solution.py:504
  43.6 2.2 %collective-permute-done.14.refs_5_ = f32[8,128]{1,0:T(8,128)S(1)} collective-permute-done((f32[8,128]{1,0:T(8,128)S(1)}, f32[8,128]{1,0:T(8,128)S(1)}, u32[]{:S(2)}, u32[]{:S(2)}) %collective-permute-start.14) | collective-permute-done | bytes 4128 | tf_op jit(solution)/shard_map/ppermute | solution.py:43
  45.8 0.0 collective-permute-done.15.refs_7_
  45.8 0.8 %gradient.1 = (f32[16,2176]{1,0:T(8,128)S(1)}, bf16[16,2176]{1,0:T(8,128)(2,1)S(1)}, f32[32,128]{1,0:T(8,128)S(1)}) custom-call(s32[2]{0:T(128)S(1)} %copy-done.3, s32[2]{0:T(128)S(1)} %copy-done.4, f32[8,128]{1,0:T(8,128)S(1)} %get-tuple-element.25.first_ref.refs_2_, f32[8,128]{1,0:T(8,128)S(1)} %collective-permute-done.10.second_ref.refs_3_, ...), custom_call_target="tpu_custom_call" | custom-call | tf_op jit(solution)/shard_map/gradient/pallas_call | solution.py:506
  46.7 1.5 %collective-permute-start.16 = (bf16[16,2176]{1,0:T(8,128)(2,1)S(1)}, bf16[16,2176]{1,0:T(8,128)(2,1)S(1)}, u32[]{:S(2)}, u32[]{:S(2)}) collective-permute-start(bf16[16,2176]{1,0:T(8,128)(2,1)S(1)} %get-tuple-element.31.dep_ref.rest_0_), channel_id=1, source_target_pairs={{0,16},{2,18},{4,20},{6,22},{8,24},{10,26},{12,28},{14,30},{16,0},... | collective-permute-start | bytes 208904 | tf_op jit(solution)/shard_map/ppermute | solution.py:43
  48.2 4.6 %collective-permute-done.16 = bf16[16,2176]{1,0:T(8,128)(2,1)S(1)} collective-permute-done((bf16[16,2176]{1,0:T(8,128)(2,1)S(1)}, bf16[16,2176]{1,0:T(8,128)(2,1)S(1)}, u32[]{:S(2)}, u32[]{:S(2)}) %collective-permute-start.16) | collective-permute-done | bytes 69664 | tf_op jit(solution)/shard_map/ppermute | solution.py:43
  52.8 0.1 collective-permute-start.17
  52.9 1.8 %collective-permute-start.18 = (bf16[16,2176]{1,0:T(8,128)(2,1)S(1)}, bf16[16,2176]{1,0:T(8,128)(2,1)S(1)}, u32[]{:S(2)}, u32[]{:S(2)}) collective-permute-start(bf16[16,2176]{1,0:T(8,128)(2,1)S(1)} %add_convert_fusion.dep_ref.refs_0_.rest_0_), channel_id=1, source_target_pairs={{0,8},{2,10},{4,12},{6,14},{8,0},{10,2},{12,4},{14,6},{16,24},{18,... | collective-permute-start | bytes 208904 | tf_op jit(solution)/shard_map/ppermute | solution.py:43
  54.7 1.7 %collective-permute-start.19 = (bf16[16,2176]{1,0:T(8,128)(2,1)S(1)}, bf16[16,2176]{1,0:T(8,128)(2,1)S(1)}, u32[]{:S(2)}, u32[]{:S(2)}) collective-permute-start(bf16[16,2176]{1,0:T(8,128)(2,1)S(1)} %add_convert_fusion.dep_ref.refs_0_.rest_0_), channel_id=1, source_target_pairs={{0,12},{2,14},{4,8},{6,10},{8,4},{10,6},{12,0},{14,2},{16,28},{18,... | collective-permute-start | bytes 208904 | tf_op jit(solution)/shard_map/ppermute | solution.py:43
  56.4 0.8 %collective-permute-done.17.refs_1_ = bf16[16,2176]{1,0:T(8,128)(2,1)S(1)} collective-permute-done((bf16[16,2176]{1,0:T(8,128)(2,1)S(1)}, bf16[16,2176]{1,0:T(8,128)(2,1)S(1)}, u32[]{:S(2)}, u32[]{:S(2)}) %collective-permute-start.17) | collective-permute-done | bytes 69664 | tf_op jit(solution)/shard_map/ppermute | solution.py:43
  57.2 0.1 collective-permute-done.18.refs_2_
  57.3 2.7 %collective-permute-done.19.refs_3_ = bf16[16,2176]{1,0:T(8,128)(2,1)S(1)} collective-permute-done((bf16[16,2176]{1,0:T(8,128)(2,1)S(1)}, bf16[16,2176]{1,0:T(8,128)(2,1)S(1)}, u32[]{:S(2)}, u32[]{:S(2)}) %collective-permute-start.19) | collective-permute-done | bytes 69664 | tf_op jit(solution)/shard_map/ppermute | solution.py:43
  60.0 0.1 collective-permute-start.20
  60.0 0.1 fusion.refs_0_
  60.1 0.3 dlogits.1
  60.4 2.7 %head_grad.2.rest_1_ = bf16[988,4096]{1,0:T(8,128)(2,1)} custom-call(bf16[988,32]{1,0:T(8,128)(2,1)S(1)} %get-tuple-element.35.dlogits_ref, bf16[32,4096]{1,0:T(8,128)(2,1)S(1)} %get-tuple-element.36.normed_ref, bf16[16,2176]{1,0:T(8,128)(2,1)S(1)} %get-tuple-element.31.dep_ref.rest_0_), custom_call_target="tpu_custom_call" | custom-call | bytes 4046848 | tf_op jit(solution)/shard_map/head_grad/pallas_call | solution.py:530
  63.0 0.6 loss.1
  63.6 2.6 %head_grad.3 = bf16[988,4096]{1,0:T(8,128)(2,1)} custom-call(bf16[988,32]{1,0:T(8,128)(2,1)S(1)} %get-tuple-element.35.dlogits_ref, bf16[32,4096]{1,0:T(8,128)(2,1)S(1)} %get-tuple-element.36.normed_ref, bf16[16,2176]{1,0:T(8,128)(2,1)S(1)} %add_convert_fusion.dep_ref.refs_0_.rest_0_, bf16[988,4096]{1,0:T(8,128)(2,1)} %head_grad.2.rest_1_), custom_call_target="tpu_custom_call", output_to_operand_aliasing={{}: (3, {})} | custom-call | bytes 4046848 | tf_op jit(solution)/shard_map/head_grad/pallas_call | solution.py:530
  66.3 1.3 %final.2.refs_7_ = bf16[256,4096]{1,0:T(8,128)(2,1)} custom-call(bf16[16,256]{1,0:T(8,128)(2,1)S(1)} %fusion.refs_0_, bf16[16,2176]{1,0:T(8,128)(2,1)S(1)} %join.3.refs_1_.refs_6_, bf16[16,4096]{1,0:T(8,128)(2,1)S(1)} %get-tuple-element.32.refs_2_, f32[32,128]{1,0:T(8,128)S(1)} %get-tuple-element.28.refs_9_.refs_3_, ...), custom_call_target="tpu_custom_call" | custom-call | tf_op jit(solution)/shard_map/final/pallas_call | solution.py:573
  67.6 0.0 collective-permute-done.20.refs_1_
  67.6 1.4 %final.3 = (bf16[256,4096]{1,0:T(8,128)(2,1)}, f32[1,4096]{1,0:T(1,128)}) custom-call(bf16[16,256]{1,0:T(8,128)(2,1)S(1)} %fusion.refs_0_, bf16[16,2176]{1,0:T(8,128)(2,1)S(1)} %collective-permute-done.20.refs_1_, bf16[16,4096]{1,0:T(8,128)(2,1)S(1)} %get-tuple-element.32.refs_2_, ...), custom_call_target="tpu_custom_call", output_to_operand_aliasing={{0}: (7, {})} | custom-call | tf_op jit(solution)/shard_map/final/pallas_call | solution.py:573
  (15 shorter events, 0.2 us)
Async XLA Ops:
  0.6 1.6 %copy-start = (bf16[256,4096]{1,0:T(8,128)(2,1)S(1)}, bf16[256,4096]{1,0:T(8,128)(2,1)}, u32[]{:S(2)}) copy-start(bf16[256,4096]{1,0:T(8,128)(2,1)} %param.7) | copy-start | bytes 6291460
  2.8 6.2 %collective-permute-start = (bf16[16,2176]{1,0:T(8,128)(2,1)S(1)}, bf16[16,2176]{1,0:T(8,128)(2,1)S(1)}, u32[]{:S(2)}, u32[]{:S(2)}) collective-permute-start(bf16[16,2176]{1,0:T(8,128)(2,1)S(1)} %get-tuple-element.22), channel_id=1, source_target_pairs={{0,2},{2,0},{4,6},{6,4},{8,10},{10,8},{12,14},{14,12},{16,18},{18,... | collective-permute-start | bytes 208904 | tf_op jit(solution)/shard_map/ppermute | solution.py:43
  3.4 4.2 %collective-permute-start.1 = (f32[16,128]{1,0:T(8,128)S(1)}, f32[16,128]{1,0:T(8,128)S(1)}, u32[]{:S(2)}, u32[]{:S(2)}) collective-permute-start(f32[16,128]{1,0:T(8,128)S(1)} %get-tuple-element.23.squares_ref), channel_id=1, source_target_pairs={{0,1},{1,0},{2,3},{3,2},{4,5},{5,4},{6,7},{7,6},{8,9},{9,8},{10,11... | collective-permute-start | bytes 24584 | tf_op jit(solution)/shard_map/ppermute | solution.py:43
  5.9 3.1 %collective-permute-start.2 = (f32[16,128]{1,0:T(8,128)S(1)}, f32[16,128]{1,0:T(8,128)S(1)}, u32[]{:S(2)}, u32[]{:S(2)}) collective-permute-start(f32[16,128]{1,0:T(8,128)S(1)} %get-tuple-element.23.squares_ref), channel_id=1, source_target_pairs={{0,3},{1,2},{2,1},{3,0},{4,7},{5,6},{6,5},{7,4},{8,11},{9,10},{10,... | collective-permute-start | bytes 24584 | tf_op jit(solution)/shard_map/ppermute | solution.py:378
  9.1 4.3 %collective-permute-start.3 = (bf16[16,2176]{1,0:T(8,128)(2,1)S(1)}, bf16[16,2176]{1,0:T(8,128)(2,1)S(1)}, u32[]{:S(2)}, u32[]{:S(2)}) collective-permute-start(bf16[16,2176]{1,0:T(8,128)(2,1)S(1)} %settle.1.refs_0_), channel_id=1, source_target_pairs={{0,4},{2,6},{4,0},{6,2},{8,12},{10,14},{12,8},{14,10},{16,20},{18,... | collective-permute-start | bytes 208904 | tf_op jit(solution)/shard_map/ppermute | solution.py:43
  10.6 4.9 %collective-permute-start.4 = (bf16[16,2176]{1,0:T(8,128)(2,1)S(1)}, bf16[16,2176]{1,0:T(8,128)(2,1)S(1)}, u32[]{:S(2)}, u32[]{:S(2)}) collective-permute-start(bf16[16,2176]{1,0:T(8,128)(2,1)S(1)} %settle.1.refs_0_), channel_id=1, source_target_pairs={{0,8},{2,10},{4,12},{6,14},{8,0},{10,2},{12,4},{14,6},{16,24},{18,... | collective-permute-start | bytes 208904 | tf_op jit(solution)/shard_map/ppermute | solution.py:43
  12.2 5.2 %collective-permute-start.5 = (bf16[16,2176]{1,0:T(8,128)(2,1)S(1)}, bf16[16,2176]{1,0:T(8,128)(2,1)S(1)}, u32[]{:S(2)}, u32[]{:S(2)}) collective-permute-start(bf16[16,2176]{1,0:T(8,128)(2,1)S(1)} %settle.1.refs_0_), channel_id=1, source_target_pairs={{0,12},{2,14},{4,8},{6,10},{8,4},{10,6},{12,0},{14,2},{16,28},{18,... | collective-permute-start | bytes 208904 | tf_op jit(solution)/shard_map/ppermute | solution.py:43
  17.5 7.1 %collective-permute-start.6 = (bf16[16,2176]{1,0:T(8,128)(2,1)S(1)}, bf16[16,2176]{1,0:T(8,128)(2,1)S(1)}, u32[]{:S(2)}, u32[]{:S(2)}) collective-permute-start(bf16[16,2176]{1,0:T(8,128)(2,1)S(1)} %join.2.refs_0_.refs_1_), channel_id=1, source_target_pairs={{0,16},{2,18},{4,20},{6,22},{8,24},{10,26},{12,28},{14,30},{16,0},... | collective-permute-start | bytes 208904 | tf_op jit(solution)/shard_map/ppermute | solution.py:43
  22.3 2.8 %copy-start.1 = (f32[4096]{0:T(1024)S(1)}, f32[4096]{0:T(1024)}, u32[]{:S(2)}) copy-start(f32[4096]{0:T(1024)} %param.8) | copy-start | bytes 49156
  24.5 2.0 %collective-permute-start.7 = (bf16[16,2176]{1,0:T(8,128)(2,1)S(1)}, bf16[16,2176]{1,0:T(8,128)(2,1)S(1)}, u32[]{:S(2)}, u32[]{:S(2)}) collective-permute-start(bf16[16,2176]{1,0:T(8,128)(2,1)S(1)} %join.2.refs_0_.refs_1_), channel_id=1, source_target_pairs={{0,2},{2,0},{4,6},{6,4},{8,10},{10,8},{12,14},{14,12},{16,18},{18,... | collective-permute-start | bytes 208904 | tf_op jit(solution)/shard_map/ppermute | solution.py:43
  24.6 1.9 %collective-permute-start.8 = (bf16[16,2176]{1,0:T(8,128)(2,1)S(1)}, bf16[16,2176]{1,0:T(8,128)(2,1)S(1)}, u32[]{:S(2)}, u32[]{:S(2)}) collective-permute-start(bf16[16,2176]{1,0:T(8,128)(2,1)S(1)} %collective-permute-done.6.refs_1_), channel_id=1, source_target_pairs={{0,2},{2,0},{4,6},{6,4},{8,10},{10,8},{12,14},{14,12},{16,18},{18,... | collective-permute-start | bytes 208904 | tf_op jit(solution)/shard_map/ppermute | solution.py:43
  25.2 3.3 %copy-start.2 = (s32[2,16]{1,0:T(2,128)S(1)}, s32[2,16]{1,0:T(2,128)}, u32[]{:S(2)}) copy-start(s32[2,16]{1,0:T(2,128)} %refs_0_.6) | copy-start | bytes 388
  27.9 5.5 %collective-permute-start.9 = (f32[32,988]{1,0:T(8,128)S(1)}, f32[32,988]{1,0:T(8,128)S(1)}, u32[]{:S(2)}, u32[]{:S(2)}) collective-permute-start(f32[32,988]{1,0:T(8,128)S(1)} %convolution_add_fusion.refs_1_.first_ref), channel_id=1, source_target_pairs={{0,1},{1,0},{2,3},{3,2},{4,5},{5,4},{6,7},{7,6},{8,9},{9,8},{10,11... | collective-permute-start | bytes 379400 | tf_op jit(solution)/shard_map/ppermute | solution.py:43
  33.8 1.2 %collective-permute-start.10 = (f32[8,128]{1,0:T(8,128)S(1)}, f32[8,128]{1,0:T(8,128)S(1)}, u32[]{:S(2)}, u32[]{:S(2)}) collective-permute-start(f32[8,128]{1,0:T(8,128)S(1)} %get-tuple-element.25.first_ref.refs_2_), channel_id=1, source_target_pairs={{0,2},{2,0},{4,6},{6,4},{8,10},{10,8},{12,14},{14,12},{16,18},{18,... | collective-permute-start | bytes 12296 | tf_op jit(solution)/shard_map/ppermute | solution.py:43
  35.0 4.5 %collective-permute-start.11 = (f32[8,128]{1,0:T(8,128)S(1)}, f32[8,128]{1,0:T(8,128)S(1)}, u32[]{:S(2)}, u32[]{:S(2)}) collective-permute-start(f32[8,128]{1,0:T(8,128)S(1)} %merge.1.a_ref), channel_id=1, source_target_pairs={{0,4},{2,6},{4,0},{6,2},{8,12},{10,14},{12,8},{14,10},{16,20},{18,... | collective-permute-start | bytes 12296 | tf_op jit(solution)/shard_map/ppermute | solution.py:43
  35.6 3.9 %collective-permute-start.12 = (f32[8,128]{1,0:T(8,128)S(1)}, f32[8,128]{1,0:T(8,128)S(1)}, u32[]{:S(2)}, u32[]{:S(2)}) collective-permute-start(f32[8,128]{1,0:T(8,128)S(1)} %merge.1.a_ref), channel_id=1, source_target_pairs={{0,8},{2,10},{4,12},{6,14},{8,0},{10,2},{12,4},{14,6},{16,24},{18,... | collective-permute-start | bytes 12296 | tf_op jit(solution)/shard_map/ppermute | solution.py:43
  36.7 4.5 %collective-permute-start.13 = (f32[8,128]{1,0:T(8,128)S(1)}, f32[8,128]{1,0:T(8,128)S(1)}, u32[]{:S(2)}, u32[]{:S(2)}) collective-permute-start(f32[8,128]{1,0:T(8,128)S(1)} %merge.1.a_ref), channel_id=1, source_target_pairs={{0,12},{2,14},{4,8},{6,10},{8,4},{10,6},{12,0},{14,2},{16,28},{18,... | collective-permute-start | bytes 12296 | tf_op jit(solution)/shard_map/ppermute | solution.py:43
  38.5 7.3 %copy-start.3 = (s32[2]{0:T(128)S(1)}, s32[2]{0:T(128)}, u32[]{:S(2)}) copy-start(s32[2]{0:T(128)} %refs_0_.7) | copy-start | bytes 28
  38.5 7.3 %copy-start.4 = (s32[2]{0:T(128)S(1)}, s32[2]{0:T(128)}, u32[]{:S(2)}) copy-start(s32[2]{0:T(128)} %refs_1_.1) | copy-start | bytes 28
  39.4 6.5 %collective-permute-start.15 = (bf16[64,2048]{1,0:T(8,128)(2,1)S(1)}, bf16[64,2048]{1,0:T(8,128)(2,1)S(1)}, u32[]{:S(2)}, u32[]{:S(2)}) collective-permute-start(bf16[64,2048]{1,0:T(8,128)(2,1)S(1)} %convolution_convert_fusion), channel_id=1, source_target_pairs={{0,2},{2,0},{4,6},{6,4},{8,10},{10,8},{12,14},{14,12},{16,18},{18,... | collective-permute-start | bytes 786440 | tf_op jit(solution)/shard_map/ppermute | solution.py:43
  41.3 4.6 %collective-permute-start.14 = (f32[8,128]{1,0:T(8,128)S(1)}, f32[8,128]{1,0:T(8,128)S(1)}, u32[]{:S(2)}, u32[]{:S(2)}) collective-permute-start(f32[8,128]{1,0:T(8,128)S(1)} %merge_four.1.refs_4_), channel_id=1, source_target_pairs={{0,16},{2,18},{4,20},{6,22},{8,24},{10,26},{12,28},{14,30},{16,0},... | collective-permute-start | bytes 12296 | tf_op jit(solution)/shard_map/ppermute | solution.py:43
  46.7 6.1 %collective-permute-start.16 = (bf16[16,2176]{1,0:T(8,128)(2,1)S(1)}, bf16[16,2176]{1,0:T(8,128)(2,1)S(1)}, u32[]{:S(2)}, u32[]{:S(2)}) collective-permute-start(bf16[16,2176]{1,0:T(8,128)(2,1)S(1)} %get-tuple-element.31.dep_ref.rest_0_), channel_id=1, source_target_pairs={{0,16},{2,18},{4,20},{6,22},{8,24},{10,26},{12,28},{14,30},{16,0},... | collective-permute-start | bytes 208904 | tf_op jit(solution)/shard_map/ppermute | solution.py:43
  52.8 4.4 %collective-permute-start.17 = (bf16[16,2176]{1,0:T(8,128)(2,1)S(1)}, bf16[16,2176]{1,0:T(8,128)(2,1)S(1)}, u32[]{:S(2)}, u32[]{:S(2)}) collective-permute-start(bf16[16,2176]{1,0:T(8,128)(2,1)S(1)} %add_convert_fusion.dep_ref.refs_0_.rest_0_), channel_id=1, source_target_pairs={{0,4},{2,6},{4,0},{6,2},{8,12},{10,14},{12,8},{14,10},{16,20},{18,... | collective-permute-start | bytes 208904 | tf_op jit(solution)/shard_map/ppermute | solution.py:43
  52.9 4.3 %collective-permute-start.18 = (bf16[16,2176]{1,0:T(8,128)(2,1)S(1)}, bf16[16,2176]{1,0:T(8,128)(2,1)S(1)}, u32[]{:S(2)}, u32[]{:S(2)}) collective-permute-start(bf16[16,2176]{1,0:T(8,128)(2,1)S(1)} %add_convert_fusion.dep_ref.refs_0_.rest_0_), channel_id=1, source_target_pairs={{0,8},{2,10},{4,12},{6,14},{8,0},{10,2},{12,4},{14,6},{16,24},{18,... | collective-permute-start | bytes 208904 | tf_op jit(solution)/shard_map/ppermute | solution.py:43
  54.7 5.2 %collective-permute-start.19 = (bf16[16,2176]{1,0:T(8,128)(2,1)S(1)}, bf16[16,2176]{1,0:T(8,128)(2,1)S(1)}, u32[]{:S(2)}, u32[]{:S(2)}) collective-permute-start(bf16[16,2176]{1,0:T(8,128)(2,1)S(1)} %add_convert_fusion.dep_ref.refs_0_.rest_0_), channel_id=1, source_target_pairs={{0,12},{2,14},{4,8},{6,10},{8,4},{10,6},{12,0},{14,2},{16,28},{18,... | collective-permute-start | bytes 208904 | tf_op jit(solution)/shard_map/ppermute | solution.py:43
  60.0 7.7 %collective-permute-start.20 = (bf16[16,2176]{1,0:T(8,128)(2,1)S(1)}, bf16[16,2176]{1,0:T(8,128)(2,1)S(1)}, u32[]{:S(2)}, u32[]{:S(2)}) collective-permute-start(bf16[16,2176]{1,0:T(8,128)(2,1)S(1)} %join.3.refs_1_.refs_6_), channel_id=1, source_target_pairs={{0,2},{2,0},{4,6},{6,4},{8,10},{10,8},{12,14},{14,12},{16,18},{18,... | collective-permute-start | bytes 208904 | tf_op jit(solution)/shard_map/ppermute | solution.py:43
